TPU v7x, 512 devices: a whole 4x4x16 slice. The times are simulated.
512 devices in a mesh: ctx: 64 (over x, z), head: 8 (over y, core).
Axes of the slice: x: 4, y: 4, z: 16, core: 2. Of those that a mesh axis runs over, the one named last changes fastest.
Arguments:
- lin_query: bfloat16 [16384, 4096], P('ctx', 'head'), may hold values from -200 to 200
- lin_keys: bfloat16 [16384, 4096], P('ctx', 'head'), may hold values from -6 to 6
- lin_values: bfloat16 [16384, 4096], P('ctx', 'head'), may hold values from -6 to 6
- lin_grad: bfloat16 [16384, 4096], P('ctx', 'head'), may hold values from -6 to 6
- norm_gain: float32 [4096], P('head'), may hold values from 0.1 to 1.9
- log_decay: float32 [32, 16384], P('head'), may hold values from -1 to 0, as said below
- state_in: bfloat16 [64, 32, 128, 128], P('ctx', 'head'), may hold values from -96 to 96
- soft_query: bfloat16 [16384, 8192], P('ctx', 'head'), may hold values from -10 to 10
- soft_keys: bfloat16 [16384, 1024], P('ctx', 'head'), may hold values from -4 to 4
- soft_values: bfloat16 [16384, 1024], P('ctx', 'head'), may hold values from -6 to 6
- soft_grad: bfloat16 [16384, 8192], P('ctx', 'head'), may hold values from -6 to 6
- projections: bfloat16 [2, 4096, 1024], P(None, None, 'head'), may hold values from -0.125 to 0.125
- doc_lengths: int32 [32], replicated, may hold values from 1 to 768, 16384 in all
Outputs:
- lin_dq: bfloat16 [16384, 4096], P('ctx', 'head')
- lin_dk: bfloat16 [16384, 4096], P('ctx', 'head')
- lin_dv: bfloat16 [16384, 4096], P('ctx', 'head')
- soft_dq: bfloat16 [16384, 8192], P('ctx', 'head')
- soft_dk: bfloat16 [16384, 1024], P('ctx', 'head')
- soft_dv: bfloat16 [16384, 1024], P('ctx', 'head')
Inputs may be any that keep to these rules, and one draw needn't show every extreme that they name: `log_decay`: strictly negative. `doc_lengths`: positive lengths that add up to 16384; the largest is exactly 768.
All inputs are finite; a program needn't handle non-finite values.
Results may differ from a plain program's by a relative error of at most 0.011.
Values may be sent and summed in bfloat16 or wider, within the bound.
No kernel may reach another device: no remote copies, remote signals or barrier semaphores. Data moves between devices by JAX's collectives and lax.ppermute only.
A program may use at most 128 MiB of HBM per device.

v0:
```python
import jax
import jax.numpy as jnp
from jax import lax
from jax.sharding import PartitionSpec as P

DH = 128
Q_HEADS = 64
KV_HEADS = 8
LIGHTNING_HEADS = 32
SUB = 4


epsilon = 1e-06
precise = lax.Precision.HIGHEST


def passed_along(block, axis, distance):
    devices = range(lax.axis_size(axis))
    route = [(i - distance, i) for i in devices if i - distance in devices]
    return lax.ppermute(block, axis, route)


def document_of(positions, doc_lengths):
    doc_ends = jnp.cumsum(doc_lengths)
    return jnp.sum((doc_ends[None, :] <= positions[:, None]).astype(jnp.int32), axis=1)


def decay_weights(log_block):
    running = jnp.cumsum(log_block, axis=1)
    position = jnp.arange(log_block.shape[1], dtype=jnp.int32)
    before = position[:, None] >= position[None, :]
    log_gap = running[:, :, None] - running[:, None, :]
    weights = jnp.where(before[None], jnp.exp(jnp.minimum(log_gap, 0.0)), 0.0)
    return (running, weights)


def lightning_part(lin_query, lin_keys, lin_values, cotangent, norm_gain, log_decay, state_in):
    length = lin_query.shape[0]
    head_count = lin_query.shape[1] // DH
    device = lax.axis_index("ctx")
    chain = lax.axis_size("ctx")
    log_block = lax.dynamic_slice_in_dim(log_decay, device * length, length, 1)
    running, weights = decay_weights(log_block)
    query_blk = lin_query.reshape(length, head_count, DH)
    key_blk = lin_keys.reshape(length, head_count, DH)
    value_blk = lin_values.reshape(length, head_count, DH)
    grad_blk = cotangent.reshape(length, head_count, DH)
    state_blk = state_in[0]
    near_terms = (
        jnp.einsum("thd,shd->hts", query_blk, key_blk, preferred_element_type=jnp.float32) * weights
    ).astype(jnp.bfloat16)
    growth = jnp.exp(running).T[:, :, None]
    scaled = (query_blk.astype(jnp.float32) * growth).astype(jnp.bfloat16)
    inside = jnp.einsum("hts,shd->thd", near_terms, value_blk, preferred_element_type=jnp.float32)
    carried = jnp.einsum("thd,hde->the", scaled, state_blk, preferred_element_type=jnp.float32)
    lin_out = (inside + carried) / DH
    gated = norm_gain.reshape(head_count, DH)[None] * grad_blk
    squares, cross_term = lax.psum(
        (jnp.sum(lin_out * lin_out, axis=(1, 2)), jnp.sum(gated * lin_out, axis=(1, 2))), "head"
    )
    features = LIGHTNING_HEADS * DH
    spread = jnp.sqrt(squares / features + epsilon)
    out_grad = (
        gated / spread[:, None, None]
        - lin_out * (cross_term / (features * spread**3))[:, None, None]
    ).astype(jnp.bfloat16)
    far_terms = (
        jnp.einsum("the,she->hts", out_grad, value_blk, preferred_element_type=jnp.float32)
        * weights
    ).astype(jnp.bfloat16)
    grad_query = (
        jnp.einsum("hts,shd->thd", far_terms, key_blk, preferred_element_type=jnp.float32)
        + growth
        * jnp.einsum("the,hde->thd", out_grad, state_blk, preferred_element_type=jnp.float32)
    ) / DH
    summary = jnp.einsum(
        "thd,the->hde", scaled, out_grad, preferred_element_type=jnp.float32
    ).astype(jnp.bfloat16)
    own_total = running[:, -1]
    totals = jnp.sum(log_decay.reshape(head_count, chain, length), axis=2)
    starts = jnp.concatenate(
        [jnp.zeros((head_count, 1), jnp.float32), jnp.cumsum(totals, axis=1)], axis=1
    )
    anchor = lax.dynamic_slice_in_dim(starts, device + 1, 1, 1)
    block_in = lax.all_gather(summary[None], "ctx", axis=0, tiled=True)
    block_count = block_in.shape[0]
    block_index = jnp.arange(block_count, dtype=jnp.int32)
    log_level = lax.slice_in_dim(starts, 0, block_count, axis=1)
    factors = jnp.where(
        block_index[None, :] > device, jnp.exp(jnp.minimum(log_level - anchor, 0.0)), 0.0
    )
    after_state = jnp.einsum(
        "hn,nhde->hde", factors, block_in.astype(jnp.float32), precision=precise
    )
    after_low = after_state.astype(jnp.bfloat16)
    tail_decay = jnp.exp(own_total[:, None] - running).T[:, :, None]
    grad_key = (
        jnp.einsum("hst,shd->thd", far_terms, query_blk, preferred_element_type=jnp.float32)
        + tail_decay
        * jnp.einsum("the,hde->thd", value_blk, after_low, preferred_element_type=jnp.float32)
    ) / DH
    grad_value = (
        jnp.einsum("hst,she->the", near_terms, out_grad, preferred_element_type=jnp.float32)
        + tail_decay
        * jnp.einsum("thd,hde->the", key_blk, after_low, preferred_element_type=jnp.float32)
    ) / DH
    flat = (length, head_count * DH)
    return (
        grad_query.astype(jnp.bfloat16).reshape(flat),
        grad_key.astype(jnp.bfloat16).reshape(flat),
        grad_value.astype(jnp.bfloat16).reshape(flat),
    )


def softmax_head(query_heads, grad_heads, key_win, value_win, visible):
    head_count, length, features = query_heads.shape
    per_turn = min(head_count, max(1, 512 // length))
    turn_count = head_count // per_turn
    query_steps = query_heads.reshape(turn_count, per_turn * length, features)
    grad_steps = grad_heads.reshape(turn_count, per_turn * length, features)
    visible_rows = jnp.tile(visible, (per_turn, 1))
    score_scale = DH ** (-0.5)
    contract_last = (((1,), (1,)), ((), ()))
    contract_first = (((0,), (0,)), ((), ()))

    def one_turn(running_sums, pieces):
        query_rows, grad_rows = pieces
        scores = (
            lax.dot_general(query_rows, key_win, contract_last, preferred_element_type=jnp.float32)
            * score_scale
        )
        scores = jnp.where(visible_rows, scores, -1e30)
        highest = jnp.max(scores, axis=1, keepdims=True)
        raised = jnp.where(visible_rows, jnp.exp(scores - highest), 0.0)
        attention = raised / jnp.sum(raised, axis=1, keepdims=True)
        prob_low = attention.astype(jnp.bfloat16)
        output = jnp.dot(prob_low, value_win, preferred_element_type=jnp.float32)
        row_delta = jnp.sum(grad_rows.astype(jnp.float32) * output, axis=1, keepdims=True)
        grad_probs = lax.dot_general(
            grad_rows, value_win, contract_last, preferred_element_type=jnp.float32
        )
        dscore = (attention * (grad_probs - row_delta) * score_scale).astype(jnp.bfloat16)
        grad_query = jnp.dot(dscore, key_win, preferred_element_type=jnp.float32).astype(
            jnp.bfloat16
        )
        part_key = lax.dot_general(
            dscore, query_rows, contract_first, preferred_element_type=jnp.float32
        )
        part_value = lax.dot_general(
            prob_low, grad_rows, contract_first, preferred_element_type=jnp.float32
        )
        return ((running_sums[0] + part_key, running_sums[1] + part_value), grad_query)

    zero_rows = jnp.zeros((key_win.shape[0], features), jnp.float32)
    sums_out, grad_query = lax.scan(one_turn, (zero_rows, zero_rows), (query_steps, grad_steps))
    return (sums_out[0], sums_out[1], grad_query.reshape(head_count, length, features))


def softmax_part(soft_query, soft_keys, soft_values, soft_grad, doc_lengths):
    length = soft_query.shape[0]
    kv_local = soft_keys.shape[1] // DH
    group_size = Q_HEADS // KV_HEADS
    device = lax.axis_index("ctx")
    stacked = jnp.stack([soft_keys, soft_values])
    arrived = [stacked] + [passed_along(stacked, "ctx", offset) for offset in range(1, SUB)]
    window = jnp.concatenate(arrived[::-1], axis=1)
    query_pos = device * length + jnp.arange(length, dtype=jnp.int32)
    key_pos = (device - (SUB - 1)) * length + jnp.arange(SUB * length, dtype=jnp.int32)
    visible = (
        (key_pos[None, :] <= query_pos[:, None])
        & (key_pos[None, :] >= 0)
        & (
            document_of(key_pos, doc_lengths)[None, :]
            == document_of(query_pos, doc_lengths)[:, None]
        )
    )
    query_split = soft_query.reshape(length, kv_local, group_size, DH)
    grad_split = soft_grad.reshape(length, kv_local, group_size, DH)
    key_win = window[0, :, 0:DH]
    value_win = window[1, :, 0:DH]
    query_heads = jnp.transpose(query_split[:, 0], (1, 0, 2))
    grad_heads = jnp.transpose(grad_split[:, 0], (1, 0, 2))
    grad_key, grad_value, grad_query = softmax_head(
        query_heads, grad_heads, key_win, value_win, visible
    )
    query_grads = [jnp.transpose(grad_query, (1, 0, 2))]
    soft_dq = jnp.stack(query_grads, axis=1).reshape(length, kv_local * group_size * DH)
    partial_value = jnp.stack([grad_key, grad_value])

    def block_of(offset):
        slot = SUB - 1 - offset
        return partial_value[:, slot * length : (slot + 1) * length]

    summed = block_of(0)
    for offset in range(1, SUB):
        summed = summed + passed_along(block_of(offset), "ctx", -offset)
    return (soft_dq, summed[0].astype(jnp.bfloat16), summed[1].astype(jnp.bfloat16))


def per_device(
    lin_query,
    lin_keys,
    lin_values,
    lin_grad,
    norm_gain,
    log_decay,
    state_in,
    soft_query,
    soft_keys,
    soft_values,
    soft_grad,
    projections,
    doc_lengths,
):
    soft_dq, soft_dk, soft_dv = softmax_part(
        soft_query, soft_keys, soft_values, soft_grad, doc_lengths
    )
    kv_grads = jnp.stack([soft_dk, soft_dv], axis=1)
    carried_back = lax.psum_scatter(
        jnp.einsum("crk,tck->rt", projections, kv_grads, preferred_element_type=jnp.float32),
        "head",
        scatter_dimension=0,
        tiled=True,
    )
    cotangent = lin_grad.astype(jnp.float32) + carried_back.T
    lin_dq, lin_dk, lin_dv = lightning_part(
        lin_query, lin_keys, lin_values, cotangent, norm_gain, log_decay, state_in
    )
    return (lin_dq, lin_dk, lin_dv, soft_dq, soft_dk, soft_dv)


def solution(mesh):
    in_specs = (
        P("ctx", "head"),
        P("ctx", "head"),
        P("ctx", "head"),
        P("ctx", "head"),
        P("head"),
        P("head", None),
        P("ctx", "head", None, None),
        P("ctx", "head"),
        P("ctx", "head"),
        P("ctx", "head"),
        P("ctx", "head"),
        P(None, None, "head"),
        P(),
    )
    out_specs = (
        P("ctx", "head"),
        P("ctx", "head"),
        P("ctx", "head"),
        P("ctx", "head"),
        P("ctx", "head"),
        P("ctx", "head"),
    )
    return jax.shard_map(
        per_device, mesh=mesh, in_specs=in_specs, out_specs=out_specs, check_vma=False
    )
```

profile of v0, /device:TPU:32, one launch (start us, length us, event | category | flops | bytes accessed | tf_op | source)
XLA Modules:
  0.0 368.0 jit_solution(18281954963981145327)
XLA Ops:
  7.2 1.0 pad_maximum_fusion.1
  8.3 3.8 %collective-permute-start.2 = (bf16[2,256,128]{2,1,0:T(8,128)(2,1)S(1)}, bf16[2,256,128]{2,1,0:T(8,128)(2,1)S(1)}, u32[]{:S(2)}, u32[]{:S(2)}) collective-permute-start(bf16[2,256,128]{2,1,0:T(8,128)(2,1)S(1)} %pad_maximum_fusion.1), channel_id=1, source_target_pairs={{0,8},{8,16},{16,24},{24,32},{32,40},{40,48},{48,56},{56,64},{64,7... | collective-permute-start | bytes 393224 | tf_op jit(solution)/shard_map/ppermute | solution.py:20
  12.1 7.0 %collective-permute-start.1 = (bf16[2,256,128]{2,1,0:T(8,128)(2,1)S(1)}, bf16[2,256,128]{2,1,0:T(8,128)(2,1)}, u32[]{:S(2)}, u32[]{:S(2)}) collective-permute-start(bf16[2,256,128]{2,1,0:T(8,128)(2,1)S(1)} %pad_maximum_fusion.1), channel_id=1, source_target_pairs={{0,16},{8,24},{16,32},{24,40},{32,48},{40,56},{48,64},{56,72},{64,... | collective-permute-start | bytes 393224 | tf_op jit(solution)/shard_map/ppermute | solution.py:20
  19.2 6.5 %collective-permute-start = (bf16[2,256,128]{2,1,0:T(8,128)(2,1)S(1)}, bf16[2,256,128]{2,1,0:T(8,128)(2,1)}, u32[]{:S(2)}, u32[]{:S(2)}) collective-permute-start(bf16[2,256,128]{2,1,0:T(8,128)(2,1)S(1)} %pad_maximum_fusion.1), channel_id=1, source_target_pairs={{0,24},{8,32},{16,40},{24,48},{32,56},{40,64},{48,72},{56,80},{64,... | collective-permute-start | bytes 393224 | tf_op jit(solution)/shard_map/ppermute | solution.py:20
  27.4 1.9 copy_bitcast_fusion.1
  29.3 1.2 copy.123
  30.6 1.0 copy.124
  31.6 1.0 compare_and_fusion
  32.8 1.0 maximum_maximum_fusion
  33.8 39.3 %while.15 = (s32[]{:T(128)}, f32[1024,128]{1,0:T(8,128)}, f32[1024,128]{1,0:T(8,128)S(1)}, bf16[4,512,128]{2,1,0:T(8,128)(2,1)}, bf16[4,512,128]{2,1,0:T(8,128)(...) while((s32[]{:T(128)}, f32[1024,128]{1,0:T(8,128)}, ...), condition=%wide.region_7.8_spmd.clone, body=%wide.region_3.7_spmd.clone.sunk | while | flops 816052736 | bytes 27801824 | solution.py:155
  33.8 0.9 constant_dynamic-slice_fusion.3
  34.8 0.8 copy.205
  35.5 1.5 fusion.122
  37.1 0.8 fusion.123
  41.0 1.5 convolution_add_fusion.5
  42.6 1.1 fusion.126
  43.7 0.9 constant_dynamic-slice_fusion.3
  45.4 1.5 fusion.122
  46.9 0.8 fusion.123
  50.9 1.5 convolution_add_fusion.5
  52.4 1.1 fusion.126
  53.5 0.9 constant_dynamic-slice_fusion.3
  55.2 1.5 fusion.122
  56.7 0.8 fusion.123
  60.7 1.5 convolution_add_fusion.5
  62.2 1.1 fusion.126
  63.3 0.9 constant_dynamic-slice_fusion.3
  65.0 1.5 fusion.122
  66.5 0.8 fusion.123
  70.5 1.5 convolution_add_fusion.5
  72.0 1.1 fusion.126
  73.1 1.1 fusion.43
  74.3 1.9 collective-permute-start.3
  76.2 1.3 collective-permute-start.5
  77.5 1.3 collective-permute-start.4
  78.8 10.3 %collective-permute-done.3 = f32[2,256,128]{2,1,0:T(8,128)S(1)} collective-permute-done((f32[2,256,128]{2,1,0:T(8,128)S(1)}, f32[2,256,128]{2,1,0:T(8,128)S(1)}, u32[]{:S(2)}, u32[]{:S(2)}) %collective-permute-start.3) | collective-permute-done | bytes 262176 | tf_op jit(solution)/shard_map/ppermute | solution.py:20
  89.1 19.3 %collective-permute-done.5 = f32[2,256,128]{2,1,0:T(8,128)S(1)} collective-permute-done((f32[2,256,128]{2,1,0:T(8,128)S(1)}, f32[2,256,128]{2,1,0:T(8,128)S(1)}, u32[]{:S(2)}, u32[]{:S(2)}) %collective-permute-start.5) | collective-permute-done | bytes 262176 | tf_op jit(solution)/shard_map/ppermute | solution.py:20
  108.5 4.6 %collective-permute-done.4 = f32[2,256,128]{2,1,0:T(8,128)S(1)} collective-permute-done((f32[2,256,128]{2,1,0:T(8,128)S(1)}, f32[2,256,128]{2,1,0:T(8,128)S(1)}, u32[]{:S(2)}, u32[]{:S(2)}) %collective-permute-start.4) | collective-permute-done | bytes 262176 | tf_op jit(solution)/shard_map/ppermute | solution.py:20
  113.8 2.7 convolution_bitcast_fusion
  117.3 1.2 reduce-window.19
  120.4 0.8 copy-done.5
  121.2 1.1 fusion.44
  122.3 42.6 %reduce-scatter.2.cloned.1.call-done = f32[512,256]{0,1:T(8,128)} async-done(((f32[4096,256]{0,1:T(8,128)}), f32[512,256]{0,1:T(8,128)}) %reduce-scatter.2.cloned.1.call-update) | async-done | bytes 524304 | tf_op jit(solution)/shard_map/reduce_scatter | solution.py:219
  164.9 1.9 bitcast_add_fusion
  166.8 1.2 copy.159
  168.1 2.2 fusion.36
  170.3 13.1 %all-reduce.1 = (f32[256]{0:T(256)S(1)}, f32[256]{0:T(256)S(1)}) all-reduce(f32[256]{0:T(256)S(1)} %get-tuple-element.158, f32[256]{0:T(256)S(1)} %get-tuple-element.157), channel_id=1, replica_groups=mesh['ctx'=64,'head'=8] {'head'}, use_global_device_ids=true, to_apply=%region_14.15 | all-reduce | flops 512 | bytes 4096 | tf_op jit(solution)/shard_map/psum | solution.py:58
  183.4 1.2 fusion.35
  184.6 0.9 convolution_convert_fusion.1
  185.5 1.1 bitcast_reduce_fusion
  187.1 1.4 copy.145
  188.5 0.9 copy.202
  189.4 1.5 fusion.22
  190.9 0.9 copy-done.8
  192.3 0.8 copy.146
  193.1 1.1 convolution_bitcast_fusion.4
  194.2 1.3 convolution_bitcast_fusion.1
  195.5 146.7 %all-gather.3.cloned.1.call-done = bf16[256,128,128]{2,1,0:T(8,128)(2,1)} async-done(((bf16[4,128,128]{2,1,0:T(8,128)(2,1)}), bf16[256,128,128]{2,1,0:T(8,128)(2,1)}) %all-gather.3.cloned.1.call-update) | async-done | bytes 8388624 | tf_op jit(solution)/shard_map/all_gather | solution.py:85
  342.2 12.2 %fusion.19 = bf16[4,1,128,128]{3,1,2,0:T(2,128)(2,1)} fusion(f32[4,64,1,1]{1,2,3,0:T(1,128)S(1)} %bitcast.267, bf16[64,4,128,128]{3,2,1,0:T(8,128)(2,1)} %bitcast.244), kind=kOutput, calls=%fused_computation.26 | convolution fusion | flops 50331648 | bytes 8520704 | tf_op jit(solution)/shard_map/hn,nhde->hde/dot_general | solution.py:92
  354.3 1.1 copy.157
  355.4 1.9 fusion.33
  357.3 1.8 copy.148
  359.1 1.2 fusion.34
  360.3 0.8 copy.147
  (114 shorter events, 21.1 us)
Async XLA Ops:
  7.2 106.6 %copy-start = (bf16[2,4096,128]{2,1,0:T(8,128)(2,1)S(1)}, bf16[2,4096,128]{2,1,0:T(8,128)(2,1)}, u32[]{:S(2)}) copy-start(bf16[2,4096,128]{2,1,0:T(8,128)(2,1)} %param.26) | copy-start | bytes 6291460
  7.2 25.6 %copy-start.14 = (bf16[256,128]{1,0:T(8,128)(2,1)S(1)}, bf16[256,128]{1,0:T(8,128)(2,1)}, u32[]{:S(2)}) copy-start(bf16[256,128]{1,0:T(8,128)(2,1)} %param.24) | copy-start | bytes 196612
  7.2 25.6 %copy-start.15 = (bf16[256,128]{1,0:T(8,128)(2,1)S(1)}, bf16[256,128]{1,0:T(8,128)(2,1)}, u32[]{:S(2)}) copy-start(bf16[256,128]{1,0:T(8,128)(2,1)} %param.23) | copy-start | bytes 196612
  7.2 157.7 %reduce-scatter.2.cloned.1.call-start = ((), (), s32[]{:S(2)}) async-start(), calls=%async_computation.1 | async-start | bytes 4718592 | tf_op jit(solution)/shard_map/reduce_scatter | solution.py:219
  8.3 24.3 %collective-permute-start.2 = (bf16[2,256,128]{2,1,0:T(8,128)(2,1)S(1)}, bf16[2,256,128]{2,1,0:T(8,128)(2,1)S(1)}, u32[]{:S(2)}, u32[]{:S(2)}) collective-permute-start(bf16[2,256,128]{2,1,0:T(8,128)(2,1)S(1)} %pad_maximum_fusion.1), channel_id=1, source_target_pairs={{0,8},{8,16},{16,24},{24,32},{32,40},{40,48},{48,56},{56,64},{64,7... | collective-permute-start | bytes 393224 | tf_op jit(solution)/shard_map/ppermute | solution.py:20
  12.1 20.5 %collective-permute-start.1 = (bf16[2,256,128]{2,1,0:T(8,128)(2,1)S(1)}, bf16[2,256,128]{2,1,0:T(8,128)(2,1)}, u32[]{:S(2)}, u32[]{:S(2)}) collective-permute-start(bf16[2,256,128]{2,1,0:T(8,128)(2,1)S(1)} %pad_maximum_fusion.1), channel_id=1, source_target_pairs={{0,16},{8,24},{16,32},{24,40},{32,48},{40,56},{48,64},{56,72},{64,... | collective-permute-start | bytes 393224 | tf_op jit(solution)/shard_map/ppermute | solution.py:20
  19.2 13.6 %collective-permute-start = (bf16[2,256,128]{2,1,0:T(8,128)(2,1)S(1)}, bf16[2,256,128]{2,1,0:T(8,128)(2,1)}, u32[]{:S(2)}, u32[]{:S(2)}) collective-permute-start(bf16[2,256,128]{2,1,0:T(8,128)(2,1)S(1)} %pad_maximum_fusion.1), channel_id=1, source_target_pairs={{0,24},{8,32},{16,40},{24,48},{32,56},{40,64},{48,72},{56,80},{64,... | collective-permute-start | bytes 393224 | tf_op jit(solution)/shard_map/ppermute | solution.py:20
  37.9 0.9 copy-start.4
  40.0 1.0 copy-start.1
  42.5 1.1 copy-start.2
  47.7 0.9 copy-start.4
  49.8 1.0 copy-start.1
  52.4 1.1 copy-start.2
  57.5 0.9 copy-start.4
  59.6 1.0 copy-start.1
  62.2 1.1 copy-start.2
  67.4 0.9 copy-start.4
  69.4 1.0 copy-start.1
  72.0 1.1 copy-start.2
  73.1 39.9 %copy-start.3 = (f32[1024,128]{1,0:T(8,128)S(1)}, f32[1024,128]{1,0:T(8,128)}, u32[]{:S(2)}) copy-start(f32[1024,128]{1,0:T(8,128)} %get-tuple-element.55) | copy-start | bytes 1572868
  74.3 14.9 %collective-permute-start.3 = (f32[2,256,128]{2,1,0:T(8,128)S(1)}, f32[2,256,128]{2,1,0:T(8,128)S(1)}, u32[]{:S(2)}, u32[]{:S(2)}) collective-permute-start(f32[2,256,128]{2,1,0:T(8,128)S(1)} %get-tuple-element.181), channel_id=1, source_target_pairs={{8,0},{16,8},{24,16},{32,24},{40,32},{48,40},{56,48},{64,56},{72,6... | collective-permute-start | bytes 786440 | tf_op jit(solution)/shard_map/ppermute | solution.py:20
  76.2 32.3 %collective-permute-start.5 = (f32[2,256,128]{2,1,0:T(8,128)S(1)}, f32[2,256,128]{2,1,0:T(8,128)S(1)}, u32[]{:S(2)}, u32[]{:S(2)}) collective-permute-start(f32[2,256,128]{2,1,0:T(8,128)S(1)} %get-tuple-element.182), channel_id=1, source_target_pairs={{24,0},{32,8},{40,16},{48,24},{56,32},{64,40},{72,48},{80,56},{88,... | collective-permute-start | bytes 786440 | tf_op jit(solution)/shard_map/ppermute | solution.py:20
  77.5 35.5 %collective-permute-start.4 = (f32[2,256,128]{2,1,0:T(8,128)S(1)}, f32[2,256,128]{2,1,0:T(8,128)S(1)}, u32[]{:S(2)}, u32[]{:S(2)}) collective-permute-start(f32[2,256,128]{2,1,0:T(8,128)S(1)} %get-tuple-element.183), channel_id=1, source_target_pairs={{16,0},{24,8},{32,16},{40,24},{48,32},{56,40},{64,48},{72,56},{80,... | collective-permute-start | bytes 786440 | tf_op jit(solution)/shard_map/ppermute | solution.py:20
  116.4 2.6 copy-start.13
  116.5 3.4 copy-start.9
  116.5 4.7 %copy-start.10 = (bf16[256,512]{1,0:T(8,128)(2,1)S(1)}, bf16[256,512]{1,0:T(8,128)(2,1)}, u32[]{:S(2)}) copy-start(bf16[256,512]{1,0:T(8,128)(2,1)} %param.17) | copy-start | bytes 786436
  116.5 225.7 %all-gather.3.cloned.1.call-start = ((), (), s32[]{:S(2)}) async-start(), calls=%async_computation.2 | async-start | bytes 8519680 | tf_op jit(solution)/shard_map/all_gather | solution.py:85
  118.6 46.3 %copy-start.12 = (bf16[256,512]{1,0:T(8,128)(2,1)S(1)}, bf16[256,512]{1,0:T(8,128)(2,1)}, u32[]{:S(2)}) copy-start(bf16[256,512]{1,0:T(8,128)(2,1)} %param.18) | copy-start | bytes 786436
  119.3 0.6 copy-start.16
  120.4 0.8 copy-start.5
  121.2 46.9 %copy-start.11 = (bf16[1,4,128,128]{3,2,1,0:T(8,128)(2,1)S(1)}, bf16[1,4,128,128]{3,2,1,0:T(8,128)(2,1)}, u32[]{:S(2)}) copy-start(bf16[1,4,128,128]{3,2,1,0:T(8,128)(2,1)} %param.21) | copy-start | bytes 393220
  121.2 46.9 %copy-start.17 = (f32[512]{0:T(512)S(1)}, f32[512]{0:T(512)}, u32[]{:S(2)}) copy-start(f32[512]{0:T(512)} %param.19) | copy-start | bytes 6148
  189.4 3.7 %copy-start.6 = (bf16[4,256,256]{2,1,0:T(8,128)(2,1)S(1)}, bf16[4,256,256]{2,1,0:T(8,128)(2,1)}, u32[]{:S(2)}) copy-start(bf16[4,256,256]{2,1,0:T(8,128)(2,1)} %copy-done.5) | copy-start | bytes 1572868
  190.9 0.9 copy-start.8
  342.2 13.3 %copy-start.7 = (f32[256,4,128]{0,2,1:T(8,128)S(1)}, f32[256,4,128]{0,2,1:T(8,128)}, u32[]{:S(2)}) copy-start(f32[256,4,128]{0,2,1:T(8,128)} %convolution_bitcast_fusion.4) | copy-start | bytes 1572868
Sparse Core Ops, SparseCore 0:
  116.6 48.2 reduce-scatter.1
  185.7 156.4 all-gather.2
where the time goes:
time: 369 us; the launch traced here: 368 us
  waiting for transfers between devices  224 us (61%)
  matrix products  49.9 us (14%)
  local copies, waits for them, and re-layouts  27.2 us (7%)
  starting transfers between devices  22 us (6%)
  other arithmetic  17.5 us (5%)
  between operations  14.3 us (4%)
  blocking collectives  13.1 us (4%)
    all_gather x1, waiting for transfers between devices, lightning_part(): block_in = lax.all_gather(summary[None], 'ctx', axis=0, tiled=True)  147 us
    reduce_scatter x1, waiting for transfers between devices, per_device(): lax.psum_scatter(jnp.einsum('crk,tck->rt', projections, kv_grads, preferr...  42.6 us
    ppermute x6, waiting for transfers between devices, passed_along(): return lax.ppermute(block, axis, route)  34.4 us
    ppermute x6, starting transfers between devices, passed_along(): return lax.ppermute(block, axis, route)  21.9 us
    psum x1, blocking collectives, lightning_part(): lax.psum((jnp.sum(lin_out * lin_out, axis=(1, 2)), jnp.sum(gated * lin_ou...  13.1 us
    dot_general x1, matrix products, lightning_part(): jnp.einsum('hn,nhde->hde', factors, block_in.astype(jnp.float32), precisi...  12.2 us
    unnamed x38, local copies, waits for them, and re-layouts  8.16 us
  transfers between devices with their start and end apart: 8, of which 6 were waited for; matrix products, arithmetic and copies ran while one was open for 6% of the time, Pallas kernels for 0%

commit v1 on v0

v1 whole, which is shorter than its diff:
```python
import functools
import math

import jax
import jax.numpy as jnp
from jax import lax
from jax.experimental import pallas as pl
from jax.experimental.pallas import tpu as pltpu
from jax.sharding import PartitionSpec as P

DH = 128
Q_HEADS = 64
KV_HEADS = 8
GROUP = Q_HEADS // KV_HEADS
LIGHTNING_HEADS = 32
FEATURES = LIGHTNING_HEADS * DH
SUB = 4
QUAD = 4
epsilon = 1e-06

F32 = jnp.float32
BF16 = jnp.bfloat16
NT = (((1,), (1,)), ((), ()))
NN = (((1,), (0,)), ((), ()))
TN = (((0,), (0,)), ((), ()))
VMEM_LIMIT = 48 * 1024 * 1024


def mm(a, b, dims=NN):
    return lax.dot_general(a, b, dims, preferred_element_type=F32)


def iota2(shape, dim):
    return lax.broadcasted_iota(jnp.int32, shape, dim)


def to_column(row):
    n = row.shape[1]
    return jnp.sum(jnp.where(iota2((n, n), 0) == iota2((n, n), 1), row, 0.0), axis=1, keepdims=True)


def to_row(column):
    n = column.shape[0]
    return jnp.sum(jnp.where(iota2((n, n), 0) == iota2((n, n), 1), column, 0.0), axis=0, keepdims=True)


def decay_sums(log_row):
    n = log_row.shape[1]
    first, second = iota2((n, n), 0), iota2((n, n), 1)
    g_col = jnp.sum(jnp.where(second <= first, log_row, 0.0), axis=1, keepdims=True)
    return g_col, to_row(g_col)


def softmax_kernel(
    length, base_ref, lens_ref, q_ref, do_ref, kv3, kv2, kv1, kv0,
    dq_ref, part3, part2, part1, own, k_win, v_win, k_t, bias, acc_k, acc_v,
):
    step = pl.program_id(0)
    window = SUB * length
    scale = DH ** -0.5

    @pl.when(step == 0)
    def _():
        for slot, kv in enumerate((kv3, kv2, kv1, kv0)):
            rows = slice(slot * length, (slot + 1) * length)
            k_win[rows, :] = kv[0]
            v_win[rows, :] = kv[1]
            k_t[:, rows] = kv[0].astype(F32).T.astype(BF16)
        docs = lens_ref.shape[1]
        lens = jnp.where(iota2((docs, docs), 1) <= iota2((docs, docs), 0), lens_ref[...], 0)
        ends = jnp.sum(lens, axis=1, keepdims=True)
        base = base_ref[0]
        t_row = base + iota2((docs, length), 1)
        start = jnp.max(jnp.where(ends <= t_row, ends, 0), axis=0, keepdims=True)
        s_pos = base - (SUB - 1) * length + iota2((window, length), 0)
        t_pos = base + iota2((window, length), 1)
        visible = (s_pos <= t_pos) & (s_pos >= start)
        bias[...] = jnp.where(visible, 0.0, -1e30)
        acc_k[...] = jnp.zeros_like(acc_k)
        acc_v[...] = jnp.zeros_like(acc_v)

    q = q_ref[...]
    do = do_ref[...]
    scores = mm(k_win[...], q, NT) * (scale * math.log2(math.e)) + bias[...]
    highest = jnp.max(scores, axis=0, keepdims=True)
    raised = jnp.exp2(scores - highest)
    inverse = 1.0 / jnp.sum(raised, axis=0, keepdims=True)
    prob = raised * inverse
    prob_low = prob.astype(BF16)
    grad_probs = mm(v_win[...], do, NT)
    delta = jnp.sum(prob_low.astype(F32) * grad_probs, axis=0, keepdims=True)
    dscore = (prob * ((grad_probs - delta) * scale)).astype(BF16)
    acc_v[...] += mm(prob_low, do)
    acc_k[...] += mm(dscore, q)
    dq_ref[...] = mm(k_t[...], dscore).T.astype(BF16)

    @pl.when(step == pl.num_programs(0) - 1)
    def _():
        for slot, out in enumerate((part3, part2, part1, own)):
            rows = slice(slot * length, (slot + 1) * length)
            out[:, :DH] = acc_k[rows, :].astype(out.dtype)
            out[:, DH:] = acc_v[rows, :].astype(out.dtype)


def softmax_call(base, lens, q, do, windows):
    length = q.shape[0]
    whole = lambda *shape: pl.BlockSpec(shape, lambda j: (0,) * len(shape))
    per_head = pl.BlockSpec((length, DH), lambda j: (0, j))
    window = SUB * length
    pair = jax.ShapeDtypeStruct((length, 2 * DH), BF16)
    return pl.pallas_call(
        functools.partial(softmax_kernel, length),
        out_shape=(
            jax.ShapeDtypeStruct(q.shape, BF16), pair, pair, pair,
            jax.ShapeDtypeStruct((length, 2 * DH), F32),
        ),
        grid=(GROUP,),
        in_specs=[
            pl.BlockSpec(memory_space=pltpu.SMEM), whole(1, lens.shape[1]), per_head, per_head,
        ] + [whole(2, length, DH)] * SUB,
        out_specs=(per_head,) + (whole(length, 2 * DH),) * SUB,
        scratch_shapes=[
            pltpu.VMEM((window, DH), BF16), pltpu.VMEM((window, DH), BF16),
            pltpu.VMEM((DH, window), BF16), pltpu.VMEM((window, length), F32),
            pltpu.VMEM((window, DH), F32), pltpu.VMEM((window, DH), F32),
        ],
        compiler_params=pltpu.CompilerParams(vmem_limit_bytes=VMEM_LIMIT),
        cost_estimate=pl.CostEstimate(
            flops=10 * GROUP * window * length * DH * 4, bytes_accessed=4 * 1024 * 1024,
            transcendentals=GROUP * window * length,
        ),
        name="softmax_backward",
    )(base, lens, q, do, *windows)


def forward_kernel(block_ref, q_ref, k_ref, v_ref, log_ref, state_ref, out_ref):
    head = pl.program_id(0)
    length = q_ref.shape[0]
    g_col, g_row = decay_sums(log_ref[pl.ds(head, 1), :])
    causal = iota2((length, length), 0) >= iota2((length, length), 1)
    weights = jnp.where(causal, jnp.exp(jnp.minimum(g_col - g_row, 0.0)), 0.0)
    near = (mm(q_ref[...], k_ref[...], NT) * weights).astype(BF16)
    scaled = (q_ref[...].astype(F32) * jnp.exp(g_col)).astype(BF16)
    out_ref[...] = (mm(near, v_ref[...]) + mm(scaled, state_ref[0, 0])) * (1.0 / DH)


def per_head_spec(length):
    return pl.BlockSpec((length, DH), lambda h, b: (0, h))


def state_spec():
    return pl.BlockSpec((1, 1, DH, DH), lambda h, b: (0, h, 0, 0))


def log_spec(heads, length):
    return pl.BlockSpec((heads, length), lambda h, b: (0, b[0]))


def forward_call(block, q, k, v, log_decay, state):
    length, heads = q.shape[0], q.shape[1] // DH
    wide = per_head_spec(length)
    return pl.pallas_call(
        forward_kernel,
        out_shape=jax.ShapeDtypeStruct(q.shape, F32),
        grid_spec=pltpu.PrefetchScalarGridSpec(
            num_scalar_prefetch=1, grid=(heads,),
            in_specs=[wide, wide, wide, log_spec(heads, length), state_spec()],
            out_specs=wide,
        ),
        cost_estimate=pl.CostEstimate(
            flops=heads * length * DH * (4 * length + 2 * DH) * 8, bytes_accessed=2 * 1024 * 1024,
            transcendentals=heads * length * length,
        ),
        name="lightning_forward",
    )(block, q, k, v, log_decay, state)


def cotangent_kernel(dkv_ref, proj_ref, grad_ref, gain_ref, out_ref, gated_ref, stats_ref):
    total = grad_ref[...].astype(F32)
    for g in range(KV_HEADS):
        for side in range(2):
            total += mm(dkv_ref[g, :, side * DH:(side + 1) * DH], proj_ref[side, g], NT)
    gated = gain_ref[...] * total
    gated_ref[...] = gated
    out = out_ref[...]
    squares = to_row(jnp.sum(out * out, axis=1, keepdims=True))
    cross = to_row(jnp.sum(gated * out, axis=1, keepdims=True))
    rows = iota2(stats_ref.shape, 0)
    stats_ref[...] = jnp.where(rows == 0, squares, jnp.where(rows == 1, cross, 0.0))


def cotangent_call(dkv, proj, grad, gain, out):
    length, width = grad.shape
    return pl.pallas_call(
        cotangent_kernel,
        out_shape=(
            jax.ShapeDtypeStruct((length, width), F32), jax.ShapeDtypeStruct((8, length), F32),
        ),
        compiler_params=pltpu.CompilerParams(vmem_limit_bytes=VMEM_LIMIT),
        name="cotangent",
    )(dkv, proj, grad, gain, out)


def dout_kernel(block_ref, stats_ref, gated_ref, out_ref, q_ref, log_ref, dout_ref, summary_ref):
    head = pl.program_id(0)
    g_col, _ = decay_sums(log_ref[pl.ds(head, 1), :])
    squares = to_column(stats_ref[0:1, :])
    cross = to_column(stats_ref[1:2, :])
    spread = jnp.sqrt(squares * (1.0 / FEATURES) + epsilon)
    inverse = 1.0 / spread
    factor = cross * (inverse * inverse * inverse) * (1.0 / FEATURES)
    dout = (gated_ref[...] * inverse - out_ref[...] * factor).astype(BF16)
    dout_ref[...] = dout
    scaled = (q_ref[...].astype(F32) * jnp.exp(g_col)).astype(BF16)
    summary_ref[0] = mm(scaled, dout, TN).astype(BF16)


def dout_call(block, stats, gated, out, q, log_decay):
    length, heads = q.shape[0], q.shape[1] // DH
    wide = per_head_spec(length)
    return pl.pallas_call(
        dout_kernel,
        out_shape=(jax.ShapeDtypeStruct(q.shape, BF16), jax.ShapeDtypeStruct((heads, DH, DH), BF16)),
        grid_spec=pltpu.PrefetchScalarGridSpec(
            num_scalar_prefetch=1, grid=(heads,),
            in_specs=[
                pl.BlockSpec((8, length), lambda h, b: (0, 0)), wide, wide, wide,
                log_spec(heads, length),
            ],
            out_specs=(wide, pl.BlockSpec((1, DH, DH), lambda h, b: (h, 0, 0))),
        ),
        name="dout_summary",
    )(block, stats, gated, out, q, log_decay)


def near_far_kernel(
    block_ref, q_ref, k_ref, v_ref, dout_ref, log_ref, state_ref, dq_ref, dk_ref, dv_ref
):
    head = pl.program_id(0)
    length = q_ref.shape[0]
    g_col, g_row = decay_sums(log_ref[pl.ds(head, 1), :])
    first, second = iota2((length, length), 0), iota2((length, length), 1)
    gap = g_col - g_row
    weights = jnp.where(first >= second, jnp.exp(jnp.minimum(gap, 0.0)), 0.0)
    turned = jnp.where(second >= first, jnp.exp(jnp.minimum(-gap, 0.0)), 0.0)
    q, k, v, dout = q_ref[...], k_ref[...], v_ref[...], dout_ref[...]
    far = (mm(dout, v, NT) * weights).astype(BF16)
    far_turned = (mm(v, dout, NT) * turned).astype(BF16)
    near_turned = (mm(k, q, NT) * turned).astype(BF16)
    dq = mm(far, k) + jnp.exp(g_col) * mm(dout, state_ref[0, 0], NT)
    dq_ref[...] = (dq * (1.0 / DH)).astype(BF16)
    dk_ref[...] = mm(far_turned, q)
    dv_ref[...] = mm(near_turned, dout)


def near_far_call(block, q, k, v, dout, log_decay, state):
    length, heads = q.shape[0], q.shape[1] // DH
    wide = per_head_spec(length)
    return pl.pallas_call(
        near_far_kernel,
        out_shape=(
            jax.ShapeDtypeStruct(q.shape, BF16), jax.ShapeDtypeStruct(q.shape, F32),
            jax.ShapeDtypeStruct(q.shape, F32),
        ),
        grid_spec=pltpu.PrefetchScalarGridSpec(
            num_scalar_prefetch=1, grid=(heads,),
            in_specs=[wide, wide, wide, wide, log_spec(heads, length), state_spec()],
            out_specs=(wide, wide, wide),
        ),
        cost_estimate=pl.CostEstimate(
            flops=heads * length * DH * (12 * length + 2 * DH) * 8, bytes_accessed=4 * 1024 * 1024,
            transcendentals=2 * heads * length * length,
        ),
        name="near_far",
    )(block, q, k, v, dout, log_decay, state)


def last_kernel(block_ref, k_ref, v_ref, dk_ref, dv_ref, after_ref, log_ref, dk_out, dv_out):
    head = pl.program_id(0)
    length = k_ref.shape[0]
    log_row = log_ref[pl.ds(head, 1), :]
    first, second = iota2((length, length), 0), iota2((length, length), 1)
    tail = jnp.exp(jnp.sum(jnp.where(second > first, log_row, 0.0), axis=1, keepdims=True))
    after = after_ref[0]
    dk_out[...] = ((dk_ref[...] + tail * mm(v_ref[...], after, NT)) * (1.0 / DH)).astype(BF16)
    dv_out[...] = ((dv_ref[...] + tail * mm(k_ref[...], after)) * (1.0 / DH)).astype(BF16)


def last_call(block, k, v, dk, dv, after, log_decay):
    length, heads = k.shape[0], k.shape[1] // DH
    wide = per_head_spec(length)
    return pl.pallas_call(
        last_kernel,
        out_shape=(jax.ShapeDtypeStruct(k.shape, BF16), jax.ShapeDtypeStruct(k.shape, BF16)),
        grid_spec=pltpu.PrefetchScalarGridSpec(
            num_scalar_prefetch=1, grid=(heads,),
            in_specs=[
                wide, wide, wide, wide, pl.BlockSpec((1, DH, DH), lambda h, b: (h, 0, 0)),
                log_spec(heads, length),
            ],
            out_specs=(wide, wide),
        ),
        name="last",
    )(block, k, v, dk, dv, after, log_decay)


def total_kernel(weight_ref, blocks_ref, total_ref):
    total = jnp.zeros(total_ref.shape, F32)
    for z in range(QUAD):
        total += weight_ref[z] * blocks_ref[z].astype(F32)
    total_ref[...] = total.astype(total_ref.dtype)


def after_kernel(inner_ref, carry_ref, leave_ref, blocks_ref, totals_ref, after_ref):
    carry = jnp.zeros(after_ref.shape[1:], F32)
    for g in range(totals_ref.shape[0]):
        carry += carry_ref[g] * totals_ref[g].astype(F32)
    for z in range(QUAD):
        after = leave_ref[z] * carry
        for later in range(z + 1, QUAD):
            after += inner_ref[z, later] * blocks_ref[later].astype(F32)
        after_ref[z] = after.astype(BF16)


def state_weights(log_decay, length, device):
    place = device % QUAD
    group = device // QUAD
    row = lax.dynamic_slice_in_dim(log_decay, place, 1, 0)
    gamma = jnp.sum(row.reshape(-1, length), axis=1)
    count = gamma.shape[0]
    block = jnp.arange(count, dtype=jnp.int32)
    groups = count // QUAD
    quad = jnp.arange(QUAD, dtype=jnp.int32)
    start = group * QUAD

    def factor(low, high):
        inside = (block > low[..., None]) & (block < high[..., None])
        return jnp.exp(jnp.sum(jnp.where(inside, gamma, 0.0), axis=-1))

    enter = factor(jnp.broadcast_to(start - 1, (QUAD,)), start + quad)
    inner = factor((start + quad)[:, None], (start + quad)[None, :])
    leave = factor(start + quad, jnp.broadcast_to(start + QUAD, (QUAD,)))
    later = jnp.arange(groups, dtype=jnp.int32)
    carry = factor(jnp.broadcast_to(start + QUAD - 1, (groups,)), later * QUAD)
    carry = jnp.where(later > group, carry, 0.0)
    return enter, inner, leave, carry


def after_states(summary, weights):
    enter, inner, leave, carry = weights
    count = lax.axis_size("ctx")
    quads = [[g * QUAD + z for z in range(QUAD)] for g in range(count // QUAD)]
    strided = [[g * QUAD + z for g in range(count // QUAD)] for z in range(QUAD)]
    smem = pl.BlockSpec(memory_space=pltpu.SMEM)
    vmem = pl.BlockSpec(memory_space=pltpu.VMEM)
    blocks = lax.all_to_all(summary, "ctx", 0, 0, tiled=True, axis_index_groups=quads)
    total = pl.pallas_call(
        total_kernel, out_shape=jax.ShapeDtypeStruct((DH, DH), BF16),
        in_specs=[smem, vmem], out_specs=vmem, name="group_total",
    )(enter, blocks)
    totals = lax.all_gather(total, "ctx", axis=0, axis_index_groups=strided)
    after = pl.pallas_call(
        after_kernel, out_shape=jax.ShapeDtypeStruct((QUAD, DH, DH), BF16),
        in_specs=[smem, smem, smem, vmem, vmem], out_specs=vmem, name="after_states",
    )(inner, carry, leave, blocks, totals)
    return lax.all_to_all(after, "ctx", 0, 0, tiled=True, axis_index_groups=quads)


def passed_along(block, distance):
    devices = range(lax.axis_size("ctx"))
    route = [(i - distance, i) for i in devices if i - distance in devices]
    return lax.ppermute(block, "ctx", route)


def per_device(
    lin_query, lin_keys, lin_values, lin_grad, norm_gain, log_decay, state_in,
    soft_query, soft_keys, soft_values, soft_grad, projections, doc_lengths,
):
    length = lin_query.shape[0]
    width = lin_query.shape[1]
    device = lax.axis_index("ctx").astype(jnp.int32)
    block = device.reshape(1)

    stacked = jnp.stack([soft_keys, soft_values])
    arrived = [passed_along(stacked, offset) for offset in range(SUB - 1, 0, -1)]
    proj = projections.reshape(2, KV_HEADS, width, DH)
    proj = lax.all_to_all(proj, "head", 1, 1, tiled=True)
    weights = state_weights(log_decay, length, device)
    lin_out = forward_call(block, lin_query, lin_keys, lin_values, log_decay, state_in)

    soft_dq, part3, part2, part1, own = softmax_call(
        block * length, doc_lengths.reshape(1, -1), soft_query, soft_grad, arrived + [stacked]
    )
    summed = own
    for offset, part in ((3, part3), (2, part2), (1, part1)):
        summed = summed + passed_along(part, -offset).astype(F32)
    dkv = summed.astype(BF16)
    soft_dk, soft_dv = dkv[:, :DH], dkv[:, DH:]

    dkv_all = lax.all_gather(dkv, "head", axis=0)
    gated, stats = cotangent_call(dkv_all, proj, lin_grad, norm_gain.reshape(1, width), lin_out)
    stats = lax.psum(stats, "head")
    dout, summary = dout_call(block, stats, gated, lin_out, lin_query, log_decay)
    lin_dq, dk, dv = near_far_call(
        block, lin_query, lin_keys, lin_values, dout, log_decay, state_in
    )
    after = after_states(summary, weights)
    lin_dk, lin_dv = last_call(block, lin_keys, lin_values, dk, dv, after, log_decay)
    return (lin_dq, lin_dk, lin_dv, soft_dq, soft_dk, soft_dv)


def solution(mesh):
    in_specs = (
        P("ctx", "head"), P("ctx", "head"), P("ctx", "head"), P("ctx", "head"),
        P("head"), P("head", None), P("ctx", "head", None, None),
        P("ctx", "head"), P("ctx", "head"), P("ctx", "head"), P("ctx", "head"),
        P(None, None, "head"), P(),
    )
    out_specs = (P("ctx", "head"),) * 6
    return jax.shard_map(
        per_device, mesh=mesh, in_specs=in_specs, out_specs=out_specs, check_vma=False
    )
```

time: 369 us -> 222 us (0.60)
  waiting for transfers between devices: 224 us -> 48.5 us
  blocking collectives: 13.1 us -> 74.9 us
  matrix products: 49.9 us -> 0 us
  Pallas kernels: 0 us -> 33.1 us
  other arithmetic: 17.5 us -> 2.76 us
  local copies, waits for them, and re-layouts: 27.2 us -> 12.9 us
  starting transfers between devices: 22 us -> 34.3 us
    all_gather x1, waiting for transfers between devices: 147 us -> 15.1 us  [per_device(): dkv_all = lax.all_gather(dkv, 'head', axis=0)]
    all_gather x0 -> x1, blocking collectives: none -> 60.7 us  [after_states(): totals = lax.all_gather(total, 'ctx', axis=0, axis_index_groups=strided)]
    dot_general x37 -> x0, matrix products: 49.9 us -> none  [the longest x1 12.2 us: lightning_part(): jnp.einsum('hn,nhde->hde', factors, block_in.astype(jnp.float32), precisi...]
    reduce_scatter x1 -> x0, waiting for transfers between devices: 42.6 us -> none  [per_device(): lax.psum_scatter(jnp.einsum('crk,tck->rt', projections, kv_grads, preferr...]
    pallas_call x0 -> x8, Pallas kernels: none -> 33.1 us  [the longest x1 12.6 us: softmax_call(): pl.pallas_call(functools.partial(softmax_kernel, length), out_shape=(jax....]
    ppermute x6, waiting for transfers between devices: 34.4 us -> 19.5 us  [passed_along(): return lax.ppermute(block, 'ctx', route)]
    all_to_all x0 -> x3, waiting for transfers between devices: none -> 13.9 us  [the longest x1 10.8 us: per_device(): proj = lax.all_to_all(proj, 'head', 1, 1, tiled=True)]
    all_to_all x0 -> x3, starting transfers between devices: none -> 13 us  [the longest x1 5.27 us: after_states(): lax.all_to_all(summary, 'ctx', 0, 0, tiled=True, axis_index_groups=quads)]
  transfers between devices with their start and end apart: 8 -> 10, of which waited for: 6 -> 9; matrix products, arithmetic and copies ran while one was open for 6% -> 4% of each run, Pallas kernels for 0% -> 4%
where the time goes in v1:
time: 222 us; the launch traced here: 221 us
  blocking collectives  74.9 us (34%)
  waiting for transfers between devices  48.5 us (22%)
  starting transfers between devices  34.3 us (15%)
  Pallas kernels  33.1 us (15%)
  between operations  14.2 us (6%)
  local copies, waits for them, and re-layouts  12.9 us (6%)
  other arithmetic  2.76 us (1%)
    all_gather x1, blocking collectives, after_states(): totals = lax.all_gather(total, 'ctx', axis=0, axis_index_groups=strided)  60.7 us
    ppermute x6, starting transfers between devices, passed_along(): return lax.ppermute(block, 'ctx', route)  21.2 us
    ppermute x6, waiting for transfers between devices, passed_along(): return lax.ppermute(block, 'ctx', route)  19.5 us
    all_gather x1, waiting for transfers between devices, per_device(): dkv_all = lax.all_gather(dkv, 'head', axis=0)  15.1 us
    psum x1, blocking collectives, per_device(): stats = lax.psum(stats, 'head')  14.2 us
    pallas_call x1, Pallas kernels, softmax_call(): pl.pallas_call(functools.partial(softmax_kernel, length), out_shape=(jax....  12.6 us
    all_to_all x1, waiting for transfers between devices, per_device(): proj = lax.all_to_all(proj, 'head', 1, 1, tiled=True)  10.8 us
    unnamed x24, local copies, waits for them, and re-layouts  6.06 us
  transfers between devices with their start and end apart: 10, of which 9 were waited for; matrix products, arithmetic and copies ran while one was open for 4% of the time, Pallas kernels for 4%

profile of v1, /device:TPU:32, one launch (start us, length us, event | category | flops | bytes accessed | tf_op | source)
XLA Modules:
  0.0 220.7 jit_solution(13757810600070338759)
XLA Ops:
  7.2 0.9 pad_maximum_fusion.kv0
  8.1 7.7 %collective-permute-start = (bf16[2,256,128]{2,1,0:T(8,128)(2,1)S(1)}, bf16[2,256,128]{2,1,0:T(8,128)(2,1)S(1)}, u32[]{:S(2)}, u32[]{:S(2)}) collective-permute-start(bf16[2,256,128]{2,1,0:T(8,128)(2,1)S(1)} %pad_maximum_fusion.kv0), channel_id=1, source_target_pairs={{0,24},{8,32},{16,40},{24,48},{32,56},{40,64},{48,72},{56,80},{64,... | collective-permute-start | bytes 393224 | tf_op jit(solution)/shard_map/ppermute | solution.py:372
  15.8 5.2 %collective-permute-start.1 = (bf16[2,256,128]{2,1,0:T(8,128)(2,1)S(1)}, bf16[2,256,128]{2,1,0:T(8,128)(2,1)S(1)}, u32[]{:S(2)}, u32[]{:S(2)}) collective-permute-start(bf16[2,256,128]{2,1,0:T(8,128)(2,1)S(1)} %pad_maximum_fusion.kv0), channel_id=1, source_target_pairs={{0,16},{8,24},{16,32},{24,40},{32,48},{40,56},{48,64},{56,72},{64,... | collective-permute-start | bytes 393224 | tf_op jit(solution)/shard_map/ppermute | solution.py:372
  21.0 3.8 %collective-permute-start.2 = (bf16[2,256,128]{2,1,0:T(8,128)(2,1)S(1)}, bf16[2,256,128]{2,1,0:T(8,128)(2,1)S(1)}, u32[]{:S(2)}, u32[]{:S(2)}) collective-permute-start(bf16[2,256,128]{2,1,0:T(8,128)(2,1)S(1)} %pad_maximum_fusion.kv0), channel_id=1, source_target_pairs={{0,8},{8,16},{16,24},{24,32},{32,40},{40,48},{48,56},{56,64},{64,7... | collective-permute-start | bytes 393224 | tf_op jit(solution)/shard_map/ppermute | solution.py:372
  24.8 0.0 collective-permute-done.kv3
  24.8 2.3 %collective-permute-done.1.kv2 = bf16[2,256,128]{2,1,0:T(8,128)(2,1)S(1)} collective-permute-done((bf16[2,256,128]{2,1,0:T(8,128)(2,1)S(1)}, bf16[2,256,128]{2,1,0:T(8,128)(2,1)S(1)}, u32[]{:S(2)}, u32[]{:S(2)}) %collective-permute-start.1) | collective-permute-done | bytes 131104 | tf_op jit(solution)/shard_map/ppermute | solution.py:372
  27.1 7.1 %collective-permute-done.2.kv1 = bf16[2,256,128]{2,1,0:T(8,128)(2,1)S(1)} collective-permute-done((bf16[2,256,128]{2,1,0:T(8,128)(2,1)S(1)}, bf16[2,256,128]{2,1,0:T(8,128)(2,1)S(1)}, u32[]{:S(2)}, u32[]{:S(2)}) %collective-permute-start.2) | collective-permute-done | bytes 131104 | tf_op jit(solution)/shard_map/ppermute | solution.py:372
  34.2 0.0 copy-start.5
  34.2 1.0 copy-done.5
  35.2 0.0 copy-start.6
  35.3 1.0 copy-done.6
  36.3 0.0 copy-start.7
  36.3 0.7 copy-done.7
  36.9 0.0 copy-start.8
  37.0 12.6 %softmax_backward.1 = (bf16[256,1024]{1,0:T(8,128)(2,1)}, bf16[256,256]{1,0:T(8,128)(2,1)S(1)}, bf16[256,256]{1,0:T(8,128)(2,1)S(1)}, bf16[256,256]{1,0:T(8,128)(2,1)S(1)}, f32[256,256]{1,0:T(8,128)S(1)}) custom-call(s32[1]{0:T(128)S(6)} %mul.13.base_ref, s32[1,32]{1,0:T(1,128)S(1)} %bitcast.10, bf16[256,1024]{1,0:T(8,128)(2,1)S(1)} %copy-done.5, ...), custom_call_target="tpu_custom_call" | custom-call | flops 10737418240 | bytes 4194304 | tf_op jit(solution)/shard_map/softmax_backward/pallas_call | solution.py:111
  49.6 1.9 collective-permute-start.5
  51.5 1.3 collective-permute-start.4
  52.8 1.3 collective-permute-start.3
  54.1 0.0 copy-done.8
  54.1 1.5 copy.22
  55.6 4.5 %all-to-all-start = ((bf16[2,8,512,128]{3,2,0,1:T(8,128)(2,1)}), bf16[2,8,512,128]{3,2,0,1:T(8,128)(2,1)}, u32[]{:S(2)}, u32[]{:S(2)}) async-start(bf16[2,8,512,128]{3,2,0,1:T(8,128)(2,1)} %copy.22), calls=%async_computation | async-start | bytes 4194304 | tf_op jit(solution)/shard_map/all_to_all | solution.py:387
  60.1 0.0 all-gather.4.cloned.1.call-start
  60.1 1.2 collective-permute-done.5
  61.3 1.1 collective-permute-done.4
  62.4 7.8 %collective-permute-done.3 = bf16[256,256]{1,0:T(8,128)(2,1)S(1)} collective-permute-done((bf16[256,256]{1,0:T(8,128)(2,1)S(1)}, bf16[256,256]{1,0:T(8,128)(2,1)S(1)}, u32[]{:S(2)}, u32[]{:S(2)}) %collective-permute-start.3) | collective-permute-done | bytes 131104 | tf_op jit(solution)/shard_map/ppermute | solution.py:372
  70.2 0.7 add_convert_fusion
  70.9 0.0 all-gather.4.cloned.1.call-update
  71.0 1.1 dynamic-slice_reduce_fusion
  72.2 0.1 reduce_sum.45
  72.3 0.1 iota_compare_fusion.2
  72.4 0.1 select_reduce_fusion.1
  72.5 0.2 select_reduce_fusion.2
  72.7 3.9 %lightning_forward.1.out_ref = f32[256,512]{1,0:T(8,128)} custom-call(s32[1]{0:T(128)} %bitcast.block_ref, bf16[256,512]{1,0:T(8,128)(2,1)} %q_ref.7, bf16[256,512]{1,0:T(8,128)(2,1)} %k_ref.5, bf16[256,512]{1,0:T(8,128)(2,1)} %v_ref.5, f32[4,16384]{1,0:T(4,128)} %log_ref.7, bf16[1,4,128,128]{3,2,1,0:T(8,128)(2,1)} %state_ref.3), custom_call_target="tpu_custom_call" | custom-call | flops 1342177280 | bytes 2097152 | tf_op jit(solution)/shard_map/lightning_forward/pallas_call | solution.py:162
  76.5 0.0 copy-start.4
  76.5 10.8 %all-to-all-done = bf16[2,8,512,128]{3,2,0,1:T(8,128)(2,1)} async-done(((bf16[2,8,512,128]{3,2,0,1:T(8,128)(2,1)}), bf16[2,8,512,128]{3,2,0,1:T(8,128)(2,1)}, u32[]{:S(2)}, u32[]{:S(2)}) %all-to-all-start) | async-done | bytes 2097184 | tf_op jit(solution)/shard_map/all_to_all | solution.py:387
  87.4 1.7 copy.23.proj_ref
  89.1 15.1 %all-gather.4.cloned.1.call-done = bf16[2048,256]{1,0:T(8,128)(2,1)} async-done(((bf16[256,256]{1,0:T(8,128)(2,1)}), bf16[2048,256]{1,0:T(8,128)(2,1)}) %all-gather.4.cloned.1.call-update) | async-done | bytes 1048592 | tf_op jit(solution)/shard_map/all_gather | solution.py:400
  104.2 0.0 copy-done
  104.2 0.0 copy-done.3
  104.2 0.0 copy-done.4
  104.2 1.2 copy-done.1
  105.4 1.4 cotangent.1
  106.8 0.0 copy-start.2
  106.8 0.8 copy-done.2
  107.6 14.2 %psum.7.stats_ref = f32[8,256]{1,0:T(8,128)} all-reduce(f32[8,256]{1,0:T(8,128)S(1)} %get-tuple-element.24), channel_id=1, replica_groups=mesh['ctx'=64,'head'=8] {'head'}, use_global_device_ids=true, to_apply=%region_0.1 | all-reduce | flops 2048 | bytes 16384 | tf_op jit(solution)/shard_map/psum | solution.py:402
  121.8 3.9 %dout_summary.1 = (bf16[256,512]{1,0:T(8,128)(2,1)}, bf16[4,128,128]{2,1,0:T(8,128)(2,1)}) custom-call(s32[1]{0:T(128)} %bitcast.block_ref, f32[8,256]{1,0:T(8,128)} %psum.7.stats_ref, f32[256,512]{1,0:T(8,128)} %copy-done.2, f32[256,512]{1,0:T(8,128)} %lightning_forward.1.out_ref, bf16[256,512]{1,0:T(8,128)(2,1)} %q_ref.7, f32[4,16384]{1,0:T(4,128)} %log_ref.7), custom_call_target="tpu_custom_call" | custom-call | tf_op jit(solution)/shard_map/dout_summary/pallas_call | solution.py:221
  125.7 5.3 %all-to-all-start.1 = ((bf16[4,128,128]{2,1,0:T(8,128)(2,1)}), bf16[4,128,128]{2,1,0:T(8,128)(2,1)S(1)}, u32[]{:S(2)}, u32[]{:S(2)}) async-start(bf16[4,128,128]{2,1,0:T(8,128)(2,1)} %get-tuple-element.30), calls=%async_computation.1 | async-start | bytes 262144 | tf_op jit(solution)/shard_map/all_to_all | solution.py:356
  131.0 0.6 exp.12.inner_ref
  131.5 0.6 exp.14.leave_ref
  132.1 0.6 exp.15.weight_ref
  132.7 0.2 select_reduce_fusion
  132.9 0.5 compare_select_fusion.carry_ref
  133.4 2.7 %all-to-all-done.1.blocks_ref = bf16[4,128,128]{2,1,0:T(8,128)(2,1)S(1)} async-done(((bf16[4,128,128]{2,1,0:T(8,128)(2,1)}), bf16[4,128,128]{2,1,0:T(8,128)(2,1)S(1)}, u32[]{:S(2)}, u32[]{:S(2)}) %all-to-all-start.1) | async-done | bytes 131104 | tf_op jit(solution)/shard_map/all_to_all | solution.py:356
  136.1 0.7 copy-done.10
  136.8 1.6 group_total.1
  138.3 60.7 %all-gather.1 = bf16[2048,128]{1,0:T(8,128)(2,1)} all-gather(bf16[128,128]{1,0:T(8,128)(2,1)} %group_total.1), channel_id=3, replica_groups={{0,32,64,96,128,160,192,224,256,288,320,352,384,416,448,480},{8,40,72,1..., dimensions={0}, use_global_device_ids=true | all-gather | bytes 557056 | tf_op jit(solution)/shard_map/all_gather | solution.py:361
  199.0 1.9 after_states.1
  201.0 3.3 %all-to-all-start.2 = ((bf16[4,128,128]{2,1,0:T(8,128)(2,1)}), bf16[4,128,128]{2,1,0:T(8,128)(2,1)S(1)}, u32[]{:S(2)}, u32[]{:S(2)}) async-start(bf16[4,128,128]{2,1,0:T(8,128)(2,1)} %after_states.1), calls=%async_computation.2 | async-start | bytes 262144 | tf_op jit(solution)/shard_map/all_to_all | solution.py:366
  204.3 0.0 copy-done.9
  204.3 0.7 fusion.1
  205.0 4.1 %near_far.1 = (bf16[256,512]{1,0:T(8,128)(2,1)}, f32[256,512]{1,0:T(8,128)}, f32[256,512]{1,0:T(8,128)}) custom-call(s32[1]{0:T(128)} %bitcast.block_ref, bf16[256,512]{1,0:T(8,128)(2,1)} %q_ref.7, bf16[256,512]{1,0:T(8,128)(2,1)} %k_ref.5, bf16[256,512]{1,0:T(8,128)(2,1)} %v_ref.5, bf16[256,512]{1,0:T(8,128)(2,1)} %get-tuple-element.26.dout_ref, ...), custom_call_target="tpu_custom_call" | custom-call | flops 3489660928 | bytes 4194304 | tf_op jit(solution)/shard_map/near_far/pallas_call | solution.py:259
  209.1 0.3 all-to-all-done.2.after_ref
  209.4 0.6 copy-done.11
  210.1 3.8 %last.1 = (bf16[256,512]{1,0:T(8,128)(2,1)}, bf16[256,512]{1,0:T(8,128)(2,1)}) custom-call(s32[1]{0:T(128)} %bitcast.block_ref, bf16[256,512]{1,0:T(8,128)(2,1)} %k_ref.5, bf16[256,512]{1,0:T(8,128)(2,1)} %v_ref.5, f32[256,512]{1,0:T(8,128)} %get-tuple-element.28.dk_ref, f32[256,512]{1,0:T(8,128)} %get-tuple-element.29.dv_ref, ...), custom_call_target="tpu_custom_call" | custom-call | tf_op jit(solution)/shard_map/last/pallas_call | solution.py:292
  (11 shorter events, 0.1 us)
Async XLA Ops:
  8.1 16.8 %collective-permute-start = (bf16[2,256,128]{2,1,0:T(8,128)(2,1)S(1)}, bf16[2,256,128]{2,1,0:T(8,128)(2,1)S(1)}, u32[]{:S(2)}, u32[]{:S(2)}) collective-permute-start(bf16[2,256,128]{2,1,0:T(8,128)(2,1)S(1)} %pad_maximum_fusion.kv0), channel_id=1, source_target_pairs={{0,24},{8,32},{16,40},{24,48},{32,56},{40,64},{48,72},{56,80},{64,... | collective-permute-start | bytes 393224 | tf_op jit(solution)/shard_map/ppermute | solution.py:372
  15.8 11.3 %collective-permute-start.1 = (bf16[2,256,128]{2,1,0:T(8,128)(2,1)S(1)}, bf16[2,256,128]{2,1,0:T(8,128)(2,1)S(1)}, u32[]{:S(2)}, u32[]{:S(2)}) collective-permute-start(bf16[2,256,128]{2,1,0:T(8,128)(2,1)S(1)} %pad_maximum_fusion.kv0), channel_id=1, source_target_pairs={{0,16},{8,24},{16,32},{24,40},{32,48},{40,56},{48,64},{56,72},{64,... | collective-permute-start | bytes 393224 | tf_op jit(solution)/shard_map/ppermute | solution.py:372
  21.0 13.2 %collective-permute-start.2 = (bf16[2,256,128]{2,1,0:T(8,128)(2,1)S(1)}, bf16[2,256,128]{2,1,0:T(8,128)(2,1)S(1)}, u32[]{:S(2)}, u32[]{:S(2)}) collective-permute-start(bf16[2,256,128]{2,1,0:T(8,128)(2,1)S(1)} %pad_maximum_fusion.kv0), channel_id=1, source_target_pairs={{0,8},{8,16},{16,24},{24,32},{32,40},{40,48},{48,56},{56,64},{64,7... | collective-permute-start | bytes 393224 | tf_op jit(solution)/shard_map/ppermute | solution.py:372
  34.2 1.0 copy-start.5
  35.2 1.0 copy-start.6
  36.3 0.7 copy-start.7
  36.9 17.1 %copy-start.8 = (bf16[2,4096,128]{2,1,0:T(8,128)(2,1)S(1)}, bf16[2,4096,128]{2,1,0:T(8,128)(2,1)}, u32[]{:S(2)}) copy-start(bf16[2,4096,128]{2,1,0:T(8,128)(2,1)} %param.24) | copy-start | bytes 6291460
  49.6 11.7 %collective-permute-start.5 = (bf16[256,256]{1,0:T(8,128)(2,1)S(1)}, bf16[256,256]{1,0:T(8,128)(2,1)S(1)}, u32[]{:S(2)}, u32[]{:S(2)}) collective-permute-start(bf16[256,256]{1,0:T(8,128)(2,1)S(1)} %get-tuple-element.23), channel_id=1, source_target_pairs={{8,0},{16,8},{24,16},{32,24},{40,32},{48,40},{56,48},{64,56},{72,6... | collective-permute-start | bytes 393224 | tf_op jit(solution)/shard_map/ppermute | solution.py:372
  51.5 10.9 %collective-permute-start.4 = (bf16[256,256]{1,0:T(8,128)(2,1)S(1)}, bf16[256,256]{1,0:T(8,128)(2,1)S(1)}, u32[]{:S(2)}, u32[]{:S(2)}) collective-permute-start(bf16[256,256]{1,0:T(8,128)(2,1)S(1)} %get-tuple-element.22), channel_id=1, source_target_pairs={{16,0},{24,8},{32,16},{40,24},{48,32},{56,40},{64,48},{72,56},{80,... | collective-permute-start | bytes 393224 | tf_op jit(solution)/shard_map/ppermute | solution.py:372
  52.8 17.4 %collective-permute-start.3 = (bf16[256,256]{1,0:T(8,128)(2,1)S(1)}, bf16[256,256]{1,0:T(8,128)(2,1)S(1)}, u32[]{:S(2)}, u32[]{:S(2)}) collective-permute-start(bf16[256,256]{1,0:T(8,128)(2,1)S(1)} %get-tuple-element.21), channel_id=1, source_target_pairs={{24,0},{32,8},{40,16},{48,24},{56,32},{64,40},{72,48},{80,56},{88,... | collective-permute-start | bytes 393224 | tf_op jit(solution)/shard_map/ppermute | solution.py:372
  55.6 31.8 %all-to-all-start = ((bf16[2,8,512,128]{3,2,0,1:T(8,128)(2,1)}), bf16[2,8,512,128]{3,2,0,1:T(8,128)(2,1)}, u32[]{:S(2)}, u32[]{:S(2)}) async-start(bf16[2,8,512,128]{3,2,0,1:T(8,128)(2,1)} %copy.22), calls=%async_computation | async-start | bytes 4194304 | tf_op jit(solution)/shard_map/all_to_all | solution.py:387
  60.1 44.2 %all-gather.4.cloned.1.call-start = ((), (), s32[]{:S(2)}) async-start(), calls=%async_computation.3 | async-start | bytes 1179648 | tf_op jit(solution)/shard_map/all_gather | solution.py:400
  76.5 27.7 %copy-start = (f32[256,512]{1,0:T(8,128)S(1)}, f32[256,512]{1,0:T(8,128)}, u32[]{:S(2)}) copy-start(f32[256,512]{1,0:T(8,128)} %lightning_forward.1.out_ref) | copy-start | bytes 1572868
  76.5 27.7 %copy-start.3 = (bf16[256,512]{1,0:T(8,128)(2,1)S(1)}, bf16[256,512]{1,0:T(8,128)(2,1)}, u32[]{:S(2)}) copy-start(bf16[256,512]{1,0:T(8,128)(2,1)} %grad_ref.1) | copy-start | bytes 786436
  76.5 27.7 %copy-start.4 = (f32[512]{0:T(512)S(1)}, f32[512]{0:T(512)}, u32[]{:S(2)}) copy-start(f32[512]{0:T(512)} %param.17) | copy-start | bytes 6148
  104.2 1.2 copy-start.1
  106.8 0.8 copy-start.2
  107.6 96.7 %copy-start.9 = (bf16[256,256]{1,0:T(8,128)(2,1)S(1)}, bf16[256,256]{1,0:T(8,128)(2,1)}, u32[]{:S(2)}) copy-start(bf16[256,256]{1,0:T(8,128)(2,1)} %add_convert_fusion) | copy-start | bytes 393220
  125.7 10.4 %all-to-all-start.1 = ((bf16[4,128,128]{2,1,0:T(8,128)(2,1)}), bf16[4,128,128]{2,1,0:T(8,128)(2,1)S(1)}, u32[]{:S(2)}, u32[]{:S(2)}) async-start(bf16[4,128,128]{2,1,0:T(8,128)(2,1)} %get-tuple-element.30), calls=%async_computation.1 | async-start | bytes 262144 | tf_op jit(solution)/shard_map/all_to_all | solution.py:356
  136.1 0.7 copy-start.10
  201.0 8.5 %all-to-all-start.2 = ((bf16[4,128,128]{2,1,0:T(8,128)(2,1)}), bf16[4,128,128]{2,1,0:T(8,128)(2,1)S(1)}, u32[]{:S(2)}, u32[]{:S(2)}) async-start(bf16[4,128,128]{2,1,0:T(8,128)(2,1)} %after_states.1), calls=%async_computation.2 | async-start | bytes 262144 | tf_op jit(solution)/shard_map/all_to_all | solution.py:366
  209.4 0.6 copy-start.11
Sparse Core Ops, SparseCore 0:
  71.1 33.0 all-gather.3

commit v2 on v1

v2 whole, which is shorter than its diff:
```python
import functools
import math

import jax
import jax.numpy as jnp
from jax import lax
from jax.experimental import pallas as pl
from jax.experimental.pallas import tpu as pltpu
from jax.sharding import PartitionSpec as P

DH = 128
Q_HEADS = 64
KV_HEADS = 8
GROUP = Q_HEADS // KV_HEADS
LIGHTNING_HEADS = 32
FEATURES = LIGHTNING_HEADS * DH
SUB = 4
QUAD = 4
AT_ONCE = 2
TILES = 2
epsilon = 1e-06

F32 = jnp.float32
BF16 = jnp.bfloat16
NT = (((1,), (1,)), ((), ()))
NN = (((1,), (0,)), ((), ()))
TN = (((0,), (0,)), ((), ()))
VMEM_LIMIT = 48 * 1024 * 1024


def mm(a, b, dims=NN):
    return lax.dot_general(a, b, dims, preferred_element_type=F32)


def iota2(shape, dim):
    return lax.broadcasted_iota(jnp.int32, shape, dim)


def to_column(row):
    n = row.shape[1]
    return jnp.sum(jnp.where(iota2((n, n), 0) == iota2((n, n), 1), row, 0.0), axis=1, keepdims=True)


def to_row(column):
    n = column.shape[0]
    return jnp.sum(jnp.where(iota2((n, n), 0) == iota2((n, n), 1), column, 0.0), axis=0, keepdims=True)


def decay_sums(log_row):
    n = log_row.shape[1]
    first, second = iota2((n, n), 0), iota2((n, n), 1)
    g_col = jnp.sum(jnp.where(second <= first, log_row, 0.0), axis=1, keepdims=True)
    return g_col, to_row(g_col)


def softmax_kernel(
    length, base_ref, lens_ref, q_ref, do_ref, kv3, kv2, kv1, kv0,
    dq_ref, part3, part2, part1, own, k_win, v_win, k_t, bias, acc_k, acc_v,
):
    tile, pair = pl.program_id(0), pl.program_id(1)
    first = jnp.logical_and(tile == 0, pair == 0)
    final = jnp.logical_and(tile == pl.num_programs(0) - 1, pair == pl.num_programs(1) - 1)
    rows = q_ref.shape[0]
    reach = bias.shape[0]
    scale = DH ** -0.5

    @pl.when(first)
    def _():
        for slot, kv in enumerate((kv3, kv2, kv1, kv0)):
            here = slice(slot * length, (slot + 1) * length)
            k_win[here, :] = kv[0]
            v_win[here, :] = kv[1]
            k_t[:, here] = kv[0].astype(F32).T.astype(BF16)
        acc_k[...] = jnp.zeros_like(acc_k)
        acc_v[...] = jnp.zeros_like(acc_v)

    @pl.when(pair == 0)
    def _():
        docs = lens_ref.shape[1]
        lens = jnp.where(iota2((docs, docs), 1) <= iota2((docs, docs), 0), lens_ref[...], 0)
        ends = jnp.sum(lens, axis=1, keepdims=True)
        base = base_ref[0] + tile * rows
        t_row = base + iota2((docs, rows), 1)
        start = jnp.max(jnp.where(ends <= t_row, ends, 0), axis=0, keepdims=True)
        s_pos = base - (SUB - 1) * length + iota2((reach, rows), 0)
        t_pos = base + iota2((reach, rows), 1)
        hidden = jnp.where((s_pos <= t_pos) & (s_pos >= start), 0.0, -1e30)
        for head in range(AT_ONCE):
            bias[:, head * rows:(head + 1) * rows] = hidden

    def stacked(ref):
        return jnp.concatenate([ref[:, h * DH:(h + 1) * DH] for h in range(AT_ONCE)], axis=0)

    window = pl.ds(pl.multiple_of(tile * rows, rows), reach)
    q = stacked(q_ref)
    do = stacked(do_ref)
    scores = mm(k_win[window, :], q, NT) * (scale * math.log2(math.e)) + bias[...]
    highest = jnp.max(scores, axis=0, keepdims=True)
    raised = jnp.exp2(scores - highest)
    inverse = 1.0 / jnp.sum(raised, axis=0, keepdims=True)
    grad_probs = mm(v_win[window, :], do, NT)
    delta = jnp.sum(raised * grad_probs, axis=0, keepdims=True) * inverse
    prob = raised * inverse
    dscore = (prob * (grad_probs - delta)).astype(BF16)
    acc_v[window, :] += mm(prob.astype(BF16), do)
    acc_k[window, :] += mm(dscore, q)
    dq = (mm(k_t[:, window], dscore) * scale).T
    for head in range(AT_ONCE):
        dq_ref[:, head * DH:(head + 1) * DH] = dq[head * rows:(head + 1) * rows, :].astype(BF16)

    @pl.when(final)
    def _():
        for slot, out in enumerate((part3, part2, part1, own)):
            here = slice(slot * length, (slot + 1) * length)
            out[:, :DH] = (acc_k[here, :] * scale).astype(out.dtype)
            out[:, DH:] = acc_v[here, :].astype(out.dtype)


def softmax_call(base, lens, q, do, windows):
    length = q.shape[0]
    rows = length // TILES
    whole = lambda *shape: pl.BlockSpec(shape, lambda i, j: (0,) * len(shape))
    per_pair = pl.BlockSpec((rows, AT_ONCE * DH), lambda i, j: (i, j))
    window = SUB * length
    reach = window - length + rows
    pair = jax.ShapeDtypeStruct((length, 2 * DH), BF16)
    return pl.pallas_call(
        functools.partial(softmax_kernel, length),
        out_shape=(
            jax.ShapeDtypeStruct(q.shape, BF16), pair, pair, pair,
            jax.ShapeDtypeStruct((length, 2 * DH), F32),
        ),
        grid=(TILES, GROUP // AT_ONCE),
        in_specs=[
            pl.BlockSpec(memory_space=pltpu.SMEM), whole(1, lens.shape[1]), per_pair, per_pair,
        ] + [whole(2, length, DH)] * SUB,
        out_specs=(per_pair,) + (whole(length, 2 * DH),) * SUB,
        scratch_shapes=[
            pltpu.VMEM((window, DH), BF16), pltpu.VMEM((window, DH), BF16),
            pltpu.VMEM((DH, window), BF16), pltpu.VMEM((reach, AT_ONCE * rows), F32),
            pltpu.VMEM((window, DH), F32), pltpu.VMEM((window, DH), F32),
        ],
        compiler_params=pltpu.CompilerParams(vmem_limit_bytes=VMEM_LIMIT),
        cost_estimate=pl.CostEstimate(
            flops=200 * GROUP * window * length * DH * 4, bytes_accessed=4 * 1024 * 1024,
            transcendentals=GROUP * window * length,
        ),
        name="softmax_backward",
    )(base, lens, q, do, *windows)


def forward_kernel(
    block_ref, q_ref, k_ref, v_ref, log_ref, state_ref, out_ref, scaled_ref, tail_ref
):
    head = pl.program_id(0)
    length = q_ref.shape[0]
    g_col, g_row = decay_sums(log_ref[pl.ds(head, 1), :])
    causal = iota2((length, length), 0) >= iota2((length, length), 1)
    weights = jnp.where(causal, jnp.exp(jnp.minimum(g_col - g_row, 0.0)), 0.0)
    near = (mm(q_ref[...], k_ref[...], NT) * weights).astype(BF16)
    scaled = (q_ref[...].astype(F32) * jnp.exp(g_col)).astype(BF16)
    out = (mm(near, v_ref[...]) + mm(scaled, state_ref[0, 0])) * (1.0 / DH)
    out_ref[...] = out
    scaled_ref[...] = scaled
    tail_ref[...] = jnp.broadcast_to(jnp.exp(g_col[length - 1:, :] - g_col), out.shape)


def per_head_spec(length):
    return pl.BlockSpec((length, DH), lambda h, b: (0, h))


def state_spec():
    return pl.BlockSpec((1, 1, DH, DH), lambda h, b: (0, h, 0, 0))


def log_spec(heads, length):
    return pl.BlockSpec((heads, length), lambda h, b: (0, b[0]))


def forward_call(block, q, k, v, log_decay, state):
    length, heads = q.shape[0], q.shape[1] // DH
    wide = per_head_spec(length)
    like = lambda dtype: jax.ShapeDtypeStruct(q.shape, dtype)
    return pl.pallas_call(
        forward_kernel,
        out_shape=(like(F32), like(BF16), like(F32)),
        grid_spec=pltpu.PrefetchScalarGridSpec(
            num_scalar_prefetch=1, grid=(heads,),
            in_specs=[wide, wide, wide, log_spec(heads, length), state_spec()],
            out_specs=(wide, wide, wide),
        ),
        cost_estimate=pl.CostEstimate(
            flops=heads * length * DH * (4 * length + 2 * DH) * 8, bytes_accessed=4 * 1024 * 1024,
            transcendentals=heads * length * length,
        ),
        name="lightning_forward",
    )(block, q, k, v, log_decay, state)


def cotangent_kernel(
    core_ref, own_ref, other_ref, proj_ref, grad_ref, gain_ref, out_ref, gated_ref, stats_ref
):
    core = core_ref[0]
    total = grad_ref[...].astype(F32)
    for chip in range(own_ref.shape[0]):
        for dkv_ref, g in ((own_ref, 2 * chip + core), (other_ref, 2 * chip + 1 - core)):
            for side in range(2):
                total += mm(dkv_ref[chip, :, side * DH:(side + 1) * DH], proj_ref[g, side], NT)
    gated = gain_ref[...] * total
    gated_ref[...] = gated
    out = out_ref[...]
    squares = to_row(jnp.sum(out * out, axis=1, keepdims=True))
    cross = to_row(jnp.sum(gated * out, axis=1, keepdims=True))
    rows = iota2(stats_ref.shape[1:], 0)
    stats = jnp.where(rows == 0, squares, jnp.where(rows == 1, cross, 0.0))
    for copy in range(stats_ref.shape[0]):
        stats_ref[copy] = stats


def cotangent_call(core, own, other, proj, grad, gain, out):
    vmem = pl.BlockSpec(memory_space=pltpu.VMEM)
    return pl.pallas_call(
        cotangent_kernel,
        in_specs=[pl.BlockSpec(memory_space=pltpu.SMEM)] + [vmem] * 6,
        out_shape=(
            jax.ShapeDtypeStruct(grad.shape, F32),
            jax.ShapeDtypeStruct((KV_HEADS, 8, grad.shape[0]), F32),
        ),
        compiler_params=pltpu.CompilerParams(vmem_limit_bytes=VMEM_LIMIT),
        name="cotangent",
    )(core, own, other, proj, grad, gain, out)


def dout_kernel(stats_ref, gated_ref, out_ref, scaled_ref, dout_ref, summary_ref):
    stats = stats_ref[0]
    for source in range(1, stats_ref.shape[0]):
        stats += stats_ref[source]
    inverse = 1.0 / jnp.sqrt(stats[0:1, :] * (1.0 / FEATURES) + epsilon)
    factor = stats[1:2, :] * (inverse * inverse * inverse) * (1.0 / FEATURES)
    low = (gated_ref[...] * to_column(inverse) - out_ref[...] * to_column(factor)).astype(BF16)
    dout_ref[...] = low
    for head in range(summary_ref.shape[0]):
        columns = slice(head * DH, (head + 1) * DH)
        summary_ref[head] = mm(scaled_ref[:, columns], low[:, columns], TN).astype(BF16)


def dout_call(stats, gated, out, scaled):
    return pl.pallas_call(
        dout_kernel,
        out_shape=(
            jax.ShapeDtypeStruct(out.shape, BF16),
            jax.ShapeDtypeStruct((out.shape[1] // DH, DH, DH), BF16),
        ),
        name="dout_summary",
    )(stats, gated, out, scaled)


def near_far_kernel(
    block_ref, q_ref, k_ref, v_ref, dout_ref, log_ref, state_ref, dq_ref, dk_ref, dv_ref
):
    head = pl.program_id(0)
    length = q_ref.shape[0]
    g_col, g_row = decay_sums(log_ref[pl.ds(head, 1), :])
    first, second = iota2((length, length), 0), iota2((length, length), 1)
    gap = g_col - g_row
    weights = jnp.where(first >= second, jnp.exp(jnp.minimum(gap, 0.0)), 0.0)
    turned = jnp.where(second >= first, jnp.exp(jnp.minimum(-gap, 0.0)), 0.0)
    q, k, v, dout = q_ref[...], k_ref[...], v_ref[...], dout_ref[...]
    far = (mm(dout, v, NT) * weights).astype(BF16)
    far_turned = (mm(v, dout, NT) * turned).astype(BF16)
    near_turned = (mm(k, q, NT) * turned).astype(BF16)
    dq = mm(far, k) + jnp.exp(g_col) * mm(dout, state_ref[0, 0], NT)
    dq_ref[...] = (dq * (1.0 / DH)).astype(BF16)
    dk_ref[...] = mm(far_turned, q)
    dv_ref[...] = mm(near_turned, dout)


def near_far_call(block, q, k, v, dout, log_decay, state):
    length, heads = q.shape[0], q.shape[1] // DH
    wide = per_head_spec(length)
    return pl.pallas_call(
        near_far_kernel,
        out_shape=(
            jax.ShapeDtypeStruct(q.shape, BF16), jax.ShapeDtypeStruct(q.shape, F32),
            jax.ShapeDtypeStruct(q.shape, F32),
        ),
        grid_spec=pltpu.PrefetchScalarGridSpec(
            num_scalar_prefetch=1, grid=(heads,),
            in_specs=[wide, wide, wide, wide, log_spec(heads, length), state_spec()],
            out_specs=(wide, wide, wide),
        ),
        cost_estimate=pl.CostEstimate(
            flops=heads * length * DH * (12 * length + 2 * DH) * 8, bytes_accessed=4 * 1024 * 1024,
            transcendentals=2 * heads * length * length,
        ),
        name="near_far",
    )(block, q, k, v, dout, log_decay, state)


def last_kernel(k_ref, v_ref, dk_ref, dv_ref, tail_ref, after_ref, dk_out, dv_out):
    for head in range(after_ref.shape[0]):
        at = slice(head * DH, (head + 1) * DH)
        tail = tail_ref[:, at]
        after = after_ref[head]
        dk = dk_ref[:, at] + tail * mm(v_ref[:, at], after, NT)
        dv = dv_ref[:, at] + tail * mm(k_ref[:, at], after)
        dk_out[:, at] = (dk * (1.0 / DH)).astype(BF16)
        dv_out[:, at] = (dv * (1.0 / DH)).astype(BF16)


def last_call(k, v, dk, dv, tail, after):
    return pl.pallas_call(
        last_kernel,
        out_shape=(jax.ShapeDtypeStruct(k.shape, BF16), jax.ShapeDtypeStruct(k.shape, BF16)),
        name="last",
    )(k, v, dk, dv, tail, after)


ENTER, RISE, GROUPS, ROWS, LEAVE, INNER = 0, 4, 8, 12, 16, 20


def state_weights(log_decay, length, device):
    place, group, row = device % QUAD, device // QUAD, device // (QUAD * QUAD)
    decays = lax.dynamic_slice_in_dim(log_decay, place, 1, 0)
    gamma = jnp.sum(decays.reshape(-1, length), axis=1)
    block = jnp.arange(gamma.shape[0], dtype=jnp.int32)
    quad = jnp.arange(QUAD, dtype=jnp.int32)
    first, row_first = group * QUAD, row * QUAD * QUAD
    same = lambda x: jnp.broadcast_to(x, (QUAD,))
    group_first, rows_first = row_first + quad * QUAD, quad * QUAD * QUAD
    low = jnp.concatenate(
        [same(first - 1), same(row_first - 1), same(first + QUAD - 1), same(first + QUAD - 1), first + quad,
         jnp.repeat(first + quad, QUAD)]
    )
    high = jnp.concatenate(
        [first + quad, group_first, group_first, rows_first, same(first + QUAD), jnp.tile(first + quad, QUAD)]
    )
    yes = jnp.ones((QUAD,), bool)
    used = jnp.concatenate([yes, yes, group_first > first, quad > row, yes, jnp.ones((QUAD * QUAD,), bool)])
    inside = (block[None, :] > low[:, None]) & (block[None, :] < high[:, None])
    factors = jnp.exp(jnp.sum(jnp.where(inside, gamma[None, :], 0.0), axis=1))
    return jnp.where(used, factors, 0.0)


def rise_kernel(first, weight_ref, blocks_ref, total_ref):
    total = jnp.zeros(blocks_ref.shape[1:], F32)
    for z in range(QUAD):
        total += weight_ref[first + z] * blocks_ref[z].astype(F32)
    total = total.astype(BF16)
    for z in range(QUAD):
        total_ref[z] = total


def after_kernel(weight_ref, blocks_ref, groups_ref, rows_ref, after_ref):
    carry = jnp.zeros(blocks_ref.shape[1:], F32)
    for g in range(QUAD):
        carry += weight_ref[GROUPS + g] * groups_ref[g].astype(F32)
        carry += weight_ref[ROWS + g] * rows_ref[g].astype(F32)
    for z in range(QUAD):
        after = weight_ref[LEAVE + z] * carry
        for later in range(z + 1, QUAD):
            after += weight_ref[INNER + z * QUAD + later] * blocks_ref[later].astype(F32)
        after_ref[z] = after.astype(BF16)


def after_states(summary, weights, beside):
    count = lax.axis_size("ctx")
    square = QUAD * QUAD
    every = [[g * QUAD + i for i in range(QUAD)] for g in range(count // QUAD)]
    over_groups = [
        [r * square + i * QUAD + z for i in range(QUAD)] for r in range(count // square) for z in range(QUAD)
    ]
    over_rows = [[i * square + p for i in range(QUAD)] for p in range(square)]
    smem = pl.BlockSpec(memory_space=pltpu.SMEM)
    vmem = pl.BlockSpec(memory_space=pltpu.VMEM)
    shape = jax.ShapeDtypeStruct((QUAD, DH, DH), BF16)
    swap = lambda x, groups: lax.all_to_all(x, "ctx", 0, 0, tiled=True, axis_index_groups=groups)

    def rise(first, blocks):
        return pl.pallas_call(
            functools.partial(rise_kernel, first), out_shape=shape,
            in_specs=[smem, vmem], out_specs=vmem, name="rise",
        )(weights, blocks)

    blocks = swap(summary, every)
    groups = swap(rise(ENTER, blocks), over_groups)
    risen, beside = lax.optimization_barrier((rise(RISE, groups), beside))
    rows = swap(risen, over_rows)
    after = pl.pallas_call(
        after_kernel, out_shape=shape, in_specs=[smem, vmem, vmem, vmem], out_specs=vmem, name="after_states",
    )(weights, blocks, groups, rows)
    return swap(after, every), beside


def passed_along(block, distance):
    devices = range(lax.axis_size("ctx"))
    route = [(i - distance, i) for i in devices if i - distance in devices]
    return lax.ppermute(block, "ctx", route)


def per_device(
    lin_query, lin_keys, lin_values, lin_grad, norm_gain, log_decay, state_in,
    soft_query, soft_keys, soft_values, soft_grad, projections, doc_lengths,
):
    length = lin_query.shape[0]
    width = lin_query.shape[1]
    device = lax.axis_index("ctx").astype(jnp.int32)
    block = device.reshape(1)

    heads = lax.axis_size("head")
    stacked = jnp.stack([soft_keys, soft_values])
    stacked, early = lax.optimization_barrier((stacked, projections))
    kv3, kv2, kv1 = (passed_along(stacked, offset) for offset in (3, 2, 1))
    proj = early.reshape(2, KV_HEADS, width, DH).transpose(1, 0, 2, 3)
    proj = lax.all_to_all(proj, "head", 0, 0, tiled=True)
    soft_query = pltpu.with_memory_space_constraint(soft_query, pltpu.HBM)
    soft_grad = pltpu.with_memory_space_constraint(soft_grad, pltpu.HBM)
    soft_dq, part3, part2, part1, own = softmax_call(
        block * length, doc_lengths.reshape(1, -1), soft_query, soft_grad, [kv3, kv2, kv1, stacked]
    )
    lin_query, own = lax.optimization_barrier((lin_query, own))
    lin_out, scaled, tail = forward_call(
        block, lin_query, lin_keys, lin_values, log_decay, state_in
    )
    summed = own
    for offset, part in ((3, part3), (2, part2), (1, part1)):
        summed = summed + passed_along(part, -offset).astype(F32)
    dkv, lin_out, proj = lax.optimization_barrier((summed.astype(BF16), lin_out, proj))
    soft_dk, soft_dv = dkv[:, :DH], dkv[:, DH:]

    same_core = [[2 * chip + core for chip in range(heads // 2)] for core in range(2)]
    copies = jnp.broadcast_to(dkv[None], (heads // 2,) + dkv.shape)
    own_dkv = lax.all_to_all(copies, "head", 0, 0, tiled=True, axis_index_groups=same_core)
    other_dkv = lax.ppermute(own_dkv, "head", [(i, i ^ 1) for i in range(heads)])
    core = (lax.axis_index("head").astype(jnp.int32) % 2).reshape(1)
    gated, stats = cotangent_call(
        core, own_dkv, other_dkv, proj, lin_grad, norm_gain.reshape(1, width), lin_out
    )
    stats = lax.all_to_all(stats, "head", 0, 0, tiled=True)
    dout, summary = dout_call(stats, gated, lin_out, scaled)
    weights = state_weights(log_decay, length, device)
    beside = near_far_call(block, lin_query, lin_keys, lin_values, dout, log_decay, state_in)
    after, (lin_dq, dk, dv) = after_states(summary, weights, beside)
    lin_dk, lin_dv = last_call(lin_keys, lin_values, dk, dv, tail, after)
    return (lin_dq, lin_dk, lin_dv, soft_dq, soft_dk, soft_dv)


def solution(mesh):
    in_specs = (
        P("ctx", "head"), P("ctx", "head"), P("ctx", "head"), P("ctx", "head"),
        P("head"), P("head", None), P("ctx", "head", None, None),
        P("ctx", "head"), P("ctx", "head"), P("ctx", "head"), P("ctx", "head"),
        P(None, None, "head"), P(),
    )
    out_specs = (P("ctx", "head"),) * 6
    return jax.shard_map(
        per_device, mesh=mesh, in_specs=in_specs, out_specs=out_specs, check_vma=False
    )
```

time: 222 us -> 161 us (0.73)
  blocking collectives: 74.9 us -> 24.2 us
  starting transfers between devices: 34.3 us -> 52.6 us
  between operations: 14.2 us -> 0.87 us
  waiting for transfers between devices: 48.5 us -> 37.6 us
  local copies, waits for them, and re-layouts: 12.9 us -> 8.88 us
    all_gather x1 -> x0, blocking collectives: 60.7 us -> none  [after_states(): totals = lax.all_gather(total, 'ctx', axis=0, axis_index_groups=strided)]
    all_to_all x0 -> x2, blocking collectives: none -> 24.2 us  [the longest x1 13.9 us: per_device(): lax.all_to_all(copies, 'head', 0, 0, tiled=True, axis_index_groups=same_c...]
    all_to_all x3 -> x5, starting transfers between devices: 13 us -> 29.4 us  [the longest x3 21.5 us: after_states(): lax.all_to_all(x, 'ctx', 0, 0, tiled=True, axis_index_groups=groups)]
    all_gather x1 -> x0, waiting for transfers between devices: 15.1 us -> none  [per_device(): dkv_all = lax.all_gather(dkv, 'head', axis=0)]
    psum x1 -> x0, blocking collectives: 14.2 us -> none  [per_device(): stats = lax.psum(stats, 'head')]
    all_to_all x3 -> x5, waiting for transfers between devices: 13.9 us -> 23.2 us  [the longest x3 17.7 us: after_states(): lax.all_to_all(x, 'ctx', 0, 0, tiled=True, axis_index_groups=groups)]
    ppermute x6, waiting for transfers between devices: 19.5 us -> 12.5 us  [passed_along(): return lax.ppermute(block, 'ctx', route)]
    unnamed x24 -> x18, local copies, waits for them, and re-layouts: 6.06 us -> 3.39 us
  transfers between devices with their start and end apart: 10 -> 12, of which waited for: 9 -> 9; matrix products, arithmetic and copies ran while one was open for 4% -> 4% of each run, Pallas kernels for 4% -> 13%
where the time goes in v2:
time: 161 us; the launch traced here: 159 us
  starting transfers between devices  52.6 us (33%)
  waiting for transfers between devices  37.6 us (23%)
  Pallas kernels  33.5 us (21%)
  blocking collectives  24.2 us (15%)
  local copies, waits for them, and re-layouts  8.88 us (6%)
  other arithmetic  1.78 us (1%)
    all_to_all x3, starting transfers between devices, after_states(): lax.all_to_all(x, 'ctx', 0, 0, tiled=True, axis_index_groups=groups)  21.5 us
    ppermute x6, starting transfers between devices, passed_along(): return lax.ppermute(block, 'ctx', route)  21.2 us
    all_to_all x3, waiting for transfers between devices, after_states(): lax.all_to_all(x, 'ctx', 0, 0, tiled=True, axis_index_groups=groups)  17.7 us
    all_to_all x1, blocking collectives, per_device(): lax.all_to_all(copies, 'head', 0, 0, tiled=True, axis_index_groups=same_c...  13.9 us
    ppermute x6, waiting for transfers between devices, passed_along(): return lax.ppermute(block, 'ctx', route)  12.5 us
    pallas_call x1, Pallas kernels, softmax_call(): pl.pallas_call(functools.partial(softmax_kernel, length), out_shape=(jax....  11.9 us
    all_to_all x1, blocking collectives, after_states(): lax.all_to_all(x, 'ctx', 0, 0, tiled=True, axis_index_groups=groups)  10.2 us
    all_to_all x1, waiting for transfers between devices, per_device(): stats = lax.all_to_all(stats, 'head', 0, 0, tiled=True)  5.53 us
  transfers between devices with their start and end apart: 12, of which 9 were waited for; matrix products, arithmetic and copies ran while one was open for 4% of the time, Pallas kernels for 13%

profile of v2, /device:TPU:32, one launch (start us, length us, event | category | flops | bytes accessed | tf_op | source)
XLA Modules:
  0.0 159.3 jit_solution(7713897191780391193)
XLA Ops:
  0.6 0.9 pad_maximum_fusion.kv0
  1.5 7.7 %collective-permute-start = (bf16[2,256,128]{2,1,0:T(8,128)(2,1)S(1)}, bf16[2,256,128]{2,1,0:T(8,128)(2,1)S(1)}, u32[]{:S(2)}, u32[]{:S(2)}) collective-permute-start(bf16[2,256,128]{2,1,0:T(8,128)(2,1)S(1)} %pad_maximum_fusion.kv0), channel_id=1, source_target_pairs={{0,24},{8,32},{16,40},{24,48},{32,56},{40,64},{48,72},{56,80},{64,... | collective-permute-start | bytes 393224 | tf_op jit(solution)/shard_map/ppermute | solution.py:398
  9.3 5.2 %collective-permute-start.1 = (bf16[2,256,128]{2,1,0:T(8,128)(2,1)S(1)}, bf16[2,256,128]{2,1,0:T(8,128)(2,1)S(1)}, u32[]{:S(2)}, u32[]{:S(2)}) collective-permute-start(bf16[2,256,128]{2,1,0:T(8,128)(2,1)S(1)} %pad_maximum_fusion.kv0), channel_id=1, source_target_pairs={{0,16},{8,24},{16,32},{24,40},{32,48},{40,56},{48,64},{56,72},{64,... | collective-permute-start | bytes 393224 | tf_op jit(solution)/shard_map/ppermute | solution.py:398
  14.5 3.8 %collective-permute-start.2 = (bf16[2,256,128]{2,1,0:T(8,128)(2,1)S(1)}, bf16[2,256,128]{2,1,0:T(8,128)(2,1)S(1)}, u32[]{:S(2)}, u32[]{:S(2)}) collective-permute-start(bf16[2,256,128]{2,1,0:T(8,128)(2,1)S(1)} %pad_maximum_fusion.kv0), channel_id=1, source_target_pairs={{0,8},{8,16},{16,24},{24,32},{32,40},{40,48},{48,56},{56,64},{64,7... | collective-permute-start | bytes 393224 | tf_op jit(solution)/shard_map/ppermute | solution.py:398
  18.3 3.1 %copy.22 = bf16[2,8,512,128]{3,2,0,1:T(8,128)(2,1)} copy(bf16[2,8,512,128]{3,2,1,0:T(8,128)(2,1)} %bitcast.12) | data formatting | bytes 4194304 | tf_op jit(solution)/shard_map/reshape | solution.py:414
  21.4 0.0 copy-start.4
  21.4 4.6 %all-to-all-start = ((bf16[8,2,512,128]{3,2,1,0:T(8,128)(2,1)}), bf16[8,2,512,128]{3,2,1,0:T(8,128)(2,1)}, u32[]{:S(2)}, u32[]{:S(2)}) async-start(bf16[8,2,512,128]{3,2,1,0:T(8,128)(2,1)} %bitcast.9), calls=%async_computation | async-start | bytes 4194304 | tf_op jit(solution)/shard_map/all_to_all | solution.py:415
  26.0 0.0 collective-permute-done.kv3
  26.0 0.0 collective-permute-done.1.kv2
  26.0 1.7 %collective-permute-done.2.kv1 = bf16[2,256,128]{2,1,0:T(8,128)(2,1)S(1)} collective-permute-done((bf16[2,256,128]{2,1,0:T(8,128)(2,1)S(1)}, bf16[2,256,128]{2,1,0:T(8,128)(2,1)S(1)}, u32[]{:S(2)}, u32[]{:S(2)}) %collective-permute-start.2) | collective-permute-done | bytes 131104 | tf_op jit(solution)/shard_map/ppermute | solution.py:398
  27.7 0.0 copy-done.4
  27.7 11.9 %softmax_backward.1 = (bf16[256,1024]{1,0:T(8,128)(2,1)}, bf16[256,256]{1,0:T(8,128)(2,1)S(1)}, bf16[256,256]{1,0:T(8,128)(2,1)S(1)}, bf16[256,256]{1,0:T(8,128)(2,1)S(1)}, f32[256,256]{1,0:T(8,128)S(1)}) custom-call(s32[1]{0:T(128)S(6)} %mul.24.base_ref, s32[1,32]{1,0:T(1,128)S(1)} %bitcast.11, bf16[256,1024]{1,0:T(8,128)(2,1)} %q_ref.1, ...), custom_call_target="tpu_custom_call" | custom-call | flops 214748364800 | bytes 4194304 | tf_op jit(solution)/shard_map/softmax_backward/pallas_call | solution.py:127
  39.6 1.3 collective-permute-start.3
  40.9 1.3 collective-permute-start.4
  42.2 1.9 %collective-permute-start.5 = (bf16[256,256]{1,0:T(8,128)(2,1)S(1)}, bf16[256,256]{1,0:T(8,128)(2,1)S(1)}, u32[]{:S(2)}, u32[]{:S(2)}) collective-permute-start(bf16[256,256]{1,0:T(8,128)(2,1)S(1)} %get-tuple-element.39), channel_id=1, source_target_pairs={{8,0},{16,8},{24,16},{32,24},{40,32},{48,40},{56,48},{64,56},{72,6... | collective-permute-start | bytes 393224 | tf_op jit(solution)/shard_map/ppermute | solution.py:398
  44.1 3.9 %lightning_forward.1 = (f32[256,512]{1,0:T(8,128)}, bf16[256,512]{1,0:T(8,128)(2,1)}, f32[256,512]{1,0:T(8,128)}) custom-call(s32[1]{0:T(128)} %bitcast.1.block_ref, bf16[256,512]{1,0:T(8,128)(2,1)} %q_ref.3, bf16[256,512]{1,0:T(8,128)(2,1)} %k_ref.5, bf16[256,512]{1,0:T(8,128)(2,1)} %v_ref.5, f32[4,16384]{1,0:T(4,128)} %log_ref.3, ...), custom_call_target="tpu_custom_call" | custom-call | flops 1342177280 | bytes 4194304 | tf_op jit(solution)/shard_map/lightning_forward/pallas_call | solution.py:184
  48.0 0.0 copy-start
  48.0 0.0 copy-start.2
  48.1 0.0 copy-start.3
  48.1 3.7 %collective-permute-done.3 = bf16[256,256]{1,0:T(8,128)(2,1)S(1)} collective-permute-done((bf16[256,256]{1,0:T(8,128)(2,1)S(1)}, bf16[256,256]{1,0:T(8,128)(2,1)S(1)}, u32[]{:S(2)}, u32[]{:S(2)}) %collective-permute-start.3) | collective-permute-done | bytes 131104 | tf_op jit(solution)/shard_map/ppermute | solution.py:398
  51.7 6.9 %collective-permute-done.4 = bf16[256,256]{1,0:T(8,128)(2,1)S(1)} collective-permute-done((bf16[256,256]{1,0:T(8,128)(2,1)S(1)}, bf16[256,256]{1,0:T(8,128)(2,1)S(1)}, u32[]{:S(2)}, u32[]{:S(2)}) %collective-permute-start.4) | collective-permute-done | bytes 131104 | tf_op jit(solution)/shard_map/ppermute | solution.py:398
  58.6 0.3 collective-permute-done.5
  58.9 0.1 add_convert_fusion
  59.0 0.0 all-to-all-done.proj_ref
  59.1 13.9 %all_to_all.35.own_ref = bf16[4,256,256]{2,1,0:T(8,128)(2,1)S(1)} all-to-all(bf16[4,256,256]{2,1,0:T(8,128)(2,1)S(1)} %broadcast_in_dim.51), channel_id=1, replica_groups={{0,2,4,6},{1,3,5,7},{8,10,12,14},{9,11,13,15},{16,18,20,22},{17,19,21,2..., dimensions={0} | all-to-all | bytes 1048576 | tf_op jit(solution)/shard_map/all_to_all | solution.py:433
  73.0 1.9 %collective-permute-start.6 = (bf16[4,256,256]{2,1,0:T(8,128)(2,1)S(1)}, bf16[4,256,256]{2,1,0:T(8,128)(2,1)S(1)}, u32[]{:S(2)}, u32[]{:S(2)}) collective-permute-start(bf16[4,256,256]{2,1,0:T(8,128)(2,1)S(1)} %all_to_all.35.own_ref), channel_id=1, source_target_pairs={{0,1},{1,0},{2,3},{3,2},{4,5},{5,4},{6,7},{7,6},{8,9},{9,8},{10,11... | collective-permute-start | bytes 1572872 | tf_op jit(solution)/shard_map/ppermute | solution.py:434
  74.9 1.8 %collective-permute-done.6.other_ref = bf16[4,256,256]{2,1,0:T(8,128)(2,1)S(1)} collective-permute-done((bf16[4,256,256]{2,1,0:T(8,128)(2,1)S(1)}, bf16[4,256,256]{2,1,0:T(8,128)(2,1)S(1)}, u32[]{:S(2)}, u32[]{:S(2)}) %collective-permute-start.6) | collective-permute-done | bytes 524320 | tf_op jit(solution)/shard_map/ppermute | solution.py:434
  76.8 0.0 copy-done
  76.8 0.0 copy-done.2
  76.8 0.0 copy-done.3
  76.8 3.6 %cotangent.1 = (f32[256,512]{1,0:T(8,128)S(1)}, f32[8,8,256]{2,1,0:T(8,128)}) custom-call(s32[1]{0:T(128)} %bitcast.core_ref, bf16[4,256,256]{2,1,0:T(8,128)(2,1)S(1)} %all_to_all.35.own_ref, bf16[4,256,256]{2,1,0:T(8,128)(2,1)S(1)} %collective-permute-done.6.other_ref, bf16[8,2,512,128]{3,2,1,0:T(8,128)(2,1)} %all-to-all-done.proj_ref, ...), custom_call_target="tpu_custom_call" | custom-call | tf_op jit(solution)/shard_map/cotangent/pallas_call | solution.py:222
  80.4 0.0 copy-start.1
  80.4 0.8 copy-done.1
  81.2 3.4 %all-to-all-start.2 = ((f32[8,8,256]{2,1,0:T(8,128)}), f32[8,8,256]{2,1,0:T(8,128)S(1)}, u32[]{:S(2)}, u32[]{:S(2)}) async-start(f32[8,8,256]{2,1,0:T(8,128)} %get-tuple-element.46), calls=%async_computation.2 | async-start | bytes 131072 | tf_op jit(solution)/shard_map/all_to_all | solution.py:439
  84.5 5.5 %all-to-all-done.2.stats_ref = f32[8,8,256]{2,1,0:T(8,128)S(1)} async-done(((f32[8,8,256]{2,1,0:T(8,128)}), f32[8,8,256]{2,1,0:T(8,128)S(1)}, u32[]{:S(2)}, u32[]{:S(2)}) %all-to-all-start.2) | async-done | bytes 65568 | tf_op jit(solution)/shard_map/all_to_all | solution.py:439
  90.1 0.0 copy-start.8
  90.1 0.6 copy-done.8
  90.7 2.3 %dout_summary.1 = (bf16[256,512]{1,0:T(8,128)(2,1)}, bf16[4,128,128]{2,1,0:T(8,128)(2,1)}) custom-call(f32[8,8,256]{2,1,0:T(8,128)} %copy-done.8, f32[256,512]{1,0:T(8,128)} %copy-done.1, f32[256,512]{1,0:T(8,128)} %get-tuple-element.45.out_ref, bf16[256,512]{1,0:T(8,128)(2,1)} %get-tuple-element.48.scaled_ref), custom_call_target="tpu_custom_call" | custom-call | tf_op jit(solution)/shard_map/dout_summary/pallas_call | solution.py:248
  93.0 7.2 %all-to-all-start.3 = ((bf16[4,128,128]{2,1,0:T(8,128)(2,1)}), bf16[4,128,128]{2,1,0:T(8,128)(2,1)S(1)}, u32[]{:S(2)}, u32[]{:S(2)}) async-start(bf16[4,128,128]{2,1,0:T(8,128)(2,1)} %get-tuple-element.49), calls=%async_computation.3 | async-start | bytes 262144 | tf_op jit(solution)/shard_map/all_to_all | solution.py:377
  100.2 1.1 dynamic-slice_reduce_fusion
  101.4 0.1 broadcast_in_dim.46
  101.5 0.1 reshape.41
  101.5 0.1 tile.10
  101.6 0.1 reduce_sum.18
  101.8 0.1 concatenate.10
  101.9 0.1 concatenate.11
  102.0 0.1 concatenate.9
  102.1 0.2 select_reduce_fusion
  102.3 0.5 exponential_select_fusion.weight_ref
  102.8 2.6 %all-to-all-done.3.blocks_ref = bf16[4,128,128]{2,1,0:T(8,128)(2,1)S(1)} async-done(((bf16[4,128,128]{2,1,0:T(8,128)(2,1)}), bf16[4,128,128]{2,1,0:T(8,128)(2,1)S(1)}, u32[]{:S(2)}, u32[]{:S(2)}) %all-to-all-start.3) | async-done | bytes 131104 | tf_op jit(solution)/shard_map/all_to_all | solution.py:377
  105.4 0.7 copy-done.5
  106.0 1.6 rise.2
  107.6 10.5 %all-to-all-start.4 = ((bf16[4,128,128]{2,1,0:T(8,128)(2,1)}), bf16[4,128,128]{2,1,0:T(8,128)(2,1)S(1)}, u32[]{:S(2)}, u32[]{:S(2)}) async-start(bf16[4,128,128]{2,1,0:T(8,128)(2,1)} %rise.2), calls=%async_computation.4 | async-start | bytes 262144 | tf_op jit(solution)/shard_map/all_to_all | solution.py:377
  118.1 4.1 %near_far.1 = (bf16[256,512]{1,0:T(8,128)(2,1)}, f32[256,512]{1,0:T(8,128)}, f32[256,512]{1,0:T(8,128)}) custom-call(s32[1]{0:T(128)} %bitcast.1.block_ref, bf16[256,512]{1,0:T(8,128)(2,1)} %q_ref.3, bf16[256,512]{1,0:T(8,128)(2,1)} %k_ref.5, bf16[256,512]{1,0:T(8,128)(2,1)} %v_ref.5, bf16[256,512]{1,0:T(8,128)(2,1)} %get-tuple-element.50.dout_ref, ...), custom_call_target="tpu_custom_call" | custom-call | flops 3489660928 | bytes 4194304 | tf_op jit(solution)/shard_map/near_far/pallas_call | solution.py:281
  122.2 10.6 %all-to-all-done.4.blocks_ref.groups_ref = bf16[4,128,128]{2,1,0:T(8,128)(2,1)S(1)} async-done(((bf16[4,128,128]{2,1,0:T(8,128)(2,1)}), bf16[4,128,128]{2,1,0:T(8,128)(2,1)S(1)}, u32[]{:S(2)}, u32[]{:S(2)}) %all-to-all-start.4) | async-done | bytes 131104 | tf_op jit(solution)/shard_map/all_to_all | solution.py:377
  132.8 0.7 copy-done.6
  133.4 1.6 %rise.3 = bf16[4,128,128]{2,1,0:T(8,128)(2,1)} custom-call(f32[36]{0:T(128)} %exponential_select_fusion.weight_ref, bf16[4,128,128]{2,1,0:T(8,128)(2,1)} %copy-done.6), custom_call_target="tpu_custom_call" | custom-call | tf_op jit(solution)/shard_map/rise/pallas_call | solution.py:380
  135.0 10.2 %all_to_all.36.rows_ref = bf16[4,128,128]{2,1,0:T(8,128)(2,1)} all-to-all(bf16[4,128,128]{2,1,0:T(8,128)(2,1)} %rise.3), channel_id=1, replica_groups={{0,128,256,384},{8,136,264,392},{16,144,272,400},{24,152,280,408},{32,1..., dimensions={0} | all-to-all | bytes 262144 | tf_op jit(solution)/shard_map/all_to_all | solution.py:377
  145.3 1.8 %after_states.1 = bf16[4,128,128]{2,1,0:T(8,128)(2,1)} custom-call(f32[36]{0:T(128)} %exponential_select_fusion.weight_ref, bf16[4,128,128]{2,1,0:T(8,128)(2,1)} %copy-done.5, bf16[4,128,128]{2,1,0:T(8,128)(2,1)} %copy-done.6, bf16[4,128,128]{2,1,0:T(8,128)(2,1)} %all_to_all.36.rows_ref), custom_call_target="tpu_custom_call" | custom-call | tf_op jit(solution)/shard_map/after_states/pallas_call | solution.py:389
  147.1 3.8 %all-to-all-start.6 = ((bf16[4,128,128]{2,1,0:T(8,128)(2,1)}), bf16[4,128,128]{2,1,0:T(8,128)(2,1)S(1)}, u32[]{:S(2)}, u32[]{:S(2)}) async-start(bf16[4,128,128]{2,1,0:T(8,128)(2,1)} %after_states.1), calls=%async_computation.6 | async-start | bytes 262144 | tf_op jit(solution)/shard_map/all_to_all | solution.py:377
  150.9 0.7 fusion.1
  151.6 4.5 %all-to-all-done.6.after_ref = bf16[4,128,128]{2,1,0:T(8,128)(2,1)S(1)} async-done(((bf16[4,128,128]{2,1,0:T(8,128)(2,1)}), bf16[4,128,128]{2,1,0:T(8,128)(2,1)S(1)}, u32[]{:S(2)}, u32[]{:S(2)}) %all-to-all-start.6) | async-done | bytes 131104 | tf_op jit(solution)/shard_map/all_to_all | solution.py:377
  156.1 0.6 copy-done.7
  156.7 2.6 %last.1 = (bf16[256,512]{1,0:T(8,128)(2,1)}, bf16[256,512]{1,0:T(8,128)(2,1)}) custom-call(bf16[256,512]{1,0:T(8,128)(2,1)} %k_ref.5, bf16[256,512]{1,0:T(8,128)(2,1)} %v_ref.5, f32[256,512]{1,0:T(8,128)} %get-tuple-element.55.dk_ref, f32[256,512]{1,0:T(8,128)} %get-tuple-element.56.dv_ref, f32[256,512]{1,0:T(8,128)} %get-tuple-element.57.tail_ref, ...), custom_call_target="tpu_custom_call" | custom-call | tf_op jit(solution)/shard_map/last/pallas_call | solution.py:312
  (16 shorter events, 0.1 us)
Async XLA Ops:
  1.5 24.5 %collective-permute-start = (bf16[2,256,128]{2,1,0:T(8,128)(2,1)S(1)}, bf16[2,256,128]{2,1,0:T(8,128)(2,1)S(1)}, u32[]{:S(2)}, u32[]{:S(2)}) collective-permute-start(bf16[2,256,128]{2,1,0:T(8,128)(2,1)S(1)} %pad_maximum_fusion.kv0), channel_id=1, source_target_pairs={{0,24},{8,32},{16,40},{24,48},{32,56},{40,64},{48,72},{56,80},{64,... | collective-permute-start | bytes 393224 | tf_op jit(solution)/shard_map/ppermute | solution.py:398
  9.3 16.7 %collective-permute-start.1 = (bf16[2,256,128]{2,1,0:T(8,128)(2,1)S(1)}, bf16[2,256,128]{2,1,0:T(8,128)(2,1)S(1)}, u32[]{:S(2)}, u32[]{:S(2)}) collective-permute-start(bf16[2,256,128]{2,1,0:T(8,128)(2,1)S(1)} %pad_maximum_fusion.kv0), channel_id=1, source_target_pairs={{0,16},{8,24},{16,32},{24,40},{32,48},{40,56},{48,64},{56,72},{64,... | collective-permute-start | bytes 393224 | tf_op jit(solution)/shard_map/ppermute | solution.py:398
  14.5 13.2 %collective-permute-start.2 = (bf16[2,256,128]{2,1,0:T(8,128)(2,1)S(1)}, bf16[2,256,128]{2,1,0:T(8,128)(2,1)S(1)}, u32[]{:S(2)}, u32[]{:S(2)}) collective-permute-start(bf16[2,256,128]{2,1,0:T(8,128)(2,1)S(1)} %pad_maximum_fusion.kv0), channel_id=1, source_target_pairs={{0,8},{8,16},{16,24},{24,32},{32,40},{40,48},{48,56},{56,64},{64,7... | collective-permute-start | bytes 393224 | tf_op jit(solution)/shard_map/ppermute | solution.py:398
  21.4 6.3 %copy-start.4 = (s32[32]{0:T(128)S(1)}, s32[32]{0:T(128)}, u32[]{:S(2)}) copy-start(s32[32]{0:T(128)} %param.25) | copy-start | bytes 388
  21.4 37.6 %all-to-all-start = ((bf16[8,2,512,128]{3,2,1,0:T(8,128)(2,1)}), bf16[8,2,512,128]{3,2,1,0:T(8,128)(2,1)}, u32[]{:S(2)}, u32[]{:S(2)}) async-start(bf16[8,2,512,128]{3,2,1,0:T(8,128)(2,1)} %bitcast.9), calls=%async_computation | async-start | bytes 4194304 | tf_op jit(solution)/shard_map/all_to_all | solution.py:415
  39.6 12.1 %collective-permute-start.3 = (bf16[256,256]{1,0:T(8,128)(2,1)S(1)}, bf16[256,256]{1,0:T(8,128)(2,1)S(1)}, u32[]{:S(2)}, u32[]{:S(2)}) collective-permute-start(bf16[256,256]{1,0:T(8,128)(2,1)S(1)} %get-tuple-element.37), channel_id=1, source_target_pairs={{24,0},{32,8},{40,16},{48,24},{56,32},{64,40},{72,48},{80,56},{88,... | collective-permute-start | bytes 393224 | tf_op jit(solution)/shard_map/ppermute | solution.py:398
  40.9 17.7 %collective-permute-start.4 = (bf16[256,256]{1,0:T(8,128)(2,1)S(1)}, bf16[256,256]{1,0:T(8,128)(2,1)S(1)}, u32[]{:S(2)}, u32[]{:S(2)}) collective-permute-start(bf16[256,256]{1,0:T(8,128)(2,1)S(1)} %get-tuple-element.38), channel_id=1, source_target_pairs={{16,0},{24,8},{32,16},{40,24},{48,32},{56,40},{64,48},{72,56},{80,... | collective-permute-start | bytes 393224 | tf_op jit(solution)/shard_map/ppermute | solution.py:398
  42.2 16.7 %collective-permute-start.5 = (bf16[256,256]{1,0:T(8,128)(2,1)S(1)}, bf16[256,256]{1,0:T(8,128)(2,1)S(1)}, u32[]{:S(2)}, u32[]{:S(2)}) collective-permute-start(bf16[256,256]{1,0:T(8,128)(2,1)S(1)} %get-tuple-element.39), channel_id=1, source_target_pairs={{8,0},{16,8},{24,16},{32,24},{40,32},{48,40},{56,48},{64,56},{72,6... | collective-permute-start | bytes 393224 | tf_op jit(solution)/shard_map/ppermute | solution.py:398
  48.0 28.7 %copy-start = (f32[256,512]{1,0:T(8,128)S(1)}, f32[256,512]{1,0:T(8,128)}, u32[]{:S(2)}) copy-start(f32[256,512]{1,0:T(8,128)} %get-tuple-element.45.out_ref) | copy-start | bytes 1572868
  48.0 28.7 %copy-start.2 = (bf16[256,512]{1,0:T(8,128)(2,1)S(1)}, bf16[256,512]{1,0:T(8,128)(2,1)}, u32[]{:S(2)}) copy-start(bf16[256,512]{1,0:T(8,128)(2,1)} %grad_ref.1) | copy-start | bytes 786436
  48.1 28.7 %copy-start.3 = (f32[512]{0:T(512)S(1)}, f32[512]{0:T(512)}, u32[]{:S(2)}) copy-start(f32[512]{0:T(512)} %param.17) | copy-start | bytes 6148
  73.0 3.8 %collective-permute-start.6 = (bf16[4,256,256]{2,1,0:T(8,128)(2,1)S(1)}, bf16[4,256,256]{2,1,0:T(8,128)(2,1)S(1)}, u32[]{:S(2)}, u32[]{:S(2)}) collective-permute-start(bf16[4,256,256]{2,1,0:T(8,128)(2,1)S(1)} %all_to_all.35.own_ref), channel_id=1, source_target_pairs={{0,1},{1,0},{2,3},{3,2},{4,5},{5,4},{6,7},{7,6},{8,9},{9,8},{10,11... | collective-permute-start | bytes 1572872 | tf_op jit(solution)/shard_map/ppermute | solution.py:434
  80.4 0.8 copy-start.1
  81.2 8.9 %all-to-all-start.2 = ((f32[8,8,256]{2,1,0:T(8,128)}), f32[8,8,256]{2,1,0:T(8,128)S(1)}, u32[]{:S(2)}, u32[]{:S(2)}) async-start(f32[8,8,256]{2,1,0:T(8,128)} %get-tuple-element.46), calls=%async_computation.2 | async-start | bytes 131072 | tf_op jit(solution)/shard_map/all_to_all | solution.py:439
  90.1 0.6 copy-start.8
  93.0 12.4 %all-to-all-start.3 = ((bf16[4,128,128]{2,1,0:T(8,128)(2,1)}), bf16[4,128,128]{2,1,0:T(8,128)(2,1)S(1)}, u32[]{:S(2)}, u32[]{:S(2)}) async-start(bf16[4,128,128]{2,1,0:T(8,128)(2,1)} %get-tuple-element.49), calls=%async_computation.3 | async-start | bytes 262144 | tf_op jit(solution)/shard_map/all_to_all | solution.py:377
  105.4 0.7 copy-start.5
  107.6 25.2 %all-to-all-start.4 = ((bf16[4,128,128]{2,1,0:T(8,128)(2,1)}), bf16[4,128,128]{2,1,0:T(8,128)(2,1)S(1)}, u32[]{:S(2)}, u32[]{:S(2)}) async-start(bf16[4,128,128]{2,1,0:T(8,128)(2,1)} %rise.2), calls=%async_computation.4 | async-start | bytes 262144 | tf_op jit(solution)/shard_map/all_to_all | solution.py:377
  132.8 0.7 copy-start.6
  147.1 9.0 %all-to-all-start.6 = ((bf16[4,128,128]{2,1,0:T(8,128)(2,1)}), bf16[4,128,128]{2,1,0:T(8,128)(2,1)S(1)}, u32[]{:S(2)}, u32[]{:S(2)}) async-start(bf16[4,128,128]{2,1,0:T(8,128)(2,1)} %after_states.1), calls=%async_computation.6 | async-start | bytes 262144 | tf_op jit(solution)/shard_map/all_to_all | solution.py:377
  156.1 0.6 copy-start.7

commit v3 on v2

--- a/solution.py
+++ b/solution.py
@@ -16,7 +16,7 @@
 FEATURES = LIGHTNING_HEADS * DH
 SUB = 4
 QUAD = 4
-AT_ONCE = 2
+AT_ONCE = 8
 TILES = 2
 epsilon = 1e-06
 
@@ -150,7 +150,7 @@
 
 
 def forward_kernel(
-    block_ref, q_ref, k_ref, v_ref, log_ref, state_ref, out_ref, scaled_ref, tail_ref
+    block_ref, q_ref, k_ref, v_ref, gain_ref, log_ref, state_ref, out_ref, gained_ref, scaled_ref, tail_ref
 ):
     head = pl.program_id(0)
     length = q_ref.shape[0]
@@ -161,6 +161,7 @@
     scaled = (q_ref[...].astype(F32) * jnp.exp(g_col)).astype(BF16)
     out = (mm(near, v_ref[...]) + mm(scaled, state_ref[0, 0])) * (1.0 / DH)
     out_ref[...] = out
+    gained_ref[...] = (out * gain_ref[...]).astype(BF16)
     scaled_ref[...] = scaled
     tail_ref[...] = jnp.broadcast_to(jnp.exp(g_col[length - 1:, :] - g_col), out.shape)
 
@@ -177,74 +178,134 @@
     return pl.BlockSpec((heads, length), lambda h, b: (0, b[0]))
 
 
-def forward_call(block, q, k, v, log_decay, state):
+def forward_call(block, q, k, v, gain, log_decay, state):
     length, heads = q.shape[0], q.shape[1] // DH
     wide = per_head_spec(length)
     like = lambda dtype: jax.ShapeDtypeStruct(q.shape, dtype)
     return pl.pallas_call(
         forward_kernel,
-        out_shape=(like(F32), like(BF16), like(F32)),
+        out_shape=(like(F32), like(BF16), like(BF16), like(F32)),
         grid_spec=pltpu.PrefetchScalarGridSpec(
             num_scalar_prefetch=1, grid=(heads,),
-            in_specs=[wide, wide, wide, log_spec(heads, length), state_spec()],
-            out_specs=(wide, wide, wide),
+            in_specs=[
+                wide, wide, wide, pl.BlockSpec((1, DH), lambda h, b: (0, h)), log_spec(heads, length),
+                state_spec(),
+            ],
+            out_specs=(wide, wide, wide, wide),
         ),
         cost_estimate=pl.CostEstimate(
             flops=heads * length * DH * (4 * length + 2 * DH) * 8, bytes_accessed=4 * 1024 * 1024,
             transcendentals=heads * length * length,
         ),
         name="lightning_forward",
-    )(block, q, k, v, log_decay, state)
+    )(block, q, k, v, gain, log_decay, state)
+
+
+def pack_kernel(proj_ref, packed_ref):
+    packed_ref[:, :, :DH] = proj_ref[0]
+    packed_ref[:, :, DH:] = proj_ref[1]
+
+
+def pack_call(projections, chips):
+    rows = projections.shape[1] // chips
+    some = chips // 2
+    return pl.pallas_call(
+        pack_kernel,
+        grid=(chips // some,),
+        in_specs=[pl.BlockSpec((2, some, rows, DH), lambda i: (0, i, 0, 0))],
+        out_specs=pl.BlockSpec((some, rows, 2 * DH), lambda i: (i, 0, 0)),
+        out_shape=jax.ShapeDtypeStruct((chips, rows, 2 * DH), BF16),
+        cost_estimate=pl.CostEstimate(flops=0, bytes_accessed=4 * 1024 * 1024, transcendentals=0),
+        name="pack",
+    )(projections.reshape(2, chips, rows, DH))
+
+
+PARTS = 2
 
 
 def cotangent_kernel(
-    core_ref, own_ref, other_ref, proj_ref, grad_ref, gain_ref, out_ref, gated_ref, stats_ref
+    core_ref, dkv_ref, proj_ref, sibling_ref, grad_ref, gain_ref, out_ref,
+    gated_ref, carried_ref, stats_ref, squares, cross,
 ):
-    core = core_ref[0]
-    total = grad_ref[...].astype(F32)
-    for chip in range(own_ref.shape[0]):
-        for dkv_ref, g in ((own_ref, 2 * chip + core), (other_ref, 2 * chip + 1 - core)):
-            for side in range(2):
-                total += mm(dkv_ref[chip, :, side * DH:(side + 1) * DH], proj_ref[g, side], NT)
-    gated = gain_ref[...] * total
-    gated_ref[...] = gated
-    out = out_ref[...]
-    squares = to_row(jnp.sum(out * out, axis=1, keepdims=True))
-    cross = to_row(jnp.sum(gated * out, axis=1, keepdims=True))
-    rows = iota2(stats_ref.shape[1:], 0)
-    stats = jnp.where(rows == 0, squares, jnp.where(rows == 1, cross, 0.0))
-    for copy in range(stats_ref.shape[0]):
-        stats_ref[copy] = stats
-
-
-def cotangent_call(core, own, other, proj, grad, gain, out):
-    vmem = pl.BlockSpec(memory_space=pltpu.VMEM)
+    step = pl.program_id(0)
+    carried = jnp.zeros(carried_ref.shape, F32)
+    for chip in range(dkv_ref.shape[0]):
+        carried += mm(dkv_ref[chip], proj_ref[chip], NT)
+
+    @pl.when(step == 0)
+    def _():
+        squares[...] = jnp.zeros_like(squares)
+        cross[...] = jnp.zeros_like(cross)
+
+    @pl.when(step < PARTS)
+    def _():
+        carried_ref[...] = carried
+        cross[...] += jnp.sum(sibling_ref[...].astype(F32) * carried, axis=1, keepdims=True)
+
+    @pl.when(step >= PARTS)
+    def _():
+        gated = gain_ref[...] * (grad_ref[...].astype(F32) + carried)
+        gated_ref[...] = gated
+        out = out_ref[...]
+        squares[...] += jnp.sum(out * out, axis=1, keepdims=True)
+        cross[...] += jnp.sum(gated * out, axis=1, keepdims=True)
+
+    @pl.when(step == pl.num_programs(0) - 1)
+    def _():
+        rows = iota2(stats_ref.shape[1:], 0)
+        stats = jnp.where(
+            rows == 0, to_row(squares[...]), jnp.where(rows == 1, to_row(cross[...]), 0.0)
+        )
+        for copy in range(stats_ref.shape[0]):
+            stats_ref[copy] = stats
+
+
+def cotangent_call(core, dkv, proj, sibling, grad, gain, out):
+    length, width = grad.shape
+    part = width // PARTS
+    whole = lambda *shape: pl.BlockSpec(shape, lambda i, c: (0,) * len(shape))
+    early = pl.BlockSpec((length, part), lambda i, c: (0, jnp.minimum(i, PARTS - 1)))
+    late = pl.BlockSpec((length, part), lambda i, c: (0, jnp.maximum(i - PARTS, 0)))
+
+    def features(i, c):
+        side = jnp.where(i < PARTS, 1 - c[0], c[0])
+        return (0, side * PARTS + i % PARTS, 0)
+
     return pl.pallas_call(
         cotangent_kernel,
-        in_specs=[pl.BlockSpec(memory_space=pltpu.SMEM)] + [vmem] * 6,
         out_shape=(
-            jax.ShapeDtypeStruct(grad.shape, F32),
-            jax.ShapeDtypeStruct((KV_HEADS, 8, grad.shape[0]), F32),
+            jax.ShapeDtypeStruct(grad.shape, F32), jax.ShapeDtypeStruct(grad.shape, F32),
+            jax.ShapeDtypeStruct((KV_HEADS, 8, length), F32),
+        ),
+        grid_spec=pltpu.PrefetchScalarGridSpec(
+            num_scalar_prefetch=1, grid=(2 * PARTS,),
+            in_specs=[
+                whole(*dkv.shape), pl.BlockSpec((dkv.shape[0], part, 2 * DH), features), early, late,
+                pl.BlockSpec((1, part), lambda i, c: (0, jnp.maximum(i - PARTS, 0))), late,
+            ],
+            out_specs=(late, early, whole(KV_HEADS, 8, length)),
+            scratch_shapes=[pltpu.VMEM((length, 1), F32), pltpu.VMEM((length, 1), F32)],
         ),
         compiler_params=pltpu.CompilerParams(vmem_limit_bytes=VMEM_LIMIT),
         name="cotangent",
-    )(core, own, other, proj, grad, gain, out)
-
-
-def dout_kernel(stats_ref, gated_ref, out_ref, scaled_ref, dout_ref, summary_ref):
+    )(core, dkv, proj, sibling, grad, gain, out)
+
+
+def dout_kernel(stats_ref, gated_ref, carried_ref, gain_ref, out_ref, scaled_ref, dout_ref, summary_ref):
     stats = stats_ref[0]
     for source in range(1, stats_ref.shape[0]):
         stats += stats_ref[source]
     inverse = 1.0 / jnp.sqrt(stats[0:1, :] * (1.0 / FEATURES) + epsilon)
     factor = stats[1:2, :] * (inverse * inverse * inverse) * (1.0 / FEATURES)
-    low = (gated_ref[...] * to_column(inverse) - out_ref[...] * to_column(factor)).astype(BF16)
+    gated = gated_ref[...] + gain_ref[...] * carried_ref[...]
+    low = (gated * to_column(inverse) - out_ref[...] * to_column(factor)).astype(BF16)
     dout_ref[...] = low
     for head in range(summary_ref.shape[0]):
         columns = slice(head * DH, (head + 1) * DH)
         summary_ref[head] = mm(scaled_ref[:, columns], low[:, columns], TN).astype(BF16)
 
 
-def dout_call(stats, gated, out, scaled):
+def dout_call(stats, gated, carried, gain, out, scaled):
     return pl.pallas_call(
         dout_kernel,
         out_shape=(
@@ -252,7 +313,7 @@
             jax.ShapeDtypeStruct((out.shape[1] // DH, DH, DH), BF16),
         ),
         name="dout_summary",
-    )(stats, gated, out, scaled)
+    )(stats, gated, carried, gain, out, scaled)
 
 
 def near_far_kernel(
@@ -316,80 +377,78 @@
     )(k, v, dk, dv, tail, after)
 
 
-ENTER, RISE, GROUPS, ROWS, LEAVE, INNER = 0, 4, 8, 12, 16, 20
+ENTER, LEAVE, INNER, CARRY = 0, 16, 32, 96
 
 
 def state_weights(log_decay, length, device):
-    place, group, row = device % QUAD, device // QUAD, device // (QUAD * QUAD)
-    decays = lax.dynamic_slice_in_dim(log_decay, place, 1, 0)
+    square = QUAD * QUAD
+    group, row = device // QUAD % QUAD, device // square
+    decays = lax.dynamic_slice_in_dim(log_decay, row, 1, 0)
     gamma = jnp.sum(decays.reshape(-1, length), axis=1)
     block = jnp.arange(gamma.shape[0], dtype=jnp.int32)
     quad = jnp.arange(QUAD, dtype=jnp.int32)
-    first, row_first = group * QUAD, row * QUAD * QUAD
-    same = lambda x: jnp.broadcast_to(x, (QUAD,))
-    group_first, rows_first = row_first + quad * QUAD, quad * QUAD * QUAD
+    first = quad * square + group * QUAD
+    own = (first[:, None] + quad[None, :]).reshape(-1)
+    every = jnp.arange(square, dtype=jnp.int32) * QUAD
     low = jnp.concatenate(
-        [same(first - 1), same(row_first - 1), same(first + QUAD - 1), same(first + QUAD - 1), first + quad,
-         jnp.repeat(first + quad, QUAD)]
+        [jnp.repeat(first - 1, QUAD), own, jnp.repeat(own, QUAD), jnp.repeat(first + QUAD - 1, square)]
     )
     high = jnp.concatenate(
-        [first + quad, group_first, group_first, rows_first, same(first + QUAD), jnp.tile(first + quad, QUAD)]
-    )
-    yes = jnp.ones((QUAD,), bool)
-    used = jnp.concatenate([yes, yes, group_first > first, quad > row, yes, jnp.ones((QUAD * QUAD,), bool)])
+        [own, jnp.repeat(first + QUAD, QUAD), jnp.tile(own.reshape(QUAD, QUAD), (1, QUAD)).reshape(-1),
+         jnp.tile(every, QUAD)]
+    )
     inside = (block[None, :] > low[:, None]) & (block[None, :] < high[:, None])
     factors = jnp.exp(jnp.sum(jnp.where(inside, gamma[None, :], 0.0), axis=1))
-    return jnp.where(used, factors, 0.0)
-
-
-def rise_kernel(first, weight_ref, blocks_ref, total_ref):
-    total = jnp.zeros(blocks_ref.shape[1:], F32)
-    for z in range(QUAD):
-        total += weight_ref[first + z] * blocks_ref[z].astype(F32)
-    total = total.astype(BF16)
-    for z in range(QUAD):
-        total_ref[z] = total
-
-
-def after_kernel(weight_ref, blocks_ref, groups_ref, rows_ref, after_ref):
-    carry = jnp.zeros(blocks_ref.shape[1:], F32)
-    for g in range(QUAD):
-        carry += weight_ref[GROUPS + g] * groups_ref[g].astype(F32)
-        carry += weight_ref[ROWS + g] * rows_ref[g].astype(F32)
-    for z in range(QUAD):
-        after = weight_ref[LEAVE + z] * carry
-        for later in range(z + 1, QUAD):
-            after += weight_ref[INNER + z * QUAD + later] * blocks_ref[later].astype(F32)
-        after_ref[z] = after.astype(BF16)
+    return jnp.where(high > low, factors, 0.0)
+
+
+def rise_kernel(weight_ref, blocks_ref, total_ref):
+    for row in range(QUAD):
+        total = jnp.zeros(blocks_ref.shape[1:], F32)
+        for z in range(QUAD):
+            at = row * QUAD + z
+            total += weight_ref[ENTER + at] * blocks_ref[at].astype(F32)
+        total = total.astype(BF16)
+        for copy in range(QUAD):
+            total_ref[copy, row] = total
+
+
+def after_kernel(weight_ref, blocks_ref, totals_ref, after_ref):
+    square = QUAD * QUAD
+    for row in range(QUAD):
+        carry = jnp.zeros(blocks_ref.shape[1:], F32)
+        for g in range(square):
+            carry += weight_ref[CARRY + row * square + g] * totals_ref[g % QUAD, g // QUAD].astype(F32)
+        for z in range(QUAD):
+            at = row * QUAD + z
+            after = weight_ref[LEAVE + at] * carry
+            for later in range(z + 1, QUAD):
+                after += weight_ref[INNER + at * QUAD + later] * blocks_ref[row * QUAD + later].astype(F32)
+            after_ref[at] = after.astype(BF16)
 
 
 def after_states(summary, weights, beside):
-    count = lax.axis_size("ctx")
     square = QUAD * QUAD
-    every = [[g * QUAD + i for i in range(QUAD)] for g in range(count // QUAD)]
-    over_groups = [
-        [r * square + i * QUAD + z for i in range(QUAD)] for r in range(count // square) for z in range(QUAD)
+    rows = lax.axis_size("ctx") // square
+    near = [
+        [r * square + g * QUAD + z for r in range(rows) for z in range(QUAD)] for g in range(QUAD)
     ]
-    over_rows = [[i * square + p for i in range(QUAD)] for p in range(square)]
+    far = [[r * square + g * QUAD + z for g in range(QUAD)] for r in range(rows) for z in range(QUAD)]
     smem = pl.BlockSpec(memory_space=pltpu.SMEM)
     vmem = pl.BlockSpec(memory_space=pltpu.VMEM)
-    shape = jax.ShapeDtypeStruct((QUAD, DH, DH), BF16)
     swap = lambda x, groups: lax.all_to_all(x, "ctx", 0, 0, tiled=True, axis_index_groups=groups)
-
-    def rise(first, blocks):
-        return pl.pallas_call(
-            functools.partial(rise_kernel, first), out_shape=shape,
-            in_specs=[smem, vmem], out_specs=vmem, name="rise",
-        )(weights, blocks)
-
-    blocks = swap(summary, every)
-    groups = swap(rise(ENTER, blocks), over_groups)
-    risen, beside = lax.optimization_barrier((rise(RISE, groups), beside))
-    rows = swap(risen, over_rows)
+    part = summary.size // square // DH
+    blocks = swap(summary.reshape(square, part, DH), near)
+    totals = pl.pallas_call(
+        rise_kernel, out_shape=jax.ShapeDtypeStruct((QUAD, rows, part, DH), BF16),
+        in_specs=[smem, vmem], out_specs=vmem, name="rise",
+    )(weights, blocks)
+    totals, beside = lax.optimization_barrier((swap(totals, far), beside))
     after = pl.pallas_call(
-        after_kernel, out_shape=shape, in_specs=[smem, vmem, vmem, vmem], out_specs=vmem, name="after_states",
-    )(weights, blocks, groups, rows)
-    return swap(after, every), beside
+        after_kernel, out_shape=jax.ShapeDtypeStruct(blocks.shape, BF16),
+        in_specs=[smem, vmem, vmem], out_specs=vmem, name="after_states",
+    )(weights, blocks, totals)
+    return swap(after, near).reshape(summary.shape), beside
 
 
 def passed_along(block, distance):
@@ -408,37 +467,43 @@
     block = device.reshape(1)
 
     heads = lax.axis_size("head")
+    chips = heads // 2
+    same_core = [[2 * chip + core for chip in range(chips)] for core in range(2)]
+    sibling = [(i, i ^ 1) for i in range(heads)]
+    core = (lax.axis_index("head").astype(jnp.int32) % 2).reshape(1)
+    gain = norm_gain.reshape(1, width)
+
     stacked = jnp.stack([soft_keys, soft_values])
     stacked, early = lax.optimization_barrier((stacked, projections))
     kv3, kv2, kv1 = (passed_along(stacked, offset) for offset in (3, 2, 1))
-    proj = early.reshape(2, KV_HEADS, width, DH).transpose(1, 0, 2, 3)
-    proj = lax.all_to_all(proj, "head", 0, 0, tiled=True)
+    proj = lax.all_to_all(
+        pack_call(early, chips), "head", 0, 0, tiled=True, axis_index_groups=same_core
+    )
     soft_query = pltpu.with_memory_space_constraint(soft_query, pltpu.HBM)
     soft_grad = pltpu.with_memory_space_constraint(soft_grad, pltpu.HBM)
     soft_dq, part3, part2, part1, own = softmax_call(
         block * length, doc_lengths.reshape(1, -1), soft_query, soft_grad, [kv3, kv2, kv1, stacked]
     )
     lin_query, own = lax.optimization_barrier((lin_query, own))
-    lin_out, scaled, tail = forward_call(
-        block, lin_query, lin_keys, lin_values, log_decay, state_in
-    )
+    lin_out, gained, scaled, tail = forward_call(
+        block, lin_query, lin_keys, lin_values, gain, log_decay, state_in
+    )
+    gained = lax.ppermute(gained, "head", sibling)
     summed = own
     for offset, part in ((3, part3), (2, part2), (1, part1)):
         summed = summed + passed_along(part, -offset).astype(F32)
-    dkv, lin_out, proj = lax.optimization_barrier((summed.astype(BF16), lin_out, proj))
+    dkv, lin_out, gained, proj, late_decay = lax.optimization_barrier(
+        (summed.astype(BF16), lin_out, gained, proj, log_decay)
+    )
+    weights = state_weights(late_decay, length, device)
     soft_dk, soft_dv = dkv[:, :DH], dkv[:, DH:]
 
-    same_core = [[2 * chip + core for chip in range(heads // 2)] for core in range(2)]
-    copies = jnp.broadcast_to(dkv[None], (heads // 2,) + dkv.shape)
-    own_dkv = lax.all_to_all(copies, "head", 0, 0, tiled=True, axis_index_groups=same_core)
-    other_dkv = lax.ppermute(own_dkv, "head", [(i, i ^ 1) for i in range(heads)])
-    core = (lax.axis_index("head").astype(jnp.int32) % 2).reshape(1)
-    gated, stats = cotangent_call(
-        core, own_dkv, other_dkv, proj, lin_grad, norm_gain.reshape(1, width), lin_out
-    )
+    copies = jnp.broadcast_to(dkv[None], (chips,) + dkv.shape)
+    dkv_all = lax.all_to_all(copies, "head", 0, 0, tiled=True, axis_index_groups=same_core)
+    gated, carried, stats = cotangent_call(core, dkv_all, proj, gained, lin_grad, gain, lin_out)
+    carried = lax.ppermute(carried, "head", sibling)
     stats = lax.all_to_all(stats, "head", 0, 0, tiled=True)
-    dout, summary = dout_call(stats, gated, lin_out, scaled)
-    weights = state_weights(log_decay, length, device)
+    dout, summary = dout_call(stats, gated, carried, gain, lin_out, scaled)
     beside = near_far_call(block, lin_query, lin_keys, lin_values, dout, log_decay, state_in)
     after, (lin_dq, dk, dv) = after_states(summary, weights, beside)
     lin_dk, lin_dv = last_call(lin_keys, lin_values, dk, dv, tail, after)

time: 161 us -> 154 us (0.957)
  the two profiles are of different devices: /device:TPU:32 before, /device:TPU:2 now
where the time goes in v3:
time: 154 us; the launch traced here: 152 us
  starting transfers between devices  66.7 us (43%)
  waiting for transfers between devices  42.7 us (28%)
  Pallas kernels  32.8 us (21%)
  local copies, waits for them, and re-layouts  7.18 us (5%)
  other arithmetic  1.91 us (1%)
    ppermute x6, starting transfers between devices, passed_along(): return lax.ppermute(block, 'ctx', route)  29.7 us
    all_to_all x3, starting transfers between devices, after_states(): lax.all_to_all(x, 'ctx', 0, 0, tiled=True, axis_index_groups=groups)  20.5 us
    all_to_all x3, waiting for transfers between devices, after_states(): lax.all_to_all(x, 'ctx', 0, 0, tiled=True, axis_index_groups=groups)  19.5 us
    all_to_all x1, waiting for transfers between devices, per_device(): lax.all_to_all(copies, 'head', 0, 0, tiled=True, axis_index_groups=same_c...  9.66 us
    pallas_call x1, Pallas kernels, softmax_call(): pl.pallas_call(functools.partial(softmax_kernel, length), out_shape=(jax....  8.9 us
    ppermute x6, waiting for transfers between devices, passed_along(): return lax.ppermute(block, 'ctx', route)  8.03 us
    all_to_all x1, waiting for transfers between devices, per_device(): stats = lax.all_to_all(stats, 'head', 0, 0, tiled=True)  5.53 us
    all_to_all x1, starting transfers between devices, per_device(): lax.all_to_all(pack_call(early, chips), 'head', 0, 0, tiled=True, axis_in...  4.59 us
  transfers between devices with their start and end apart: 14, of which 9 were waited for; matrix products, arithmetic and copies ran while one was open for 2% of the time, Pallas kernels for 13%

profile of v3, /device:TPU:2, one launch (start us, length us, event | category | flops | bytes accessed | tf_op | source)
XLA Modules:
  0.0 152.2 jit_solution(3366029256704792953)
XLA Ops:
  0.6 0.9 pad_maximum_fusion.kv0
  1.5 6.5 %collective-permute-start = (bf16[2,256,128]{2,1,0:T(8,128)(2,1)S(1)}, bf16[2,256,128]{2,1,0:T(8,128)(2,1)S(1)}, u32[]{:S(2)}, u32[]{:S(2)}) collective-permute-start(bf16[2,256,128]{2,1,0:T(8,128)(2,1)S(1)} %pad_maximum_fusion.kv0), channel_id=1, source_target_pairs={{0,24},{8,32},{16,40},{24,48},{32,56},{40,64},{48,72},{56,80},{64,... | collective-permute-start | bytes 393224 | tf_op jit(solution)/shard_map/ppermute | solution.py:457
  8.1 6.4 %collective-permute-start.1 = (bf16[2,256,128]{2,1,0:T(8,128)(2,1)S(1)}, bf16[2,256,128]{2,1,0:T(8,128)(2,1)S(1)}, u32[]{:S(2)}, u32[]{:S(2)}) collective-permute-start(bf16[2,256,128]{2,1,0:T(8,128)(2,1)S(1)} %pad_maximum_fusion.kv0), channel_id=1, source_target_pairs={{0,16},{8,24},{16,32},{24,40},{32,48},{40,56},{48,64},{56,72},{64,... | collective-permute-start | bytes 393224 | tf_op jit(solution)/shard_map/ppermute | solution.py:457
  14.5 3.8 %collective-permute-start.2 = (bf16[2,256,128]{2,1,0:T(8,128)(2,1)S(1)}, bf16[2,256,128]{2,1,0:T(8,128)(2,1)S(1)}, u32[]{:S(2)}, u32[]{:S(2)}) collective-permute-start(bf16[2,256,128]{2,1,0:T(8,128)(2,1)S(1)} %pad_maximum_fusion.kv0), channel_id=1, source_target_pairs={{0,8},{8,16},{16,24},{24,32},{32,40},{40,48},{48,56},{56,64},{64,7... | collective-permute-start | bytes 393224 | tf_op jit(solution)/shard_map/ppermute | solution.py:457
  18.3 2.7 %pack.1 = bf16[4,1024,256]{2,1,0:T(8,128)(2,1)} custom-call(bf16[2,4,1024,128]{3,2,1,0:T(8,128)(2,1)} %bitcast.13), custom_call_target="tpu_custom_call" | custom-call | bytes 4194304 | tf_op jit(solution)/shard_map/pack/pallas_call | solution.py:212
  21.0 4.6 %all-to-all-start = ((bf16[4,1024,256]{2,1,0:T(8,128)(2,1)}), bf16[4,1024,256]{2,1,0:T(8,128)(2,1)}, u32[]{:S(2)}, u32[]{:S(2)}) async-start(bf16[4,1024,256]{2,1,0:T(8,128)(2,1)} %pack.1), calls=%async_computation | async-start | bytes 4194304 | tf_op jit(solution)/shard_map/all_to_all | solution.py:479
  25.6 0.0 collective-permute-done.kv3
  25.6 2.9 %collective-permute-done.1.kv2 = bf16[2,256,128]{2,1,0:T(8,128)(2,1)S(1)} collective-permute-done((bf16[2,256,128]{2,1,0:T(8,128)(2,1)S(1)}, bf16[2,256,128]{2,1,0:T(8,128)(2,1)S(1)}, u32[]{:S(2)}, u32[]{:S(2)}) %collective-permute-start.1) | collective-permute-done | bytes 131104 | tf_op jit(solution)/shard_map/ppermute | solution.py:457
  28.5 2.0 %collective-permute-done.2.kv1 = bf16[2,256,128]{2,1,0:T(8,128)(2,1)S(1)} collective-permute-done((bf16[2,256,128]{2,1,0:T(8,128)(2,1)S(1)}, bf16[2,256,128]{2,1,0:T(8,128)(2,1)S(1)}, u32[]{:S(2)}, u32[]{:S(2)}) %collective-permute-start.2) | collective-permute-done | bytes 131104 | tf_op jit(solution)/shard_map/ppermute | solution.py:457
  30.5 8.9 %softmax_backward.1 = (bf16[256,1024]{1,0:T(8,128)(2,1)}, bf16[256,256]{1,0:T(8,128)(2,1)S(1)}, bf16[256,256]{1,0:T(8,128)(2,1)S(1)}, bf16[256,256]{1,0:T(8,128)(2,1)S(1)}, f32[256,256]{1,0:T(8,128)S(1)}) custom-call(s32[1]{0:T(128)S(6)} %mul.23.base_ref, s32[1,32]{1,0:T(1,128)S(1)} %bitcast.12, bf16[256,1024]{1,0:T(8,128)(2,1)} %q_ref.1, ...), custom_call_target="tpu_custom_call" | custom-call | flops 214748364800 | bytes 4194304 | tf_op jit(solution)/shard_map/softmax_backward/pallas_call | solution.py:127
  39.4 5.5 %collective-permute-start.3 = (bf16[256,256]{1,0:T(8,128)(2,1)S(1)}, bf16[256,256]{1,0:T(8,128)(2,1)S(1)}, u32[]{:S(2)}, u32[]{:S(2)}) collective-permute-start(bf16[256,256]{1,0:T(8,128)(2,1)S(1)} %get-tuple-element.41), channel_id=1, source_target_pairs={{24,0},{32,8},{40,16},{48,24},{56,32},{64,40},{72,48},{80,56},{88,... | collective-permute-start | bytes 393224 | tf_op jit(solution)/shard_map/ppermute | solution.py:457
  44.9 4.6 %collective-permute-start.4 = (bf16[256,256]{1,0:T(8,128)(2,1)S(1)}, bf16[256,256]{1,0:T(8,128)(2,1)S(1)}, u32[]{:S(2)}, u32[]{:S(2)}) collective-permute-start(bf16[256,256]{1,0:T(8,128)(2,1)S(1)} %get-tuple-element.42), channel_id=1, source_target_pairs={{16,0},{24,8},{32,16},{40,24},{48,32},{56,40},{64,48},{72,56},{80,... | collective-permute-start | bytes 393224 | tf_op jit(solution)/shard_map/ppermute | solution.py:457
  49.4 2.9 %collective-permute-start.5 = (bf16[256,256]{1,0:T(8,128)(2,1)S(1)}, bf16[256,256]{1,0:T(8,128)(2,1)S(1)}, u32[]{:S(2)}, u32[]{:S(2)}) collective-permute-start(bf16[256,256]{1,0:T(8,128)(2,1)S(1)} %get-tuple-element.43), channel_id=1, source_target_pairs={{8,0},{16,8},{24,16},{32,24},{40,32},{48,40},{56,48},{64,56},{72,6... | collective-permute-start | bytes 393224 | tf_op jit(solution)/shard_map/ppermute | solution.py:457
  52.4 4.0 %lightning_forward.1 = (f32[256,512]{1,0:T(8,128)}, bf16[256,512]{1,0:T(8,128)(2,1)}, bf16[256,512]{1,0:T(8,128)(2,1)}, f32[256,512]{1,0:T(8,128)}) custom-call(s32[1]{0:T(128)} %bitcast.block_ref, bf16[256,512]{1,0:T(8,128)(2,1)} %q_ref.3, bf16[256,512]{1,0:T(8,128)(2,1)} %k_ref.5, bf16[256,512]{1,0:T(8,128)(2,1)} %v_ref.5, f32[1,512]{1,0:T(1,128)} %bitcast.9, ...), custom_call_target="tpu_custom_call" | custom-call | flops 1342177280 | bytes 4194304 | tf_op jit(solution)/shard_map/lightning_forward/pallas_call | solution.py:185
  56.3 0.0 copy-start.2
  56.4 0.0 copy-start.3
  56.4 2.1 %collective-permute-start.6 = (bf16[256,512]{1,0:T(8,128)(2,1)}, bf16[256,512]{1,0:T(8,128)(2,1)S(1)}, u32[]{:S(2)}, u32[]{:S(2)}) collective-permute-start(bf16[256,512]{1,0:T(8,128)(2,1)} %get-tuple-element.46), channel_id=1, source_target_pairs={{0,1},{1,0},{2,3},{3,2},{4,5},{5,4},{6,7},{7,6},{8,9},{9,8},{10,11... | collective-permute-start | bytes 786440 | tf_op jit(solution)/shard_map/ppermute | solution.py:491
  58.4 0.0 collective-permute-done.3
  58.4 0.7 collective-permute-done.4
  59.1 2.5 %collective-permute-done.5 = bf16[256,256]{1,0:T(8,128)(2,1)S(1)} collective-permute-done((bf16[256,256]{1,0:T(8,128)(2,1)S(1)}, bf16[256,256]{1,0:T(8,128)(2,1)S(1)}, u32[]{:S(2)}, u32[]{:S(2)}) %collective-permute-start.5) | collective-permute-done | bytes 131104 | tf_op jit(solution)/shard_map/ppermute | solution.py:457
  61.6 0.1 add_convert_fusion
  61.7 0.0 collective-permute-done.6.sibling_ref
  61.7 0.8 broadcast_in_dim.48
  62.6 4.6 %all-to-all-start.1 = ((bf16[4,256,256]{2,1,0:T(8,128)(2,1)}), bf16[4,256,256]{2,1,0:T(8,128)(2,1)S(1)}, u32[]{:S(2)}, u32[]{:S(2)}) async-start(bf16[4,256,256]{2,1,0:T(8,128)(2,1)} %broadcast_in_dim.48), calls=%async_computation.1 | async-start | bytes 1048576 | tf_op jit(solution)/shard_map/all_to_all | solution.py:502
  67.1 9.7 %all-to-all-done.1.dkv_ref = bf16[4,256,256]{2,1,0:T(8,128)(2,1)S(1)} async-done(((bf16[4,256,256]{2,1,0:T(8,128)(2,1)}), bf16[4,256,256]{2,1,0:T(8,128)(2,1)S(1)}, u32[]{:S(2)}, u32[]{:S(2)}) %all-to-all-start.1) | async-done | bytes 524320 | tf_op jit(solution)/shard_map/all_to_all | solution.py:502
  76.8 4.6 %cotangent.1 = (f32[256,512]{1,0:T(8,128)S(1)}, f32[256,512]{1,0:T(8,128)S(1)}, f32[8,8,256]{2,1,0:T(8,128)}) custom-call(s32[1]{0:T(128)} %bitcast.6.core_ref, bf16[4,256,256]{2,1,0:T(8,128)(2,1)S(1)} %all-to-all-done.1.dkv_ref, bf16[4,1024,256]{2,1,0:T(8,128)(2,1)} %all-to-all-done.proj_ref, bf16[256,512]{1,0:T(8,128)(2,1)S(1)} %collective-permute-done.6.sibling_ref, ...), custom_call_target="tpu_custom_call" | custom-call | tf_op jit(solution)/shard_map/cotangent/pallas_call | solution.py:274
  81.4 0.8 copy-done.1
  82.2 1.9 %collective-permute-start.7 = (f32[256,512]{1,0:T(8,128)S(1)}, f32[256,512]{1,0:T(8,128)S(1)}, u32[]{:S(2)}, u32[]{:S(2)}) collective-permute-start(f32[256,512]{1,0:T(8,128)S(1)} %get-tuple-element.55), channel_id=1, source_target_pairs={{0,1},{1,0},{2,3},{3,2},{4,5},{5,4},{6,7},{7,6},{8,9},{9,8},{10,11... | collective-permute-start | bytes 1572872 | tf_op jit(solution)/shard_map/ppermute | solution.py:504
  84.2 0.1 iota_add_fusion
  84.2 3.4 %all-to-all-start.2 = ((f32[8,8,256]{2,1,0:T(8,128)}), f32[8,8,256]{2,1,0:T(8,128)S(1)}, u32[]{:S(2)}, u32[]{:S(2)}) async-start(f32[8,8,256]{2,1,0:T(8,128)} %get-tuple-element.53), calls=%async_computation.2 | async-start | bytes 131072 | tf_op jit(solution)/shard_map/all_to_all | solution.py:505
  87.6 5.5 %all-to-all-done.2.stats_ref = f32[8,8,256]{2,1,0:T(8,128)S(1)} async-done(((f32[8,8,256]{2,1,0:T(8,128)}), f32[8,8,256]{2,1,0:T(8,128)S(1)}, u32[]{:S(2)}, u32[]{:S(2)}) %all-to-all-start.2) | async-done | bytes 65568 | tf_op jit(solution)/shard_map/all_to_all | solution.py:505
  93.1 0.6 copy-done.9
  93.8 0.2 copy-done.6
  94.0 2.5 %dout_summary.1 = (bf16[256,512]{1,0:T(8,128)(2,1)}, bf16[4,128,128]{2,1,0:T(8,128)(2,1)}) custom-call(f32[8,8,256]{2,1,0:T(8,128)} %copy-done.9, f32[256,512]{1,0:T(8,128)} %copy-done.1, f32[256,512]{1,0:T(8,128)} %copy-done.6, f32[1,512]{1,0:T(1,128)} %bitcast.10, f32[256,512]{1,0:T(8,128)} %get-tuple-element.52.out_ref, ...), custom_call_target="tpu_custom_call" | custom-call | tf_op jit(solution)/shard_map/dout_summary/pallas_call | solution.py:309
  96.5 5.4 %all-to-all-start.3 = ((bf16[16,32,128]{2,1,0:T(8,128)(2,1)}), bf16[16,32,128]{2,1,0:T(8,128)(2,1)S(1)}, u32[]{:S(2)}, u32[]{:S(2)}) async-start(bf16[16,32,128]{2,1,0:T(8,128)(2,1)} %bitcast.15), calls=%async_computation.3 | async-start | bytes 262144 | tf_op jit(solution)/shard_map/all_to_all | solution.py:439
  101.9 0.1 add.66
  102.0 0.1 broadcast_in_dim.43
  102.0 0.1 reshape.88
  102.1 0.1 tile.17
  102.2 0.1 broadcast_in_dim.41
  102.3 0.1 reshape.86
  102.4 0.1 broadcast_in_dim.42
  102.5 0.1 reshape.87
  102.6 0.1 broadcast_in_dim.44
  102.6 0.1 reshape.89
  102.7 0.1 tile.19
  102.8 0.1 pad_add_fusion.1
  102.9 1.1 dynamic-slice_reduce_fusion
  104.1 0.1 reduce_sum.18
  104.2 0.1 select_reduce_fusion
  104.3 0.6 compare_select_fusion.weight_ref
  104.8 4.1 %all-to-all-done.3.blocks_ref = bf16[16,32,128]{2,1,0:T(8,128)(2,1)S(1)} async-done(((bf16[16,32,128]{2,1,0:T(8,128)(2,1)}), bf16[16,32,128]{2,1,0:T(8,128)(2,1)S(1)}, u32[]{:S(2)}, u32[]{:S(2)}) %all-to-all-start.3) | async-done | bytes 131104 | tf_op jit(solution)/shard_map/all_to_all | solution.py:439
  108.9 0.7 copy-done.5
  109.6 1.6 %rise.1 = bf16[4,4,32,128]{3,2,1,0:T(8,128)(2,1)} custom-call(f32[160]{0:T(256)} %compare_select_fusion.weight_ref, bf16[16,32,128]{2,1,0:T(8,128)(2,1)} %copy-done.5), custom_call_target="tpu_custom_call" | custom-call | tf_op jit(solution)/shard_map/rise/pallas_call | solution.py:442
  111.1 9.2 %all-to-all-start.4 = ((bf16[4,4,32,128]{3,2,1,0:T(8,128)(2,1)}), bf16[4,4,32,128]{3,2,1,0:T(8,128)(2,1)S(1)}, u32[]{:S(2)}, u32[]{:S(2)}) async-start(bf16[4,4,32,128]{3,2,1,0:T(8,128)(2,1)} %rise.1), calls=%async_computation.4 | async-start | bytes 262144 | tf_op jit(solution)/shard_map/all_to_all | solution.py:439
  120.4 4.1 %near_far.1 = (bf16[256,512]{1,0:T(8,128)(2,1)}, f32[256,512]{1,0:T(8,128)}, f32[256,512]{1,0:T(8,128)}) custom-call(s32[1]{0:T(128)} %bitcast.block_ref, bf16[256,512]{1,0:T(8,128)(2,1)} %q_ref.3, bf16[256,512]{1,0:T(8,128)(2,1)} %k_ref.5, bf16[256,512]{1,0:T(8,128)(2,1)} %v_ref.5, bf16[256,512]{1,0:T(8,128)(2,1)} %get-tuple-element.58.dout_ref, ...), custom_call_target="tpu_custom_call" | custom-call | flops 3489660928 | bytes 4194304 | tf_op jit(solution)/shard_map/near_far/pallas_call | solution.py:342
  124.5 9.1 %all-to-all-done.4.totals_ref = bf16[4,4,32,128]{3,2,1,0:T(8,128)(2,1)S(1)} async-done(((bf16[4,4,32,128]{3,2,1,0:T(8,128)(2,1)}), bf16[4,4,32,128]{3,2,1,0:T(8,128)(2,1)S(1)}, u32[]{:S(2)}, u32[]{:S(2)}) %all-to-all-start.4) | async-done | bytes 131104 | tf_op jit(solution)/shard_map/all_to_all | solution.py:439
  133.6 0.7 copy-done.7
  134.2 1.8 %after_states.1 = bf16[16,32,128]{2,1,0:T(8,128)(2,1)} custom-call(f32[160]{0:T(256)} %compare_select_fusion.weight_ref, bf16[16,32,128]{2,1,0:T(8,128)(2,1)} %copy-done.5, bf16[4,4,32,128]{3,2,1,0:T(8,128)(2,1)} %copy-done.7), custom_call_target="tpu_custom_call" | custom-call | tf_op jit(solution)/shard_map/after_states/pallas_call | solution.py:447
  136.0 5.9 %all-to-all-start.5 = ((bf16[16,32,128]{2,1,0:T(8,128)(2,1)}), bf16[16,32,128]{2,1,0:T(8,128)(2,1)S(1)}, u32[]{:S(2)}, u32[]{:S(2)}) async-start(bf16[16,32,128]{2,1,0:T(8,128)(2,1)} %after_states.1), calls=%async_computation.5 | async-start | bytes 262144 | tf_op jit(solution)/shard_map/all_to_all | solution.py:439
  141.9 0.7 fusion.1
  142.6 6.4 %all-to-all-done.5 = bf16[16,32,128]{2,1,0:T(8,128)(2,1)S(1)} async-done(((bf16[16,32,128]{2,1,0:T(8,128)(2,1)}), bf16[16,32,128]{2,1,0:T(8,128)(2,1)S(1)}, u32[]{:S(2)}, u32[]{:S(2)}) %all-to-all-start.5) | async-done | bytes 131104 | tf_op jit(solution)/shard_map/all_to_all | solution.py:439
  149.0 0.6 copy-done.8
  149.6 2.6 %last.1 = (bf16[256,512]{1,0:T(8,128)(2,1)}, bf16[256,512]{1,0:T(8,128)(2,1)}) custom-call(bf16[256,512]{1,0:T(8,128)(2,1)} %k_ref.5, bf16[256,512]{1,0:T(8,128)(2,1)} %v_ref.5, f32[256,512]{1,0:T(8,128)} %get-tuple-element.63.dk_ref, f32[256,512]{1,0:T(8,128)} %get-tuple-element.64.dv_ref, f32[256,512]{1,0:T(8,128)} %get-tuple-element.65.tail_ref, ...), custom_call_target="tpu_custom_call" | custom-call | tf_op jit(solution)/shard_map/last/pallas_call | solution.py:373
  (20 shorter events, 0.1 us)
Async XLA Ops:
  1.5 24.1 %collective-permute-start = (bf16[2,256,128]{2,1,0:T(8,128)(2,1)S(1)}, bf16[2,256,128]{2,1,0:T(8,128)(2,1)S(1)}, u32[]{:S(2)}, u32[]{:S(2)}) collective-permute-start(bf16[2,256,128]{2,1,0:T(8,128)(2,1)S(1)} %pad_maximum_fusion.kv0), channel_id=1, source_target_pairs={{0,24},{8,32},{16,40},{24,48},{32,56},{40,64},{48,72},{56,80},{64,... | collective-permute-start | bytes 393224 | tf_op jit(solution)/shard_map/ppermute | solution.py:457
  8.1 20.4 %collective-permute-start.1 = (bf16[2,256,128]{2,1,0:T(8,128)(2,1)S(1)}, bf16[2,256,128]{2,1,0:T(8,128)(2,1)S(1)}, u32[]{:S(2)}, u32[]{:S(2)}) collective-permute-start(bf16[2,256,128]{2,1,0:T(8,128)(2,1)S(1)} %pad_maximum_fusion.kv0), channel_id=1, source_target_pairs={{0,16},{8,24},{16,32},{24,40},{32,48},{40,56},{48,64},{56,72},{64,... | collective-permute-start | bytes 393224 | tf_op jit(solution)/shard_map/ppermute | solution.py:457
  14.5 16.0 %collective-permute-start.2 = (bf16[2,256,128]{2,1,0:T(8,128)(2,1)S(1)}, bf16[2,256,128]{2,1,0:T(8,128)(2,1)S(1)}, u32[]{:S(2)}, u32[]{:S(2)}) collective-permute-start(bf16[2,256,128]{2,1,0:T(8,128)(2,1)S(1)} %pad_maximum_fusion.kv0), channel_id=1, source_target_pairs={{0,8},{8,16},{16,24},{24,32},{32,40},{40,48},{48,56},{56,64},{64,7... | collective-permute-start | bytes 393224 | tf_op jit(solution)/shard_map/ppermute | solution.py:457
  21.0 9.4 %copy-start.4 = (s32[32]{0:T(128)S(1)}, s32[32]{0:T(128)}, u32[]{:S(2)}) copy-start(s32[32]{0:T(128)} %param.25) | copy-start | bytes 388
  21.0 40.7 %all-to-all-start = ((bf16[4,1024,256]{2,1,0:T(8,128)(2,1)}), bf16[4,1024,256]{2,1,0:T(8,128)(2,1)}, u32[]{:S(2)}, u32[]{:S(2)}) async-start(bf16[4,1024,256]{2,1,0:T(8,128)(2,1)} %pack.1), calls=%async_computation | async-start | bytes 4194304 | tf_op jit(solution)/shard_map/all_to_all | solution.py:479
  39.4 19.1 %collective-permute-start.3 = (bf16[256,256]{1,0:T(8,128)(2,1)S(1)}, bf16[256,256]{1,0:T(8,128)(2,1)S(1)}, u32[]{:S(2)}, u32[]{:S(2)}) collective-permute-start(bf16[256,256]{1,0:T(8,128)(2,1)S(1)} %get-tuple-element.41), channel_id=1, source_target_pairs={{24,0},{32,8},{40,16},{48,24},{56,32},{64,40},{72,48},{80,56},{88,... | collective-permute-start | bytes 393224 | tf_op jit(solution)/shard_map/ppermute | solution.py:457
  44.9 14.3 %collective-permute-start.4 = (bf16[256,256]{1,0:T(8,128)(2,1)S(1)}, bf16[256,256]{1,0:T(8,128)(2,1)S(1)}, u32[]{:S(2)}, u32[]{:S(2)}) collective-permute-start(bf16[256,256]{1,0:T(8,128)(2,1)S(1)} %get-tuple-element.42), channel_id=1, source_target_pairs={{16,0},{24,8},{32,16},{40,24},{48,32},{56,40},{64,48},{72,56},{80,... | collective-permute-start | bytes 393224 | tf_op jit(solution)/shard_map/ppermute | solution.py:457
  49.4 12.2 %collective-permute-start.5 = (bf16[256,256]{1,0:T(8,128)(2,1)S(1)}, bf16[256,256]{1,0:T(8,128)(2,1)S(1)}, u32[]{:S(2)}, u32[]{:S(2)}) collective-permute-start(bf16[256,256]{1,0:T(8,128)(2,1)S(1)} %get-tuple-element.43), channel_id=1, source_target_pairs={{8,0},{16,8},{24,16},{32,24},{40,32},{48,40},{56,48},{64,56},{72,6... | collective-permute-start | bytes 393224 | tf_op jit(solution)/shard_map/ppermute | solution.py:457
  56.3 20.5 %copy-start = (f32[256,512]{1,0:T(8,128)S(1)}, f32[256,512]{1,0:T(8,128)}, u32[]{:S(2)}) copy-start(f32[256,512]{1,0:T(8,128)} %get-tuple-element.52.out_ref) | copy-start | bytes 1572868
  56.3 20.5 %copy-start.2 = (bf16[256,512]{1,0:T(8,128)(2,1)S(1)}, bf16[256,512]{1,0:T(8,128)(2,1)}, u32[]{:S(2)}) copy-start(bf16[256,512]{1,0:T(8,128)(2,1)} %grad_ref.1) | copy-start | bytes 786436
  56.4 20.5 %copy-start.3 = (f32[512]{0:T(512)S(1)}, f32[512]{0:T(512)}, u32[]{:S(2)}) copy-start(f32[512]{0:T(512)} %param.17) | copy-start | bytes 6148
  56.4 5.3 %collective-permute-start.6 = (bf16[256,512]{1,0:T(8,128)(2,1)}, bf16[256,512]{1,0:T(8,128)(2,1)S(1)}, u32[]{:S(2)}, u32[]{:S(2)}) collective-permute-start(bf16[256,512]{1,0:T(8,128)(2,1)} %get-tuple-element.46), channel_id=1, source_target_pairs={{0,1},{1,0},{2,3},{3,2},{4,5},{5,4},{6,7},{7,6},{8,9},{9,8},{10,11... | collective-permute-start | bytes 786440 | tf_op jit(solution)/shard_map/ppermute | solution.py:491
  62.6 14.2 %all-to-all-start.1 = ((bf16[4,256,256]{2,1,0:T(8,128)(2,1)}), bf16[4,256,256]{2,1,0:T(8,128)(2,1)S(1)}, u32[]{:S(2)}, u32[]{:S(2)}) async-start(bf16[4,256,256]{2,1,0:T(8,128)(2,1)} %broadcast_in_dim.48), calls=%async_computation.1 | async-start | bytes 1048576 | tf_op jit(solution)/shard_map/all_to_all | solution.py:502
  81.4 0.8 copy-start.1
  82.2 10.9 %collective-permute-start.7 = (f32[256,512]{1,0:T(8,128)S(1)}, f32[256,512]{1,0:T(8,128)S(1)}, u32[]{:S(2)}, u32[]{:S(2)}) collective-permute-start(f32[256,512]{1,0:T(8,128)S(1)} %get-tuple-element.55), channel_id=1, source_target_pairs={{0,1},{1,0},{2,3},{3,2},{4,5},{5,4},{6,7},{7,6},{8,9},{9,8},{10,11... | collective-permute-start | bytes 1572872 | tf_op jit(solution)/shard_map/ppermute | solution.py:504
  84.2 8.9 %all-to-all-start.2 = ((f32[8,8,256]{2,1,0:T(8,128)}), f32[8,8,256]{2,1,0:T(8,128)S(1)}, u32[]{:S(2)}, u32[]{:S(2)}) async-start(f32[8,8,256]{2,1,0:T(8,128)} %get-tuple-element.53), calls=%async_computation.2 | async-start | bytes 131072 | tf_op jit(solution)/shard_map/all_to_all | solution.py:505
  93.1 0.6 copy-start.9
  93.1 0.8 copy-start.6
  96.5 12.4 %all-to-all-start.3 = ((bf16[16,32,128]{2,1,0:T(8,128)(2,1)}), bf16[16,32,128]{2,1,0:T(8,128)(2,1)S(1)}, u32[]{:S(2)}, u32[]{:S(2)}) async-start(bf16[16,32,128]{2,1,0:T(8,128)(2,1)} %bitcast.15), calls=%async_computation.3 | async-start | bytes 262144 | tf_op jit(solution)/shard_map/all_to_all | solution.py:439
  108.9 0.7 copy-start.5
  111.1 22.4 %all-to-all-start.4 = ((bf16[4,4,32,128]{3,2,1,0:T(8,128)(2,1)}), bf16[4,4,32,128]{3,2,1,0:T(8,128)(2,1)S(1)}, u32[]{:S(2)}, u32[]{:S(2)}) async-start(bf16[4,4,32,128]{3,2,1,0:T(8,128)(2,1)} %rise.1), calls=%async_computation.4 | async-start | bytes 262144 | tf_op jit(solution)/shard_map/all_to_all | solution.py:439
  133.6 0.7 copy-start.7
  136.0 13.0 %all-to-all-start.5 = ((bf16[16,32,128]{2,1,0:T(8,128)(2,1)}), bf16[16,32,128]{2,1,0:T(8,128)(2,1)S(1)}, u32[]{:S(2)}, u32[]{:S(2)}) async-start(bf16[16,32,128]{2,1,0:T(8,128)(2,1)} %after_states.1), calls=%async_computation.5 | async-start | bytes 262144 | tf_op jit(solution)/shard_map/all_to_all | solution.py:439
  149.0 0.6 copy-start.8

commit v4 on v3

--- a/solution.py
+++ b/solution.py
@@ -220,7 +220,7 @@
     )(projections.reshape(2, chips, rows, DH))
 
 
-PARTS = 2
+PARTS = 1
 
 
 def cotangent_kernel(
@@ -475,9 +475,11 @@
 
     stacked = jnp.stack([soft_keys, soft_values])
     stacked, early = lax.optimization_barrier((stacked, projections))
-    kv3, kv2, kv1 = (passed_along(stacked, offset) for offset in (3, 2, 1))
+    kv2, kv1 = (passed_along(stacked, offset) for offset in (2, 1))
+    kv2, packed = lax.optimization_barrier((kv2, pack_call(early, chips)))
+    kv3 = passed_along(kv2, 1)
     proj = lax.all_to_all(
-        pack_call(early, chips), "head", 0, 0, tiled=True, axis_index_groups=same_core
+        packed, "head", 0, 0, tiled=True, axis_index_groups=same_core
     )
     soft_query = pltpu.with_memory_space_constraint(soft_query, pltpu.HBM)
     soft_grad = pltpu.with_memory_space_constraint(soft_grad, pltpu.HBM)
@@ -492,13 +494,13 @@
     summed = own
     for offset, part in ((3, part3), (2, part2), (1, part1)):
         summed = summed + passed_along(part, -offset).astype(F32)
-    dkv, lin_out, gained, proj, late_decay = lax.optimization_barrier(
-        (summed.astype(BF16), lin_out, gained, proj, log_decay)
+    dkv = summed.astype(BF16)
+    copies, lin_out, gained, proj, late_decay = lax.optimization_barrier(
+        (jnp.broadcast_to(dkv[None], (chips,) + dkv.shape), lin_out, gained, proj, log_decay)
     )
     weights = state_weights(late_decay, length, device)
     soft_dk, soft_dv = dkv[:, :DH], dkv[:, DH:]
 
-    copies = jnp.broadcast_to(dkv[None], (chips,) + dkv.shape)
     dkv_all = lax.all_to_all(copies, "head", 0, 0, tiled=True, axis_index_groups=same_core)
     gated, carried, stats = cotangent_call(core, dkv_all, proj, gained, lin_grad, gain, lin_out)
     carried = lax.ppermute(carried, "head", sibling)

time: 154 us -> 148 us (0.961)
  starting transfers between devices: 66.7 us -> 61.7 us
    ppermute x6, starting transfers between devices: 29.7 us -> 26.2 us  [passed_along(): return lax.ppermute(block, 'ctx', route)]
  transfers between devices with their start and end apart: 14 -> 14, of which waited for: 9 -> 8; matrix products, arithmetic and copies ran while one was open for 2% -> 3% of each run, Pallas kernels for 13% -> 13%
where the time goes in v4:
time: 148 us; the launch traced here: 146 us
  starting transfers between devices  61.7 us (42%)
  waiting for transfers between devices  43.2 us (29%)
  Pallas kernels  31.6 us (21%)
  local copies, waits for them, and re-layouts  7.18 us (5%)
  other arithmetic  1.91 us (1%)
    ppermute x6, starting transfers between devices, passed_along(): return lax.ppermute(block, 'ctx', route)  26.2 us
    all_to_all x3, waiting for transfers between devices, after_states(): lax.all_to_all(x, 'ctx', 0, 0, tiled=True, axis_index_groups=groups)  19.5 us
    all_to_all x3, starting transfers between devices, after_states(): lax.all_to_all(x, 'ctx', 0, 0, tiled=True, axis_index_groups=groups)  19.3 us
    all_to_all x1, waiting for transfers between devices, per_device(): lax.all_to_all(copies, 'head', 0, 0, tiled=True, axis_index_groups=same_c...  9.66 us
    pallas_call x1, Pallas kernels, softmax_call(): pl.pallas_call(functools.partial(softmax_kernel, length), out_shape=(jax....  8.9 us
    ppermute x6, waiting for transfers between devices, passed_along(): return lax.ppermute(block, 'ctx', route)  8.51 us
    all_to_all x1, waiting for transfers between devices, per_device(): stats = lax.all_to_all(stats, 'head', 0, 0, tiled=True)  5.53 us
    all_to_all x1, starting transfers between devices, per_device(): lax.all_to_all(packed, 'head', 0, 0, tiled=True, axis_index_groups=same_c...  4.48 us
  transfers between devices with their start and end apart: 14, of which 8 were waited for; matrix products, arithmetic and copies ran while one was open for 3% of the time, Pallas kernels for 13%

profile of v4, /device:TPU:2, one launch (start us, length us, event | category | flops | bytes accessed | tf_op | source)
XLA Modules:
  0.0 146.5 jit_solution(16619568864291835707)
XLA Ops:
  0.6 0.9 pad_maximum_fusion.kv0
  1.5 5.2 %collective-permute-start = (bf16[2,256,128]{2,1,0:T(8,128)(2,1)S(1)}, bf16[2,256,128]{2,1,0:T(8,128)(2,1)S(1)}, u32[]{:S(2)}, u32[]{:S(2)}) collective-permute-start(bf16[2,256,128]{2,1,0:T(8,128)(2,1)S(1)} %pad_maximum_fusion.kv0), channel_id=1, source_target_pairs={{0,16},{8,24},{16,32},{24,40},{32,48},{40,56},{48,64},{56,72},{64,... | collective-permute-start | bytes 393224 | tf_op jit(solution)/shard_map/ppermute | solution.py:457
  6.7 3.8 %collective-permute-start.2 = (bf16[2,256,128]{2,1,0:T(8,128)(2,1)S(1)}, bf16[2,256,128]{2,1,0:T(8,128)(2,1)S(1)}, u32[]{:S(2)}, u32[]{:S(2)}) collective-permute-start(bf16[2,256,128]{2,1,0:T(8,128)(2,1)S(1)} %pad_maximum_fusion.kv0), channel_id=1, source_target_pairs={{0,8},{8,16},{16,24},{24,32},{32,40},{40,48},{48,56},{56,64},{64,7... | collective-permute-start | bytes 393224 | tf_op jit(solution)/shard_map/ppermute | solution.py:457
  10.5 2.7 %pack.1 = bf16[4,1024,256]{2,1,0:T(8,128)(2,1)} custom-call(bf16[2,4,1024,128]{3,2,1,0:T(8,128)(2,1)} %bitcast.13), custom_call_target="tpu_custom_call" | custom-call | bytes 4194304 | tf_op jit(solution)/shard_map/pack/pallas_call | solution.py:212
  13.3 5.4 %collective-permute-done.kv2 = bf16[2,256,128]{2,1,0:T(8,128)(2,1)S(1)} collective-permute-done((bf16[2,256,128]{2,1,0:T(8,128)(2,1)S(1)}, bf16[2,256,128]{2,1,0:T(8,128)(2,1)S(1)}, u32[]{:S(2)}, u32[]{:S(2)}) %collective-permute-start) | collective-permute-done | bytes 131104 | tf_op jit(solution)/shard_map/ppermute | solution.py:457
  18.7 4.4 %collective-permute-start.1 = (bf16[2,256,128]{2,1,0:T(8,128)(2,1)S(1)}, bf16[2,256,128]{2,1,0:T(8,128)(2,1)S(1)}, u32[]{:S(2)}, u32[]{:S(2)}) collective-permute-start(bf16[2,256,128]{2,1,0:T(8,128)(2,1)S(1)} %collective-permute-done.kv2), channel_id=1, source_target_pairs={{0,8},{8,16},{16,24},{24,32},{32,40},{40,48},{48,56},{56,64},{64,7... | collective-permute-start | bytes 393224 | tf_op jit(solution)/shard_map/ppermute | solution.py:457
  23.1 0.0 copy-start.4
  23.1 4.5 %all-to-all-start = ((bf16[4,1024,256]{2,1,0:T(8,128)(2,1)}), bf16[4,1024,256]{2,1,0:T(8,128)(2,1)}, u32[]{:S(2)}, u32[]{:S(2)}) async-start(bf16[4,1024,256]{2,1,0:T(8,128)(2,1)} %pack.1), calls=%async_computation | async-start | bytes 4194304 | tf_op jit(solution)/shard_map/all_to_all | solution.py:481
  27.6 0.0 collective-permute-done.1.kv3
  27.6 8.9 %softmax_backward.1 = (bf16[256,1024]{1,0:T(8,128)(2,1)}, bf16[256,256]{1,0:T(8,128)(2,1)S(1)}, bf16[256,256]{1,0:T(8,128)(2,1)S(1)}, bf16[256,256]{1,0:T(8,128)(2,1)S(1)}, f32[256,256]{1,0:T(8,128)S(1)}) custom-call(s32[1]{0:T(128)S(6)} %mul.23.base_ref, s32[1,32]{1,0:T(1,128)S(1)} %bitcast.12, bf16[256,1024]{1,0:T(8,128)(2,1)} %q_ref.1, ...), custom_call_target="tpu_custom_call" | custom-call | flops 214748364800 | bytes 4194304 | tf_op jit(solution)/shard_map/softmax_backward/pallas_call | solution.py:127
  36.5 5.4 %collective-permute-start.3 = (bf16[256,256]{1,0:T(8,128)(2,1)S(1)}, bf16[256,256]{1,0:T(8,128)(2,1)S(1)}, u32[]{:S(2)}, u32[]{:S(2)}) collective-permute-start(bf16[256,256]{1,0:T(8,128)(2,1)S(1)} %get-tuple-element.45), channel_id=1, source_target_pairs={{24,0},{32,8},{40,16},{48,24},{56,32},{64,40},{72,48},{80,56},{88,... | collective-permute-start | bytes 393224 | tf_op jit(solution)/shard_map/ppermute | solution.py:457
  42.0 5.4 %collective-permute-start.4 = (bf16[256,256]{1,0:T(8,128)(2,1)S(1)}, bf16[256,256]{1,0:T(8,128)(2,1)S(1)}, u32[]{:S(2)}, u32[]{:S(2)}) collective-permute-start(bf16[256,256]{1,0:T(8,128)(2,1)S(1)} %get-tuple-element.46), channel_id=1, source_target_pairs={{16,0},{24,8},{32,16},{40,24},{48,32},{56,40},{64,48},{72,56},{80,... | collective-permute-start | bytes 393224 | tf_op jit(solution)/shard_map/ppermute | solution.py:457
  47.4 1.9 %collective-permute-start.5 = (bf16[256,256]{1,0:T(8,128)(2,1)S(1)}, bf16[256,256]{1,0:T(8,128)(2,1)S(1)}, u32[]{:S(2)}, u32[]{:S(2)}) collective-permute-start(bf16[256,256]{1,0:T(8,128)(2,1)S(1)} %get-tuple-element.47), channel_id=1, source_target_pairs={{8,0},{16,8},{24,16},{32,24},{40,32},{48,40},{56,48},{64,56},{72,6... | collective-permute-start | bytes 393224 | tf_op jit(solution)/shard_map/ppermute | solution.py:457
  49.3 4.0 %lightning_forward.1 = (f32[256,512]{1,0:T(8,128)}, bf16[256,512]{1,0:T(8,128)(2,1)}, bf16[256,512]{1,0:T(8,128)(2,1)}, f32[256,512]{1,0:T(8,128)}) custom-call(s32[1]{0:T(128)} %bitcast.block_ref, bf16[256,512]{1,0:T(8,128)(2,1)} %q_ref.3, bf16[256,512]{1,0:T(8,128)(2,1)} %k_ref.5, bf16[256,512]{1,0:T(8,128)(2,1)} %v_ref.5, f32[1,512]{1,0:T(1,128)} %bitcast.9, ...), custom_call_target="tpu_custom_call" | custom-call | flops 1342177280 | bytes 4194304 | tf_op jit(solution)/shard_map/lightning_forward/pallas_call | solution.py:185
  53.3 0.0 copy-start.2
  53.3 0.0 copy-start.3
  53.3 2.1 %collective-permute-start.6 = (bf16[256,512]{1,0:T(8,128)(2,1)}, bf16[256,512]{1,0:T(8,128)(2,1)S(1)}, u32[]{:S(2)}, u32[]{:S(2)}) collective-permute-start(bf16[256,512]{1,0:T(8,128)(2,1)} %get-tuple-element.50), channel_id=1, source_target_pairs={{0,1},{1,0},{2,3},{3,2},{4,5},{5,4},{6,7},{7,6},{8,9},{9,8},{10,11... | collective-permute-start | bytes 786440 | tf_op jit(solution)/shard_map/ppermute | solution.py:493
  55.4 0.0 collective-permute-done.3
  55.4 0.3 collective-permute-done.4
  55.7 2.8 %collective-permute-done.5 = bf16[256,256]{1,0:T(8,128)(2,1)S(1)} collective-permute-done((bf16[256,256]{1,0:T(8,128)(2,1)S(1)}, bf16[256,256]{1,0:T(8,128)(2,1)S(1)}, u32[]{:S(2)}, u32[]{:S(2)}) %collective-permute-start.5) | collective-permute-done | bytes 131104 | tf_op jit(solution)/shard_map/ppermute | solution.py:457
  58.5 0.1 add_convert_fusion
  58.5 0.0 collective-permute-done.6.sibling_ref
  58.5 0.8 broadcast_in_dim.45
  59.4 4.4 %all-to-all-start.1 = ((bf16[4,256,256]{2,1,0:T(8,128)(2,1)}), bf16[4,256,256]{2,1,0:T(8,128)(2,1)S(1)}, u32[]{:S(2)}, u32[]{:S(2)}) async-start(bf16[4,256,256]{2,1,0:T(8,128)(2,1)} %broadcast_in_dim.45), calls=%async_computation.1 | async-start | bytes 1048576 | tf_op jit(solution)/shard_map/all_to_all | solution.py:504
  63.8 9.7 %all-to-all-done.1.dkv_ref = bf16[4,256,256]{2,1,0:T(8,128)(2,1)S(1)} async-done(((bf16[4,256,256]{2,1,0:T(8,128)(2,1)}), bf16[4,256,256]{2,1,0:T(8,128)(2,1)S(1)}, u32[]{:S(2)}, u32[]{:S(2)}) %all-to-all-start.1) | async-done | bytes 524320 | tf_op jit(solution)/shard_map/all_to_all | solution.py:504
  73.5 3.3 %cotangent.1 = (f32[256,512]{1,0:T(8,128)S(1)}, f32[256,512]{1,0:T(8,128)S(1)}, f32[8,8,256]{2,1,0:T(8,128)}) custom-call(s32[1]{0:T(128)} %bitcast.6.core_ref, bf16[4,256,256]{2,1,0:T(8,128)(2,1)S(1)} %all-to-all-done.1.dkv_ref, bf16[4,1024,256]{2,1,0:T(8,128)(2,1)} %all-to-all-done.proj_ref, bf16[256,512]{1,0:T(8,128)(2,1)S(1)} %collective-permute-done.6.sibling_ref, ...), custom_call_target="tpu_custom_call" | custom-call | tf_op jit(solution)/shard_map/cotangent/pallas_call | solution.py:274
  76.8 0.8 copy-done.1
  77.6 1.9 %collective-permute-start.7 = (f32[256,512]{1,0:T(8,128)S(1)}, f32[256,512]{1,0:T(8,128)S(1)}, u32[]{:S(2)}, u32[]{:S(2)}) collective-permute-start(f32[256,512]{1,0:T(8,128)S(1)} %get-tuple-element.59), channel_id=1, source_target_pairs={{0,1},{1,0},{2,3},{3,2},{4,5},{5,4},{6,7},{7,6},{8,9},{9,8},{10,11... | collective-permute-start | bytes 1572872 | tf_op jit(solution)/shard_map/ppermute | solution.py:506
  79.6 0.1 iota_add_fusion
  79.6 3.4 %all-to-all-start.2 = ((f32[8,8,256]{2,1,0:T(8,128)}), f32[8,8,256]{2,1,0:T(8,128)S(1)}, u32[]{:S(2)}, u32[]{:S(2)}) async-start(f32[8,8,256]{2,1,0:T(8,128)} %get-tuple-element.57), calls=%async_computation.2 | async-start | bytes 131072 | tf_op jit(solution)/shard_map/all_to_all | solution.py:507
  83.0 5.5 %all-to-all-done.2.stats_ref = f32[8,8,256]{2,1,0:T(8,128)S(1)} async-done(((f32[8,8,256]{2,1,0:T(8,128)}), f32[8,8,256]{2,1,0:T(8,128)S(1)}, u32[]{:S(2)}, u32[]{:S(2)}) %all-to-all-start.2) | async-done | bytes 65568 | tf_op jit(solution)/shard_map/all_to_all | solution.py:507
  88.5 0.6 copy-done.9
  89.2 0.2 copy-done.6
  89.4 2.5 %dout_summary.1 = (bf16[256,512]{1,0:T(8,128)(2,1)}, bf16[4,128,128]{2,1,0:T(8,128)(2,1)}) custom-call(f32[8,8,256]{2,1,0:T(8,128)} %copy-done.9, f32[256,512]{1,0:T(8,128)} %copy-done.1, f32[256,512]{1,0:T(8,128)} %copy-done.6, f32[1,512]{1,0:T(1,128)} %bitcast.10, f32[256,512]{1,0:T(8,128)} %get-tuple-element.56.out_ref, ...), custom_call_target="tpu_custom_call" | custom-call | tf_op jit(solution)/shard_map/dout_summary/pallas_call | solution.py:309
  91.9 5.4 %all-to-all-start.3 = ((bf16[16,32,128]{2,1,0:T(8,128)(2,1)}), bf16[16,32,128]{2,1,0:T(8,128)(2,1)S(1)}, u32[]{:S(2)}, u32[]{:S(2)}) async-start(bf16[16,32,128]{2,1,0:T(8,128)(2,1)} %bitcast.15), calls=%async_computation.3 | async-start | bytes 262144 | tf_op jit(solution)/shard_map/all_to_all | solution.py:439
  97.3 0.1 add.66
  97.4 0.1 broadcast_in_dim.42
  97.4 0.1 reshape.87
  97.5 0.1 tile.19
  97.6 0.1 broadcast_in_dim.44
  97.7 0.1 reshape.89
  97.8 0.1 broadcast_in_dim.41
  97.8 0.1 reshape.86
  97.9 0.1 tile.17
  98.0 0.1 broadcast_in_dim.43
  98.1 0.1 reshape.88
  98.2 0.1 pad_add_fusion.1
  98.3 1.1 dynamic-slice_reduce_fusion
  99.5 0.1 reduce_sum.18
  99.6 0.1 select_reduce_fusion
  99.7 0.6 compare_select_fusion.weight_ref
  100.2 4.1 %all-to-all-done.3.blocks_ref = bf16[16,32,128]{2,1,0:T(8,128)(2,1)S(1)} async-done(((bf16[16,32,128]{2,1,0:T(8,128)(2,1)}), bf16[16,32,128]{2,1,0:T(8,128)(2,1)S(1)}, u32[]{:S(2)}, u32[]{:S(2)}) %all-to-all-start.3) | async-done | bytes 131104 | tf_op jit(solution)/shard_map/all_to_all | solution.py:439
  104.3 0.7 copy-done.5
  105.0 1.6 %rise.1 = bf16[4,4,32,128]{3,2,1,0:T(8,128)(2,1)} custom-call(f32[160]{0:T(256)} %compare_select_fusion.weight_ref, bf16[16,32,128]{2,1,0:T(8,128)(2,1)} %copy-done.5), custom_call_target="tpu_custom_call" | custom-call | tf_op jit(solution)/shard_map/rise/pallas_call | solution.py:442
  106.5 8.0 %all-to-all-start.4 = ((bf16[4,4,32,128]{3,2,1,0:T(8,128)(2,1)}), bf16[4,4,32,128]{3,2,1,0:T(8,128)(2,1)S(1)}, u32[]{:S(2)}, u32[]{:S(2)}) async-start(bf16[4,4,32,128]{3,2,1,0:T(8,128)(2,1)} %rise.1), calls=%async_computation.4 | async-start | bytes 262144 | tf_op jit(solution)/shard_map/all_to_all | solution.py:439
  114.6 4.1 %near_far.1 = (bf16[256,512]{1,0:T(8,128)(2,1)}, f32[256,512]{1,0:T(8,128)}, f32[256,512]{1,0:T(8,128)}) custom-call(s32[1]{0:T(128)} %bitcast.block_ref, bf16[256,512]{1,0:T(8,128)(2,1)} %q_ref.3, bf16[256,512]{1,0:T(8,128)(2,1)} %k_ref.5, bf16[256,512]{1,0:T(8,128)(2,1)} %v_ref.5, bf16[256,512]{1,0:T(8,128)(2,1)} %get-tuple-element.62.dout_ref, ...), custom_call_target="tpu_custom_call" | custom-call | flops 3489660928 | bytes 4194304 | tf_op jit(solution)/shard_map/near_far/pallas_call | solution.py:342
  118.7 9.1 %all-to-all-done.4.totals_ref = bf16[4,4,32,128]{3,2,1,0:T(8,128)(2,1)S(1)} async-done(((bf16[4,4,32,128]{3,2,1,0:T(8,128)(2,1)}), bf16[4,4,32,128]{3,2,1,0:T(8,128)(2,1)S(1)}, u32[]{:S(2)}, u32[]{:S(2)}) %all-to-all-start.4) | async-done | bytes 131104 | tf_op jit(solution)/shard_map/all_to_all | solution.py:439
  127.8 0.7 copy-done.7
  128.4 1.8 %after_states.1 = bf16[16,32,128]{2,1,0:T(8,128)(2,1)} custom-call(f32[160]{0:T(256)} %compare_select_fusion.weight_ref, bf16[16,32,128]{2,1,0:T(8,128)(2,1)} %copy-done.5, bf16[4,4,32,128]{3,2,1,0:T(8,128)(2,1)} %copy-done.7), custom_call_target="tpu_custom_call" | custom-call | tf_op jit(solution)/shard_map/after_states/pallas_call | solution.py:447
  130.2 5.9 %all-to-all-start.5 = ((bf16[16,32,128]{2,1,0:T(8,128)(2,1)}), bf16[16,32,128]{2,1,0:T(8,128)(2,1)S(1)}, u32[]{:S(2)}, u32[]{:S(2)}) async-start(bf16[16,32,128]{2,1,0:T(8,128)(2,1)} %after_states.1), calls=%async_computation.5 | async-start | bytes 262144 | tf_op jit(solution)/shard_map/all_to_all | solution.py:439
  136.2 0.7 fusion.1
  136.8 6.4 %all-to-all-done.5 = bf16[16,32,128]{2,1,0:T(8,128)(2,1)S(1)} async-done(((bf16[16,32,128]{2,1,0:T(8,128)(2,1)}), bf16[16,32,128]{2,1,0:T(8,128)(2,1)S(1)}, u32[]{:S(2)}, u32[]{:S(2)}) %all-to-all-start.5) | async-done | bytes 131104 | tf_op jit(solution)/shard_map/all_to_all | solution.py:439
  143.2 0.6 copy-done.8
  143.8 2.6 %last.1 = (bf16[256,512]{1,0:T(8,128)(2,1)}, bf16[256,512]{1,0:T(8,128)(2,1)}) custom-call(bf16[256,512]{1,0:T(8,128)(2,1)} %k_ref.5, bf16[256,512]{1,0:T(8,128)(2,1)} %v_ref.5, f32[256,512]{1,0:T(8,128)} %get-tuple-element.67.dk_ref, f32[256,512]{1,0:T(8,128)} %get-tuple-element.68.dv_ref, f32[256,512]{1,0:T(8,128)} %get-tuple-element.69.tail_ref, ...), custom_call_target="tpu_custom_call" | custom-call | tf_op jit(solution)/shard_map/last/pallas_call | solution.py:373
  (20 shorter events, 0.1 us)
Async XLA Ops:
  1.5 17.2 %collective-permute-start = (bf16[2,256,128]{2,1,0:T(8,128)(2,1)S(1)}, bf16[2,256,128]{2,1,0:T(8,128)(2,1)S(1)}, u32[]{:S(2)}, u32[]{:S(2)}) collective-permute-start(bf16[2,256,128]{2,1,0:T(8,128)(2,1)S(1)} %pad_maximum_fusion.kv0), channel_id=1, source_target_pairs={{0,16},{8,24},{16,32},{24,40},{32,48},{40,56},{48,64},{56,72},{64,... | collective-permute-start | bytes 393224 | tf_op jit(solution)/shard_map/ppermute | solution.py:457
  6.7 20.9 %collective-permute-start.2 = (bf16[2,256,128]{2,1,0:T(8,128)(2,1)S(1)}, bf16[2,256,128]{2,1,0:T(8,128)(2,1)S(1)}, u32[]{:S(2)}, u32[]{:S(2)}) collective-permute-start(bf16[2,256,128]{2,1,0:T(8,128)(2,1)S(1)} %pad_maximum_fusion.kv0), channel_id=1, source_target_pairs={{0,8},{8,16},{16,24},{24,32},{32,40},{40,48},{48,56},{56,64},{64,7... | collective-permute-start | bytes 393224 | tf_op jit(solution)/shard_map/ppermute | solution.py:457
  18.7 9.0 %collective-permute-start.1 = (bf16[2,256,128]{2,1,0:T(8,128)(2,1)S(1)}, bf16[2,256,128]{2,1,0:T(8,128)(2,1)S(1)}, u32[]{:S(2)}, u32[]{:S(2)}) collective-permute-start(bf16[2,256,128]{2,1,0:T(8,128)(2,1)S(1)} %collective-permute-done.kv2), channel_id=1, source_target_pairs={{0,8},{8,16},{16,24},{24,32},{32,40},{40,48},{48,56},{56,64},{64,7... | collective-permute-start | bytes 393224 | tf_op jit(solution)/shard_map/ppermute | solution.py:457
  23.1 4.6 %copy-start.4 = (s32[32]{0:T(128)S(1)}, s32[32]{0:T(128)}, u32[]{:S(2)}) copy-start(s32[32]{0:T(128)} %param.25) | copy-start | bytes 388
  23.1 35.4 %all-to-all-start = ((bf16[4,1024,256]{2,1,0:T(8,128)(2,1)}), bf16[4,1024,256]{2,1,0:T(8,128)(2,1)}, u32[]{:S(2)}, u32[]{:S(2)}) async-start(bf16[4,1024,256]{2,1,0:T(8,128)(2,1)} %pack.1), calls=%async_computation | async-start | bytes 4194304 | tf_op jit(solution)/shard_map/all_to_all | solution.py:481
  36.5 18.9 %collective-permute-start.3 = (bf16[256,256]{1,0:T(8,128)(2,1)S(1)}, bf16[256,256]{1,0:T(8,128)(2,1)S(1)}, u32[]{:S(2)}, u32[]{:S(2)}) collective-permute-start(bf16[256,256]{1,0:T(8,128)(2,1)S(1)} %get-tuple-element.45), channel_id=1, source_target_pairs={{24,0},{32,8},{40,16},{48,24},{56,32},{64,40},{72,48},{80,56},{88,... | collective-permute-start | bytes 393224 | tf_op jit(solution)/shard_map/ppermute | solution.py:457
  42.0 13.7 %collective-permute-start.4 = (bf16[256,256]{1,0:T(8,128)(2,1)S(1)}, bf16[256,256]{1,0:T(8,128)(2,1)S(1)}, u32[]{:S(2)}, u32[]{:S(2)}) collective-permute-start(bf16[256,256]{1,0:T(8,128)(2,1)S(1)} %get-tuple-element.46), channel_id=1, source_target_pairs={{16,0},{24,8},{32,16},{40,24},{48,32},{56,40},{64,48},{72,56},{80,... | collective-permute-start | bytes 393224 | tf_op jit(solution)/shard_map/ppermute | solution.py:457
  47.4 11.1 %collective-permute-start.5 = (bf16[256,256]{1,0:T(8,128)(2,1)S(1)}, bf16[256,256]{1,0:T(8,128)(2,1)S(1)}, u32[]{:S(2)}, u32[]{:S(2)}) collective-permute-start(bf16[256,256]{1,0:T(8,128)(2,1)S(1)} %get-tuple-element.47), channel_id=1, source_target_pairs={{8,0},{16,8},{24,16},{32,24},{40,32},{48,40},{56,48},{64,56},{72,6... | collective-permute-start | bytes 393224 | tf_op jit(solution)/shard_map/ppermute | solution.py:457
  53.3 20.2 %copy-start = (f32[256,512]{1,0:T(8,128)S(1)}, f32[256,512]{1,0:T(8,128)}, u32[]{:S(2)}) copy-start(f32[256,512]{1,0:T(8,128)} %get-tuple-element.56.out_ref) | copy-start | bytes 1572868
  53.3 20.2 %copy-start.2 = (bf16[256,512]{1,0:T(8,128)(2,1)S(1)}, bf16[256,512]{1,0:T(8,128)(2,1)}, u32[]{:S(2)}) copy-start(bf16[256,512]{1,0:T(8,128)(2,1)} %grad_ref.1) | copy-start | bytes 786436
  53.3 20.2 %copy-start.3 = (f32[512]{0:T(512)S(1)}, f32[512]{0:T(512)}, u32[]{:S(2)}) copy-start(f32[512]{0:T(512)} %param.17) | copy-start | bytes 6148
  53.3 5.2 %collective-permute-start.6 = (bf16[256,512]{1,0:T(8,128)(2,1)}, bf16[256,512]{1,0:T(8,128)(2,1)S(1)}, u32[]{:S(2)}, u32[]{:S(2)}) collective-permute-start(bf16[256,512]{1,0:T(8,128)(2,1)} %get-tuple-element.50), channel_id=1, source_target_pairs={{0,1},{1,0},{2,3},{3,2},{4,5},{5,4},{6,7},{7,6},{8,9},{9,8},{10,11... | collective-permute-start | bytes 786440 | tf_op jit(solution)/shard_map/ppermute | solution.py:493
  59.4 14.1 %all-to-all-start.1 = ((bf16[4,256,256]{2,1,0:T(8,128)(2,1)}), bf16[4,256,256]{2,1,0:T(8,128)(2,1)S(1)}, u32[]{:S(2)}, u32[]{:S(2)}) async-start(bf16[4,256,256]{2,1,0:T(8,128)(2,1)} %broadcast_in_dim.45), calls=%async_computation.1 | async-start | bytes 1048576 | tf_op jit(solution)/shard_map/all_to_all | solution.py:504
  76.8 0.8 copy-start.1
  77.6 10.9 %collective-permute-start.7 = (f32[256,512]{1,0:T(8,128)S(1)}, f32[256,512]{1,0:T(8,128)S(1)}, u32[]{:S(2)}, u32[]{:S(2)}) collective-permute-start(f32[256,512]{1,0:T(8,128)S(1)} %get-tuple-element.59), channel_id=1, source_target_pairs={{0,1},{1,0},{2,3},{3,2},{4,5},{5,4},{6,7},{7,6},{8,9},{9,8},{10,11... | collective-permute-start | bytes 1572872 | tf_op jit(solution)/shard_map/ppermute | solution.py:506
  79.6 8.9 %all-to-all-start.2 = ((f32[8,8,256]{2,1,0:T(8,128)}), f32[8,8,256]{2,1,0:T(8,128)S(1)}, u32[]{:S(2)}, u32[]{:S(2)}) async-start(f32[8,8,256]{2,1,0:T(8,128)} %get-tuple-element.57), calls=%async_computation.2 | async-start | bytes 131072 | tf_op jit(solution)/shard_map/all_to_all | solution.py:507
  88.5 0.6 copy-start.9
  88.5 0.8 copy-start.6
  91.9 12.4 %all-to-all-start.3 = ((bf16[16,32,128]{2,1,0:T(8,128)(2,1)}), bf16[16,32,128]{2,1,0:T(8,128)(2,1)S(1)}, u32[]{:S(2)}, u32[]{:S(2)}) async-start(bf16[16,32,128]{2,1,0:T(8,128)(2,1)} %bitcast.15), calls=%async_computation.3 | async-start | bytes 262144 | tf_op jit(solution)/shard_map/all_to_all | solution.py:439
  104.3 0.7 copy-start.5
  106.5 21.2 %all-to-all-start.4 = ((bf16[4,4,32,128]{3,2,1,0:T(8,128)(2,1)}), bf16[4,4,32,128]{3,2,1,0:T(8,128)(2,1)S(1)}, u32[]{:S(2)}, u32[]{:S(2)}) async-start(bf16[4,4,32,128]{3,2,1,0:T(8,128)(2,1)} %rise.1), calls=%async_computation.4 | async-start | bytes 262144 | tf_op jit(solution)/shard_map/all_to_all | solution.py:439
  127.8 0.7 copy-start.7
  130.2 13.0 %all-to-all-start.5 = ((bf16[16,32,128]{2,1,0:T(8,128)(2,1)}), bf16[16,32,128]{2,1,0:T(8,128)(2,1)S(1)}, u32[]{:S(2)}, u32[]{:S(2)}) async-start(bf16[16,32,128]{2,1,0:T(8,128)(2,1)} %after_states.1), calls=%async_computation.5 | async-start | bytes 262144 | tf_op jit(solution)/shard_map/all_to_all | solution.py:439
  143.2 0.6 copy-start.8

commit v5 on v4

--- a/solution.py
+++ b/solution.py
@@ -486,19 +486,20 @@
     soft_dq, part3, part2, part1, own = softmax_call(
         block * length, doc_lengths.reshape(1, -1), soft_query, soft_grad, [kv3, kv2, kv1, stacked]
     )
-    lin_query, own = lax.optimization_barrier((lin_query, own))
+    beyond = passed_along(part3, -1)
+    part1 = passed_along(part1, -1)
+    part2 = (part2.astype(F32) + beyond.astype(F32)).astype(BF16)
+    part2, lin_query = lax.optimization_barrier((part2, lin_query))
+    part2 = passed_along(part2, -2)
     lin_out, gained, scaled, tail = forward_call(
         block, lin_query, lin_keys, lin_values, gain, log_decay, state_in
     )
-    gained = lax.ppermute(gained, "head", sibling)
-    summed = own
-    for offset, part in ((3, part3), (2, part2), (1, part1)):
-        summed = summed + passed_along(part, -offset).astype(F32)
-    dkv = summed.astype(BF16)
+    dkv = (own + part1.astype(F32) + part2.astype(F32)).astype(BF16)
     copies, lin_out, gained, proj, late_decay = lax.optimization_barrier(
         (jnp.broadcast_to(dkv[None], (chips,) + dkv.shape), lin_out, gained, proj, log_decay)
     )
     weights = state_weights(late_decay, length, device)
+    gained = lax.ppermute(gained, "head", sibling)
     soft_dk, soft_dv = dkv[:, :DH], dkv[:, DH:]
 
     dkv_all = lax.all_to_all(copies, "head", 0, 0, tiled=True, axis_index_groups=same_core)

time: 148 us -> 145 us (0.980)
  waiting for transfers between devices: 43.2 us -> 37.3 us
  starting transfers between devices: 61.7 us -> 64.3 us
    all_to_all x1, waiting for transfers between devices: 9.66 us -> 4.66 us  [per_device(): lax.all_to_all(copies, 'head', 0, 0, tiled=True, axis_index_groups=same_c...]
    all_to_all x3, starting transfers between devices: 19.3 us -> 22.4 us  [after_states(): lax.all_to_all(x, 'ctx', 0, 0, tiled=True, axis_index_groups=groups)]
    ppermute x6, waiting for transfers between devices: 8.51 us -> 6.12 us  [passed_along(): return lax.ppermute(block, 'ctx', route)]
    ppermute x1, waiting for transfers between devices: 0.01 us -> 1.49 us  [per_device(): gained = lax.ppermute(gained, 'head', sibling)]
    unnamed x20 -> x22, local copies, waits for them, and re-layouts: 3.62 us -> 3.62 us
  transfers between devices with their start and end apart: 14 -> 14, of which waited for: 8 -> 9; matrix products, arithmetic and copies ran while one was open for 3% -> 3% of each run, Pallas kernels for 13% -> 14%
where the time goes in v5:
time: 145 us; the launch traced here: 143 us
  starting transfers between devices  64.3 us (44%)
  waiting for transfers between devices  37.3 us (26%)
  Pallas kernels  31.6 us (22%)
  local copies, waits for them, and re-layouts  7.18 us (5%)
  other arithmetic  1.93 us (1%)
    ppermute x6, starting transfers between devices, passed_along(): return lax.ppermute(block, 'ctx', route)  25.6 us
    all_to_all x3, starting transfers between devices, after_states(): lax.all_to_all(x, 'ctx', 0, 0, tiled=True, axis_index_groups=groups)  22.4 us
    all_to_all x3, waiting for transfers between devices, after_states(): lax.all_to_all(x, 'ctx', 0, 0, tiled=True, axis_index_groups=groups)  19.5 us
    pallas_call x1, Pallas kernels, softmax_call(): pl.pallas_call(functools.partial(softmax_kernel, length), out_shape=(jax....  8.9 us
    ppermute x6, waiting for transfers between devices, passed_along(): return lax.ppermute(block, 'ctx', route)  6.12 us
    all_to_all x1, waiting for transfers between devices, per_device(): stats = lax.all_to_all(stats, 'head', 0, 0, tiled=True)  5.53 us
    all_to_all x1, starting transfers between devices, per_device(): lax.all_to_all(copies, 'head', 0, 0, tiled=True, axis_index_groups=same_c...  4.7 us
    all_to_all x1, waiting for transfers between devices, per_device(): lax.all_to_all(copies, 'head', 0, 0, tiled=True, axis_index_groups=same_c...  4.66 us
  transfers between devices with their start and end apart: 14, of which 9 were waited for; matrix products, arithmetic and copies ran while one was open for 3% of the time, Pallas kernels for 14%

profile of v5, /device:TPU:2, one launch (start us, length us, event | category | flops | bytes accessed | tf_op | source)
XLA Modules:
  0.0 143.2 jit_solution(1480840383568311900)
XLA Ops:
  0.6 0.9 pad_maximum_fusion.kv0
  1.5 5.2 %collective-permute-start = (bf16[2,256,128]{2,1,0:T(8,128)(2,1)S(1)}, bf16[2,256,128]{2,1,0:T(8,128)(2,1)S(1)}, u32[]{:S(2)}, u32[]{:S(2)}) collective-permute-start(bf16[2,256,128]{2,1,0:T(8,128)(2,1)S(1)} %pad_maximum_fusion.kv0), channel_id=1, source_target_pairs={{0,16},{8,24},{16,32},{24,40},{32,48},{40,56},{48,64},{56,72},{64,... | collective-permute-start | bytes 393224 | tf_op jit(solution)/shard_map/ppermute | solution.py:457
  6.7 3.8 %collective-permute-start.2 = (bf16[2,256,128]{2,1,0:T(8,128)(2,1)S(1)}, bf16[2,256,128]{2,1,0:T(8,128)(2,1)S(1)}, u32[]{:S(2)}, u32[]{:S(2)}) collective-permute-start(bf16[2,256,128]{2,1,0:T(8,128)(2,1)S(1)} %pad_maximum_fusion.kv0), channel_id=1, source_target_pairs={{0,8},{8,16},{16,24},{24,32},{32,40},{40,48},{48,56},{56,64},{64,7... | collective-permute-start | bytes 393224 | tf_op jit(solution)/shard_map/ppermute | solution.py:457
  10.5 2.7 %pack.1 = bf16[4,1024,256]{2,1,0:T(8,128)(2,1)} custom-call(bf16[2,4,1024,128]{3,2,1,0:T(8,128)(2,1)} %bitcast.13), custom_call_target="tpu_custom_call" | custom-call | bytes 4194304 | tf_op jit(solution)/shard_map/pack/pallas_call | solution.py:212
  13.3 5.4 %collective-permute-done.kv2 = bf16[2,256,128]{2,1,0:T(8,128)(2,1)S(1)} collective-permute-done((bf16[2,256,128]{2,1,0:T(8,128)(2,1)S(1)}, bf16[2,256,128]{2,1,0:T(8,128)(2,1)S(1)}, u32[]{:S(2)}, u32[]{:S(2)}) %collective-permute-start) | collective-permute-done | bytes 131104 | tf_op jit(solution)/shard_map/ppermute | solution.py:457
  18.7 4.4 %collective-permute-start.1 = (bf16[2,256,128]{2,1,0:T(8,128)(2,1)S(1)}, bf16[2,256,128]{2,1,0:T(8,128)(2,1)S(1)}, u32[]{:S(2)}, u32[]{:S(2)}) collective-permute-start(bf16[2,256,128]{2,1,0:T(8,128)(2,1)S(1)} %collective-permute-done.kv2), channel_id=1, source_target_pairs={{0,8},{8,16},{16,24},{24,32},{32,40},{40,48},{48,56},{56,64},{64,7... | collective-permute-start | bytes 393224 | tf_op jit(solution)/shard_map/ppermute | solution.py:457
  23.1 0.0 copy-start.4
  23.1 4.5 %all-to-all-start = ((bf16[4,1024,256]{2,1,0:T(8,128)(2,1)}), bf16[4,1024,256]{2,1,0:T(8,128)(2,1)}, u32[]{:S(2)}, u32[]{:S(2)}) async-start(bf16[4,1024,256]{2,1,0:T(8,128)(2,1)} %pack.1), calls=%async_computation | async-start | bytes 4194304 | tf_op jit(solution)/shard_map/all_to_all | solution.py:481
  27.6 0.0 collective-permute-done.1.kv3
  27.6 8.9 %softmax_backward.1 = (bf16[256,1024]{1,0:T(8,128)(2,1)}, bf16[256,256]{1,0:T(8,128)(2,1)S(1)}, bf16[256,256]{1,0:T(8,128)(2,1)S(1)}, bf16[256,256]{1,0:T(8,128)(2,1)S(1)}, f32[256,256]{1,0:T(8,128)S(1)}) custom-call(s32[1]{0:T(128)S(6)} %mul.23.base_ref, s32[1,32]{1,0:T(1,128)S(1)} %bitcast.12, bf16[256,1024]{1,0:T(8,128)(2,1)} %q_ref.1, ...), custom_call_target="tpu_custom_call" | custom-call | flops 214748364800 | bytes 4194304 | tf_op jit(solution)/shard_map/softmax_backward/pallas_call | solution.py:127
  36.5 3.5 %collective-permute-start.4 = (bf16[256,256]{1,0:T(8,128)(2,1)S(1)}, bf16[256,256]{1,0:T(8,128)(2,1)S(1)}, u32[]{:S(2)}, u32[]{:S(2)}) collective-permute-start(bf16[256,256]{1,0:T(8,128)(2,1)S(1)} %get-tuple-element.46), channel_id=1, source_target_pairs={{8,0},{16,8},{24,16},{32,24},{40,32},{48,40},{56,48},{64,56},{72,6... | collective-permute-start | bytes 393224 | tf_op jit(solution)/shard_map/ppermute | solution.py:457
  40.1 3.5 %collective-permute-start.3 = (bf16[256,256]{1,0:T(8,128)(2,1)S(1)}, bf16[256,256]{1,0:T(8,128)(2,1)S(1)}, u32[]{:S(2)}, u32[]{:S(2)}) collective-permute-start(bf16[256,256]{1,0:T(8,128)(2,1)S(1)} %get-tuple-element.44), channel_id=1, source_target_pairs={{8,0},{16,8},{24,16},{32,24},{40,32},{48,40},{56,48},{64,56},{72,6... | collective-permute-start | bytes 393224 | tf_op jit(solution)/shard_map/ppermute | solution.py:457
  43.6 0.3 collective-permute-done.4
  44.0 5.1 %collective-permute-start.5 = (bf16[256,256]{1,0:T(8,128)(2,1)S(1)}, bf16[256,256]{1,0:T(8,128)(2,1)S(1)}, u32[]{:S(2)}, u32[]{:S(2)}) collective-permute-start(bf16[256,256]{1,0:T(8,128)(2,1)S(1)} %add_convert_fusion.1), channel_id=1, source_target_pairs={{16,0},{24,8},{32,16},{40,24},{48,32},{56,40},{64,48},{72,56},{80,... | collective-permute-start | bytes 393224 | tf_op jit(solution)/shard_map/ppermute | solution.py:457
  49.1 4.0 %lightning_forward.1 = (f32[256,512]{1,0:T(8,128)}, bf16[256,512]{1,0:T(8,128)(2,1)}, bf16[256,512]{1,0:T(8,128)(2,1)}, f32[256,512]{1,0:T(8,128)}) custom-call(s32[1]{0:T(128)} %bitcast.block_ref, bf16[256,512]{1,0:T(8,128)(2,1)} %q_ref.3, bf16[256,512]{1,0:T(8,128)(2,1)} %k_ref.5, bf16[256,512]{1,0:T(8,128)(2,1)} %v_ref.5, f32[1,512]{1,0:T(1,128)} %bitcast.9, ...), custom_call_target="tpu_custom_call" | custom-call | flops 1342177280 | bytes 4194304 | tf_op jit(solution)/shard_map/lightning_forward/pallas_call | solution.py:185
  53.1 0.0 copy-start.2
  53.1 0.0 copy-start.3
  53.1 0.0 collective-permute-done.3
  53.1 0.4 collective-permute-done.5
  53.5 0.1 add_convert_fusion
  53.6 0.8 broadcast_in_dim.45
  54.4 4.7 %all-to-all-start.1 = ((bf16[4,256,256]{2,1,0:T(8,128)(2,1)}), bf16[4,256,256]{2,1,0:T(8,128)(2,1)S(1)}, u32[]{:S(2)}, u32[]{:S(2)}) async-start(bf16[4,256,256]{2,1,0:T(8,128)(2,1)} %broadcast_in_dim.45), calls=%async_computation.1 | async-start | bytes 1048576 | tf_op jit(solution)/shard_map/all_to_all | solution.py:505
  59.1 1.9 %collective-permute-start.6 = (bf16[256,512]{1,0:T(8,128)(2,1)S(1)}, bf16[256,512]{1,0:T(8,128)(2,1)S(1)}, u32[]{:S(2)}, u32[]{:S(2)}) collective-permute-start(bf16[256,512]{1,0:T(8,128)(2,1)S(1)} %copy-done.10), channel_id=1, source_target_pairs={{0,1},{1,0},{2,3},{3,2},{4,5},{5,4},{6,7},{7,6},{8,9},{9,8},{10,11... | collective-permute-start | bytes 786440 | tf_op jit(solution)/shard_map/ppermute | solution.py:502
  61.0 1.5 %collective-permute-done.6.sibling_ref = bf16[256,512]{1,0:T(8,128)(2,1)S(1)} collective-permute-done((bf16[256,512]{1,0:T(8,128)(2,1)S(1)}, bf16[256,512]{1,0:T(8,128)(2,1)S(1)}, u32[]{:S(2)}, u32[]{:S(2)}) %collective-permute-start.6) | collective-permute-done | bytes 262176 | tf_op jit(solution)/shard_map/ppermute | solution.py:502
  62.5 4.7 %all-to-all-done.1.dkv_ref = bf16[4,256,256]{2,1,0:T(8,128)(2,1)S(1)} async-done(((bf16[4,256,256]{2,1,0:T(8,128)(2,1)}), bf16[4,256,256]{2,1,0:T(8,128)(2,1)S(1)}, u32[]{:S(2)}, u32[]{:S(2)}) %all-to-all-start.1) | async-done | bytes 524320 | tf_op jit(solution)/shard_map/all_to_all | solution.py:505
  67.2 3.3 %cotangent.1 = (f32[256,512]{1,0:T(8,128)S(1)}, f32[256,512]{1,0:T(8,128)S(1)}, f32[8,8,256]{2,1,0:T(8,128)}) custom-call(s32[1]{0:T(128)} %bitcast.6.core_ref, bf16[4,256,256]{2,1,0:T(8,128)(2,1)S(1)} %all-to-all-done.1.dkv_ref, bf16[4,1024,256]{2,1,0:T(8,128)(2,1)} %all-to-all-done.proj_ref, bf16[256,512]{1,0:T(8,128)(2,1)S(1)} %collective-permute-done.6.sibling_ref, ...), custom_call_target="tpu_custom_call" | custom-call | tf_op jit(solution)/shard_map/cotangent/pallas_call | solution.py:274
  70.5 0.8 copy-done.1
  71.3 1.9 %collective-permute-start.7 = (f32[256,512]{1,0:T(8,128)S(1)}, f32[256,512]{1,0:T(8,128)S(1)}, u32[]{:S(2)}, u32[]{:S(2)}) collective-permute-start(f32[256,512]{1,0:T(8,128)S(1)} %get-tuple-element.59), channel_id=1, source_target_pairs={{0,1},{1,0},{2,3},{3,2},{4,5},{5,4},{6,7},{7,6},{8,9},{9,8},{10,11... | collective-permute-start | bytes 1572872 | tf_op jit(solution)/shard_map/ppermute | solution.py:507
  73.3 0.1 iota_add_fusion
  73.4 3.4 %all-to-all-start.2 = ((f32[8,8,256]{2,1,0:T(8,128)}), f32[8,8,256]{2,1,0:T(8,128)S(1)}, u32[]{:S(2)}, u32[]{:S(2)}) async-start(f32[8,8,256]{2,1,0:T(8,128)} %get-tuple-element.57), calls=%async_computation.2 | async-start | bytes 131072 | tf_op jit(solution)/shard_map/all_to_all | solution.py:508
  76.7 5.5 %all-to-all-done.2.stats_ref = f32[8,8,256]{2,1,0:T(8,128)S(1)} async-done(((f32[8,8,256]{2,1,0:T(8,128)}), f32[8,8,256]{2,1,0:T(8,128)S(1)}, u32[]{:S(2)}, u32[]{:S(2)}) %all-to-all-start.2) | async-done | bytes 65568 | tf_op jit(solution)/shard_map/all_to_all | solution.py:508
  82.3 0.6 copy-done.9
  82.9 0.2 copy-done.6
  83.1 2.5 %dout_summary.1 = (bf16[256,512]{1,0:T(8,128)(2,1)}, bf16[4,128,128]{2,1,0:T(8,128)(2,1)}) custom-call(f32[8,8,256]{2,1,0:T(8,128)} %copy-done.9, f32[256,512]{1,0:T(8,128)} %copy-done.1, f32[256,512]{1,0:T(8,128)} %copy-done.6, f32[1,512]{1,0:T(1,128)} %bitcast.10, f32[256,512]{1,0:T(8,128)} %get-tuple-element.56.out_ref, ...), custom_call_target="tpu_custom_call" | custom-call | tf_op jit(solution)/shard_map/dout_summary/pallas_call | solution.py:309
  85.6 7.1 %all-to-all-start.3 = ((bf16[16,32,128]{2,1,0:T(8,128)(2,1)}), bf16[16,32,128]{2,1,0:T(8,128)(2,1)S(1)}, u32[]{:S(2)}, u32[]{:S(2)}) async-start(bf16[16,32,128]{2,1,0:T(8,128)(2,1)} %bitcast.15), calls=%async_computation.3 | async-start | bytes 262144 | tf_op jit(solution)/shard_map/all_to_all | solution.py:439
  92.8 0.1 add.66
  92.8 0.1 broadcast_in_dim.42
  92.9 0.1 reshape.87
  93.0 0.1 tile.19
  93.1 0.1 broadcast_in_dim.44
  93.2 0.1 reshape.89
  93.2 0.1 broadcast_in_dim.41
  93.3 0.1 reshape.86
  93.4 0.1 tile.17
  93.5 0.1 broadcast_in_dim.43
  93.6 0.1 reshape.88
  93.7 0.1 pad_add_fusion.1
  93.7 1.1 dynamic-slice_reduce_fusion
  94.9 0.1 reduce_sum.18
  95.0 0.1 select_reduce_fusion
  95.1 0.6 compare_select_fusion.weight_ref
  95.7 4.1 %all-to-all-done.3.blocks_ref = bf16[16,32,128]{2,1,0:T(8,128)(2,1)S(1)} async-done(((bf16[16,32,128]{2,1,0:T(8,128)(2,1)}), bf16[16,32,128]{2,1,0:T(8,128)(2,1)S(1)}, u32[]{:S(2)}, u32[]{:S(2)}) %all-to-all-start.3) | async-done | bytes 131104 | tf_op jit(solution)/shard_map/all_to_all | solution.py:439
  99.8 0.7 copy-done.5
  100.4 1.6 %rise.1 = bf16[4,4,32,128]{3,2,1,0:T(8,128)(2,1)} custom-call(f32[160]{0:T(256)} %compare_select_fusion.weight_ref, bf16[16,32,128]{2,1,0:T(8,128)(2,1)} %copy-done.5), custom_call_target="tpu_custom_call" | custom-call | tf_op jit(solution)/shard_map/rise/pallas_call | solution.py:442
  102.0 9.3 %all-to-all-start.4 = ((bf16[4,4,32,128]{3,2,1,0:T(8,128)(2,1)}), bf16[4,4,32,128]{3,2,1,0:T(8,128)(2,1)S(1)}, u32[]{:S(2)}, u32[]{:S(2)}) async-start(bf16[4,4,32,128]{3,2,1,0:T(8,128)(2,1)} %rise.1), calls=%async_computation.4 | async-start | bytes 262144 | tf_op jit(solution)/shard_map/all_to_all | solution.py:439
  111.4 4.2 %near_far.1 = (bf16[256,512]{1,0:T(8,128)(2,1)}, f32[256,512]{1,0:T(8,128)}, f32[256,512]{1,0:T(8,128)}) custom-call(s32[1]{0:T(128)} %bitcast.block_ref, bf16[256,512]{1,0:T(8,128)(2,1)} %q_ref.3, bf16[256,512]{1,0:T(8,128)(2,1)} %k_ref.5, bf16[256,512]{1,0:T(8,128)(2,1)} %v_ref.5, bf16[256,512]{1,0:T(8,128)(2,1)} %get-tuple-element.62.dout_ref, ...), custom_call_target="tpu_custom_call" | custom-call | flops 3489660928 | bytes 4194304 | tf_op jit(solution)/shard_map/near_far/pallas_call | solution.py:342
  115.5 9.0 %all-to-all-done.4.totals_ref = bf16[4,4,32,128]{3,2,1,0:T(8,128)(2,1)S(1)} async-done(((bf16[4,4,32,128]{3,2,1,0:T(8,128)(2,1)}), bf16[4,4,32,128]{3,2,1,0:T(8,128)(2,1)S(1)}, u32[]{:S(2)}, u32[]{:S(2)}) %all-to-all-start.4) | async-done | bytes 131104 | tf_op jit(solution)/shard_map/all_to_all | solution.py:439
  124.6 0.7 copy-done.7
  125.2 1.8 %after_states.1 = bf16[16,32,128]{2,1,0:T(8,128)(2,1)} custom-call(f32[160]{0:T(256)} %compare_select_fusion.weight_ref, bf16[16,32,128]{2,1,0:T(8,128)(2,1)} %copy-done.5, bf16[4,4,32,128]{3,2,1,0:T(8,128)(2,1)} %copy-done.7), custom_call_target="tpu_custom_call" | custom-call | tf_op jit(solution)/shard_map/after_states/pallas_call | solution.py:447
  127.0 5.9 %all-to-all-start.5 = ((bf16[16,32,128]{2,1,0:T(8,128)(2,1)}), bf16[16,32,128]{2,1,0:T(8,128)(2,1)S(1)}, u32[]{:S(2)}, u32[]{:S(2)}) async-start(bf16[16,32,128]{2,1,0:T(8,128)(2,1)} %after_states.1), calls=%async_computation.5 | async-start | bytes 262144 | tf_op jit(solution)/shard_map/all_to_all | solution.py:439
  132.9 0.7 fusion.1
  133.6 6.4 %all-to-all-done.5 = bf16[16,32,128]{2,1,0:T(8,128)(2,1)S(1)} async-done(((bf16[16,32,128]{2,1,0:T(8,128)(2,1)}), bf16[16,32,128]{2,1,0:T(8,128)(2,1)S(1)}, u32[]{:S(2)}, u32[]{:S(2)}) %all-to-all-start.5) | async-done | bytes 131104 | tf_op jit(solution)/shard_map/all_to_all | solution.py:439
  140.0 0.6 copy-done.8
  140.6 2.6 %last.1 = (bf16[256,512]{1,0:T(8,128)(2,1)}, bf16[256,512]{1,0:T(8,128)(2,1)}) custom-call(bf16[256,512]{1,0:T(8,128)(2,1)} %k_ref.5, bf16[256,512]{1,0:T(8,128)(2,1)} %v_ref.5, f32[256,512]{1,0:T(8,128)} %get-tuple-element.67.dk_ref, f32[256,512]{1,0:T(8,128)} %get-tuple-element.68.dv_ref, f32[256,512]{1,0:T(8,128)} %get-tuple-element.69.tail_ref, ...), custom_call_target="tpu_custom_call" | custom-call | tf_op jit(solution)/shard_map/last/pallas_call | solution.py:373
  (23 shorter events, 0.1 us)
Async XLA Ops:
  1.5 17.2 %collective-permute-start = (bf16[2,256,128]{2,1,0:T(8,128)(2,1)S(1)}, bf16[2,256,128]{2,1,0:T(8,128)(2,1)S(1)}, u32[]{:S(2)}, u32[]{:S(2)}) collective-permute-start(bf16[2,256,128]{2,1,0:T(8,128)(2,1)S(1)} %pad_maximum_fusion.kv0), channel_id=1, source_target_pairs={{0,16},{8,24},{16,32},{24,40},{32,48},{40,56},{48,64},{56,72},{64,... | collective-permute-start | bytes 393224 | tf_op jit(solution)/shard_map/ppermute | solution.py:457
  6.7 20.9 %collective-permute-start.2 = (bf16[2,256,128]{2,1,0:T(8,128)(2,1)S(1)}, bf16[2,256,128]{2,1,0:T(8,128)(2,1)S(1)}, u32[]{:S(2)}, u32[]{:S(2)}) collective-permute-start(bf16[2,256,128]{2,1,0:T(8,128)(2,1)S(1)} %pad_maximum_fusion.kv0), channel_id=1, source_target_pairs={{0,8},{8,16},{16,24},{24,32},{32,40},{40,48},{48,56},{56,64},{64,7... | collective-permute-start | bytes 393224 | tf_op jit(solution)/shard_map/ppermute | solution.py:457
  18.7 9.0 %collective-permute-start.1 = (bf16[2,256,128]{2,1,0:T(8,128)(2,1)S(1)}, bf16[2,256,128]{2,1,0:T(8,128)(2,1)S(1)}, u32[]{:S(2)}, u32[]{:S(2)}) collective-permute-start(bf16[2,256,128]{2,1,0:T(8,128)(2,1)S(1)} %collective-permute-done.kv2), channel_id=1, source_target_pairs={{0,8},{8,16},{16,24},{24,32},{32,40},{40,48},{48,56},{56,64},{64,7... | collective-permute-start | bytes 393224 | tf_op jit(solution)/shard_map/ppermute | solution.py:457
  23.1 4.5 %copy-start.4 = (s32[32]{0:T(128)S(1)}, s32[32]{0:T(128)}, u32[]{:S(2)}) copy-start(s32[32]{0:T(128)} %param.25) | copy-start | bytes 388
  23.1 30.5 %all-to-all-start = ((bf16[4,1024,256]{2,1,0:T(8,128)(2,1)}), bf16[4,1024,256]{2,1,0:T(8,128)(2,1)}, u32[]{:S(2)}, u32[]{:S(2)}) async-start(bf16[4,1024,256]{2,1,0:T(8,128)(2,1)} %pack.1), calls=%async_computation | async-start | bytes 4194304 | tf_op jit(solution)/shard_map/all_to_all | solution.py:481
  36.5 7.4 %collective-permute-start.4 = (bf16[256,256]{1,0:T(8,128)(2,1)S(1)}, bf16[256,256]{1,0:T(8,128)(2,1)S(1)}, u32[]{:S(2)}, u32[]{:S(2)}) collective-permute-start(bf16[256,256]{1,0:T(8,128)(2,1)S(1)} %get-tuple-element.46), channel_id=1, source_target_pairs={{8,0},{16,8},{24,16},{32,24},{40,32},{48,40},{56,48},{64,56},{72,6... | collective-permute-start | bytes 393224 | tf_op jit(solution)/shard_map/ppermute | solution.py:457
  40.1 13.1 %collective-permute-start.3 = (bf16[256,256]{1,0:T(8,128)(2,1)S(1)}, bf16[256,256]{1,0:T(8,128)(2,1)S(1)}, u32[]{:S(2)}, u32[]{:S(2)}) collective-permute-start(bf16[256,256]{1,0:T(8,128)(2,1)S(1)} %get-tuple-element.44), channel_id=1, source_target_pairs={{8,0},{16,8},{24,16},{32,24},{40,32},{48,40},{56,48},{64,56},{72,6... | collective-permute-start | bytes 393224 | tf_op jit(solution)/shard_map/ppermute | solution.py:457
  44.0 9.5 %collective-permute-start.5 = (bf16[256,256]{1,0:T(8,128)(2,1)S(1)}, bf16[256,256]{1,0:T(8,128)(2,1)S(1)}, u32[]{:S(2)}, u32[]{:S(2)}) collective-permute-start(bf16[256,256]{1,0:T(8,128)(2,1)S(1)} %add_convert_fusion.1), channel_id=1, source_target_pairs={{16,0},{24,8},{32,16},{40,24},{48,32},{56,40},{64,48},{72,56},{80,... | collective-permute-start | bytes 393224 | tf_op jit(solution)/shard_map/ppermute | solution.py:457
  53.1 6.0 %copy-start.10 = (bf16[256,512]{1,0:T(8,128)(2,1)S(1)}, bf16[256,512]{1,0:T(8,128)(2,1)}, u32[]{:S(2)}) copy-start(bf16[256,512]{1,0:T(8,128)(2,1)} %get-tuple-element.55) | copy-start | bytes 786436
  53.1 14.1 %copy-start = (f32[256,512]{1,0:T(8,128)S(1)}, f32[256,512]{1,0:T(8,128)}, u32[]{:S(2)}) copy-start(f32[256,512]{1,0:T(8,128)} %get-tuple-element.56.out_ref) | copy-start | bytes 1572868
  53.1 14.1 %copy-start.2 = (bf16[256,512]{1,0:T(8,128)(2,1)S(1)}, bf16[256,512]{1,0:T(8,128)(2,1)}, u32[]{:S(2)}) copy-start(bf16[256,512]{1,0:T(8,128)(2,1)} %grad_ref.1) | copy-start | bytes 786436
  53.1 14.1 %copy-start.3 = (f32[512]{0:T(512)S(1)}, f32[512]{0:T(512)}, u32[]{:S(2)}) copy-start(f32[512]{0:T(512)} %param.17) | copy-start | bytes 6148
  54.4 12.8 %all-to-all-start.1 = ((bf16[4,256,256]{2,1,0:T(8,128)(2,1)}), bf16[4,256,256]{2,1,0:T(8,128)(2,1)S(1)}, u32[]{:S(2)}, u32[]{:S(2)}) async-start(bf16[4,256,256]{2,1,0:T(8,128)(2,1)} %broadcast_in_dim.45), calls=%async_computation.1 | async-start | bytes 1048576 | tf_op jit(solution)/shard_map/all_to_all | solution.py:505
  59.1 3.4 %collective-permute-start.6 = (bf16[256,512]{1,0:T(8,128)(2,1)S(1)}, bf16[256,512]{1,0:T(8,128)(2,1)S(1)}, u32[]{:S(2)}, u32[]{:S(2)}) collective-permute-start(bf16[256,512]{1,0:T(8,128)(2,1)S(1)} %copy-done.10), channel_id=1, source_target_pairs={{0,1},{1,0},{2,3},{3,2},{4,5},{5,4},{6,7},{7,6},{8,9},{9,8},{10,11... | collective-permute-start | bytes 786440 | tf_op jit(solution)/shard_map/ppermute | solution.py:502
  70.5 0.8 copy-start.1
  71.3 10.9 %collective-permute-start.7 = (f32[256,512]{1,0:T(8,128)S(1)}, f32[256,512]{1,0:T(8,128)S(1)}, u32[]{:S(2)}, u32[]{:S(2)}) collective-permute-start(f32[256,512]{1,0:T(8,128)S(1)} %get-tuple-element.59), channel_id=1, source_target_pairs={{0,1},{1,0},{2,3},{3,2},{4,5},{5,4},{6,7},{7,6},{8,9},{9,8},{10,11... | collective-permute-start | bytes 1572872 | tf_op jit(solution)/shard_map/ppermute | solution.py:507
  73.4 8.9 %all-to-all-start.2 = ((f32[8,8,256]{2,1,0:T(8,128)}), f32[8,8,256]{2,1,0:T(8,128)S(1)}, u32[]{:S(2)}, u32[]{:S(2)}) async-start(f32[8,8,256]{2,1,0:T(8,128)} %get-tuple-element.57), calls=%async_computation.2 | async-start | bytes 131072 | tf_op jit(solution)/shard_map/all_to_all | solution.py:508
  82.3 0.6 copy-start.9
  82.3 0.8 copy-start.6
  85.6 14.1 %all-to-all-start.3 = ((bf16[16,32,128]{2,1,0:T(8,128)(2,1)}), bf16[16,32,128]{2,1,0:T(8,128)(2,1)S(1)}, u32[]{:S(2)}, u32[]{:S(2)}) async-start(bf16[16,32,128]{2,1,0:T(8,128)(2,1)} %bitcast.15), calls=%async_computation.3 | async-start | bytes 262144 | tf_op jit(solution)/shard_map/all_to_all | solution.py:439
  99.8 0.7 copy-start.5
  102.0 22.5 %all-to-all-start.4 = ((bf16[4,4,32,128]{3,2,1,0:T(8,128)(2,1)}), bf16[4,4,32,128]{3,2,1,0:T(8,128)(2,1)S(1)}, u32[]{:S(2)}, u32[]{:S(2)}) async-start(bf16[4,4,32,128]{3,2,1,0:T(8,128)(2,1)} %rise.1), calls=%async_computation.4 | async-start | bytes 262144 | tf_op jit(solution)/shard_map/all_to_all | solution.py:439
  124.5 0.7 copy-start.7
  127.0 13.0 %all-to-all-start.5 = ((bf16[16,32,128]{2,1,0:T(8,128)(2,1)}), bf16[16,32,128]{2,1,0:T(8,128)(2,1)S(1)}, u32[]{:S(2)}, u32[]{:S(2)}) async-start(bf16[16,32,128]{2,1,0:T(8,128)(2,1)} %after_states.1), calls=%async_computation.5 | async-start | bytes 262144 | tf_op jit(solution)/shard_map/all_to_all | solution.py:439
  140.0 0.6 copy-start.8
